TPU v7x, 32 devices: a whole 2x2x4 slice. The times are simulated.
32 devices in a mesh: bucket: 16 (over z, y, core), seq: 2 (over x).
Axes of the slice: x: 2, y: 2, z: 4, core: 2. Of those that a mesh axis runs over, the one named last changes fastest.
Arguments:
- tokens: bfloat16 [4096, 1536], P(('bucket', 'seq')), may hold values from -6 to 6
- cotangent: bfloat16 [4096, 1536], P(('bucket', 'seq')), may hold values from -6 to 6
- clip_slices: int32 [4], replicated, may hold values from 1 to 10, 16 in all
- caption_lengths: int32 [4], replicated, may hold values from 1 to 128, as said below
- caption: bfloat16 [4, 128, 4096], replicated, may hold values from -6 to 6
- cond: float32 [4, 1024], replicated, may hold values from -6 to 6
- ada_w: bfloat16 [9216, 1024], P('seq'), may hold values from -0.1875 to 0.1875
- norm_gain: float32 [1536], replicated, may hold values from 0.5 to 1.5
- w_qkv: bfloat16 [4608, 1536], P('seq'), may hold values from -0.15625 to 0.15625
- q_gain: float32 [1536], replicated, may hold values from 0.5 to 1.5
- k_gain: float32 [1536], replicated, may hold values from 0.5 to 1.5
- w_caption: bfloat16 [2, 1536, 4096], P(None, 'seq'), may hold values from -0.09375 to 0.09375
- ky_gain: float32 [1536], replicated, may hold values from 0.5 to 1.5
- cross_gate: float32 [24], replicated, may hold values from -1.5 to 1.5
- w_out: bfloat16 [1536, 1536], P('seq'), may hold values from -1.5 to 1.5
- ffn_gain: float32 [1536], replicated, may hold values from 0.5 to 1.5
- w_gate_up: bfloat16 [8192, 1536], P('seq'), may hold values from -0.15625 to 0.15625
- w_down: bfloat16 [4096, 1536], P('seq'), may hold values from -0.09375 to 0.09375
Outputs:
- out: bfloat16 [4096, 1536], P(('bucket', 'seq'))
- d_tokens: float32 [4096, 1536], P(('bucket', 'seq'))
- d_cond: float32 [4, 1024], replicated
- d_ada: float32 [9216, 1024], P('seq', 'bucket')
- d_norm_gain: float32 [1536], replicated
- d_qkv: float32 [4608, 1536], P('seq', 'bucket')
- d_q_gain: float32 [1536], replicated
- d_k_gain: float32 [1536], replicated
- d_caption_w: float32 [2, 1536, 4096], P(None, 'seq', 'bucket')
- d_ky_gain: float32 [1536], replicated
- d_cross_gate: float32 [24], replicated
- d_out_w: float32 [1536, 1536], P('seq', 'bucket')
- d_ffn_gain: float32 [1536], replicated
- d_gate_up: float32 [8192, 1536], P('seq', 'bucket')
- d_down: float32 [4096, 1536], P('seq', 'bucket')
Inputs may be any that keep to these rules, and one draw needn't show every extreme that they name: Clip c covers 256 * clip_slices[c] consecutive tokens, clips in order; the counts add up to the bucket indices; the longest has 10. `caption_lengths`: some clip has 128 caption tokens.
All inputs are finite; a program needn't handle non-finite values.
Results may differ from a plain program's by a relative error of at most 0.02.
Values may be sent and summed in bfloat16 or wider, within the bound.
No kernel may reach another device: no remote copies, remote signals or barrier semaphores. Data moves between devices by JAX's collectives and lax.ppermute only.
A program may use at most 576 MiB of HBM per device.

v0:
```python
import functools
import math

import jax
import jax.numpy as jnp
from jax import lax
from jax.sharding import PartitionSpec as P

H = 24
HD = 64
D = 1536
FF = 4096
YD = 4096
CD = 1024
CAP = 128
CLIPS = 4


EPSILON = 1e-06
MASKED = -1e30


def project(activations, weight):
    return lax.dot_general(
        activations, weight, (((1,), (1,)), ((), ())), preferred_element_type=jnp.float32
    )


def clip_of(rows, ends):
    return jnp.sum((rows[:, None] >= ends[None, :]).astype(jnp.int32), axis=1)


def head_norm(values, gains, head_count):
    row_count = values.shape[0]
    split = values.reshape(row_count, head_count, -1)
    inverse = lax.rsqrt(jnp.mean(split * split, axis=-1, keepdims=True) + EPSILON)
    unit_rows = split * inverse
    return (unit_rows.reshape(row_count, -1) * gains, unit_rows, inverse)


def head_norm_back(norm_grads, gains, unit_rows, inverse):
    row_count, head_count, head_width = unit_rows.shape
    gain_grad = jnp.sum(norm_grads * unit_rows.reshape(row_count, -1), axis=0)
    unit_grad = (norm_grads * gains).reshape(row_count, head_count, head_width)
    raw_grad = inverse * (
        unit_grad - unit_rows * jnp.mean(unit_grad * unit_rows, axis=-1, keepdims=True)
    )
    return (raw_grad.reshape(row_count, -1), gain_grad)


def rotate(values, positions, head_count):
    row_count = values.shape[0]
    split = values.reshape(row_count, head_count, -1)
    half_width = split.shape[-1] // 2
    frequency = jnp.exp(
        jnp.arange(half_width, dtype=jnp.float32) * (-2.0 * math.log(10000.0) / (2 * half_width))
    )
    angles = positions[:, None] * frequency[None, :]
    cosine = jnp.cos(angles)[:, None, :]
    sine = jnp.sin(angles)[:, None, :]
    first_half = split[..., :half_width]
    second_half = split[..., half_width:]
    turned = jnp.concatenate(
        [first_half * cosine - second_half * sine, first_half * sine + second_half * cosine],
        axis=-1,
    )
    return turned.reshape(row_count, -1)


def block_size(row_count):
    return 512 if row_count % 512 == 0 else row_count


def body(
    tokens,
    cotangent,
    clip_slices,
    caption_lengths,
    caption,
    cond,
    ada_w,
    norm_gain,
    w_qkv,
    q_gain,
    k_gain,
    w_caption,
    ky_gain,
    cross_gate,
    w_out,
    ffn_gain,
    w_gate_up,
    w_down,
):
    seq_count = lax.axis_size("seq")
    bucket_count = lax.axis_size("bucket")
    tok_rows = tokens.shape[0]
    slice_rows = tok_rows * seq_count
    total_rows = slice_rows * bucket_count
    local_heads = H // seq_count
    local_width = local_heads * HD
    score_scale = HD ** (-0.5)
    bucket_id = lax.axis_index("bucket")
    seq_id = lax.axis_index("seq")
    ends = jnp.cumsum(clip_slices) * slice_rows
    starts = ends - clip_slices * slice_rows
    my_clip = clip_of(jnp.reshape(bucket_id * slice_rows, (1,)), ends)[0]
    clip_mask = jnp.arange(CLIPS) == my_clip
    clip_start = jnp.sum(jnp.where(clip_mask, starts, 0))
    first_token = (bucket_id * seq_count + seq_id) * tok_rows
    positions = (first_token + jnp.arange(tok_rows, dtype=jnp.int32) - clip_start).astype(
        jnp.float32
    )
    caption_usable = jnp.arange(CAP) < jnp.sum(jnp.where(clip_mask, caption_lengths, 0))
    head_first = seq_id * local_width
    gates_local = jnp.tanh(lax.dynamic_slice_in_dim(cross_gate, seq_id * local_heads, local_heads))
    ky_gain_local = lax.dynamic_slice_in_dim(ky_gain, head_first, local_width)
    activation = jax.nn.silu(cond).astype(jnp.bfloat16)
    cond_row = lax.dynamic_index_in_dim(activation, my_clip, 0, True)
    caption_rows = lax.dynamic_index_in_dim(caption, my_clip, 0, False)
    caption_raw = jnp.einsum(
        "ty,jdy->jtd", caption_rows, w_caption, preferred_element_type=jnp.float32
    )
    caption_norm, caption_unit, caption_inverse = head_norm(
        caption_raw[0], ky_gain_local, local_heads
    )
    caption_keys = caption_norm.astype(jnp.bfloat16).reshape(CAP, local_heads, HD)
    caption_values = caption_raw[1].astype(jnp.bfloat16).reshape(CAP, local_heads, HD)
    inputs = tokens.astype(jnp.float32)

    def key_usable(first_row, row_count):
        return clip_of(first_row + jnp.arange(row_count, dtype=jnp.int32), ends) == my_clip

    def fold_keys(queries3, running, segment, first_row):
        seg_keys, seg_values = segment
        row_count = seg_keys.shape[0]
        key_rows = block_size(row_count)
        steps_count = row_count // key_rows
        usable = key_usable(first_row, row_count).reshape(steps_count, key_rows)
        key_blocks = seg_keys.reshape(steps_count, key_rows, local_heads, HD)
        value_blocks = seg_values.reshape(steps_count, key_rows, local_heads, HD)

        def update(state, item):
            key_block, value_block, usable_block = item

            def update_include(inner):
                row_max, row_total, accum = inner
                scores = (
                    jnp.einsum(
                        "qhd,khd->hqk", queries3, key_block, preferred_element_type=jnp.float32
                    )
                    * score_scale
                )
                scores = jnp.where(usable_block[None, None, :], scores, MASKED)
                new_max = jnp.maximum(row_max, jnp.max(scores, axis=-1))
                factor = jnp.exp(row_max - new_max)
                weights = jnp.exp(scores - new_max[..., None])
                row_total = row_total * factor + jnp.sum(weights, axis=-1)
                accum = accum * factor.T[:, :, None] + jnp.einsum(
                    "hqk,khd->qhd",
                    weights.astype(jnp.bfloat16),
                    value_block,
                    preferred_element_type=jnp.float32,
                )
                return (new_max, row_total, accum)

            return (
                lax.cond(jnp.any(usable_block), update_include, lambda inner: inner, state),
                None,
            )

        running, unused = lax.scan(update, running, (key_blocks, value_blocks, usable))
        return running

    def local_fold(queries3, running, keys_whole):

        def local_visit(state, piece_index):
            first_row = piece_index * slice_rows
            segment = (
                lax.dynamic_slice_in_dim(keys_whole[0], first_row, slice_rows, 0),
                lax.dynamic_slice_in_dim(keys_whole[1], first_row, slice_rows, 0),
            )
            return (fold_keys(queries3, state, segment, first_row), None)

        running, unused = lax.scan(local_visit, running, jnp.arange(bucket_count, dtype=jnp.int32))
        return running

    def forward(qkv_full, out_full, modulation, second):
        shift_vec = modulation[:D]
        scale_vec = modulation[D : 2 * D]
        gate_vec = modulation[2 * D : 3 * D]
        inverse = lax.rsqrt(jnp.mean(inputs * inputs, axis=-1, keepdims=True) + EPSILON)
        unit_rows = inputs * inverse
        hidden = (unit_rows * norm_gain * (1.0 + scale_vec) + shift_vec).astype(jnp.bfloat16)
        projected = project(hidden, qkv_full)
        query_norm, query_unit, query_inverse = head_norm(projected[:, :D], q_gain, H)
        key_norm, key_unit, key_inverse = head_norm(projected[:, D : 2 * D], k_gain, H)
        queries = rotate(query_norm, positions, H).astype(jnp.bfloat16)
        keys_tok = rotate(key_norm, positions, H).astype(jnp.bfloat16)
        values_tok = projected[:, 2 * D :].astype(jnp.bfloat16)
        head_queries, head_keys, head_values = (
            lax.all_to_all(queries, "seq", split_axis=1, concat_axis=0, tiled=True),
            lax.all_to_all(keys_tok, "seq", split_axis=1, concat_axis=0, tiled=True),
            lax.all_to_all(values_tok, "seq", split_axis=1, concat_axis=0, tiled=True),
        )
        queries3 = head_queries.reshape(slice_rows, local_heads, HD)
        start_state = (
            jnp.full((local_heads, slice_rows), MASKED, jnp.float32),
            jnp.zeros((local_heads, slice_rows), jnp.float32),
            jnp.zeros((slice_rows, local_heads, HD), jnp.float32),
        )
        folder = functools.partial(fold_keys, queries3)
        if second:
            keys_whole = (
                lax.all_gather(head_keys, "bucket", axis=0, tiled=True),
                lax.all_gather(head_values, "bucket", axis=0, tiled=True),
            )
            final_state = local_fold(queries3, start_state, keys_whole)
        else:
            keys_whole = None
            final_state = folder(
                start_state,
                (
                    lax.all_gather(head_keys, "bucket", axis=0, tiled=True),
                    lax.all_gather(head_values, "bucket", axis=0, tiled=True),
                ),
                jnp.int32(0),
            )
        row_max, row_total, accum = final_state
        own = accum / row_total.T[:, :, None]
        cross_scores = (
            jnp.einsum("qhd,khd->hqk", queries3, caption_keys, preferred_element_type=jnp.float32)
            * score_scale
        )
        cross_prob = jax.nn.softmax(
            jnp.where(caption_usable[None, None, :], cross_scores, MASKED), axis=-1
        )
        other = jnp.einsum(
            "hqk,khd->qhd",
            cross_prob.astype(jnp.bfloat16),
            caption_values,
            preferred_element_type=jnp.float32,
        )
        combined = (
            (own + gates_local[None, :, None] * other)
            .reshape(slice_rows, local_width)
            .astype(jnp.bfloat16)
        )
        attention = lax.all_to_all(combined, "seq", split_axis=0, concat_axis=1, tiled=True)
        branch = project(attention, out_full)
        return dict(
            gate_vec=gate_vec,
            scale_vec=scale_vec,
            inverse=inverse,
            unit_rows=unit_rows,
            hidden=hidden,
            query_unit=query_unit,
            query_inverse=query_inverse,
            key_unit=key_unit,
            key_inverse=key_inverse,
            queries3=queries3,
            own_keys3=head_keys.reshape(slice_rows, local_heads, HD),
            own_values3=head_values.reshape(slice_rows, local_heads, HD),
            keys_whole=keys_whole,
            row_log=row_max + jnp.log(row_total),
            own=own,
            other=other,
            cross_prob=cross_prob,
            attention=attention,
            branch=branch,
            output=inputs + gate_vec * branch,
        )

    gathered = (
        lax.all_gather(ada_w, "seq", axis=0, tiled=True),
        lax.all_gather(w_qkv, "seq", axis=0, tiled=True),
        lax.all_gather(w_out, "seq", axis=0, tiled=True),
        lax.all_gather(w_gate_up, "seq", axis=0, tiled=True),
        lax.all_gather(w_down, "seq", axis=0, tiled=True),
    )
    modulation = project(cond_row, gathered[0])[0]
    first_pass = forward(gathered[1], gathered[2], modulation, False)
    middle = first_pass["output"]
    shift_mlp = modulation[3 * D : 4 * D]
    scale_mlp = modulation[4 * D : 5 * D]
    gate_mlp = modulation[5 * D :]
    mid_inverse = lax.rsqrt(jnp.mean(middle * middle, axis=-1, keepdims=True) + EPSILON)
    mid_unit = middle * mid_inverse
    mlp_in = (mid_unit * ffn_gain * (1.0 + scale_mlp) + shift_mlp).astype(jnp.bfloat16)
    gate_up = project(mlp_in, gathered[3])
    gate_half = gate_up[:, :FF]
    up_half = gate_up[:, FF:]
    gate_sigmoid = jax.nn.sigmoid(gate_half)
    silu_gate = gate_half * gate_sigmoid
    inner = (silu_gate * up_half).astype(jnp.bfloat16)
    mlp_branch = jnp.dot(inner, gathered[4], preferred_element_type=jnp.float32)
    output = (middle + gate_mlp * mlp_branch).astype(jnp.bfloat16)
    regathered = (
        lax.all_gather(ada_w, "seq", axis=0, tiled=True),
        lax.all_gather(w_qkv, "seq", axis=0, tiled=True),
        lax.all_gather(w_out, "seq", axis=0, tiled=True),
        lax.all_gather(w_gate_up, "seq", axis=0, tiled=True),
        lax.all_gather(w_down, "seq", axis=0, tiled=True),
    )
    second_pass = forward(regathered[1], regathered[2], modulation, True)
    ada_full, qkv_full, out_full, gate_up_full, down_full = regathered
    grad_out = cotangent.astype(jnp.float32)
    mlp_gate_grad = jnp.sum(grad_out * mlp_branch, axis=0)
    grad_mlp = (grad_out * gate_mlp).astype(jnp.bfloat16)
    grad_inner = lax.dot_general(
        grad_mlp, down_full, (((1,), (1,)), ((), ())), preferred_element_type=jnp.float32
    )
    grad_gate_half = grad_inner * up_half * gate_sigmoid * (1.0 + gate_half * (1.0 - gate_sigmoid))
    grad_up_half = grad_inner * silu_gate
    grad_gate_up = jnp.concatenate([grad_gate_half, grad_up_half], axis=1).astype(jnp.bfloat16)
    mlp_in_grad = jnp.dot(grad_gate_up, gate_up_full, preferred_element_type=jnp.float32)
    ffn_gain_grad = jnp.sum(mlp_in_grad * (1.0 + scale_mlp) * mid_unit, axis=0)
    shift_mlp_grad = jnp.sum(mlp_in_grad, axis=0)
    scale_mlp_grad = jnp.sum(mlp_in_grad * mid_unit * ffn_gain, axis=0)
    mid_unit_grad = mlp_in_grad * ffn_gain * (1.0 + scale_mlp)
    residual_grad = (
        mid_inverse
        * (mid_unit_grad - mid_unit * jnp.mean(mid_unit_grad * mid_unit, axis=-1, keepdims=True))
        + grad_out
    )
    gate_grad = jnp.sum(residual_grad * second_pass["branch"], axis=0)
    grad_branch = (residual_grad * second_pass["gate_vec"]).astype(jnp.bfloat16)
    attention = second_pass["attention"]
    grad_attention = jnp.dot(grad_branch, out_full, preferred_element_type=jnp.float32).astype(
        jnp.bfloat16
    )
    grad_heads = lax.all_to_all(grad_attention, "seq", split_axis=1, concat_axis=0, tiled=True)
    grad_own16 = grad_heads.reshape(slice_rows, local_heads, HD)
    grad_own = grad_own16.astype(jnp.float32)
    queries3 = second_pass["queries3"]
    own = second_pass["own"]
    other = second_pass["other"]
    cross_prob = second_pass["cross_prob"]
    grad_other = (grad_own * gates_local[None, :, None]).astype(jnp.bfloat16)
    gate_grad_local = jnp.sum(grad_own * other, axis=(0, 2)) * (1.0 - gates_local * gates_local)
    grad_cross_prob = jnp.einsum(
        "qhd,khd->hqk", grad_other, caption_values, preferred_element_type=jnp.float32
    )
    grad_cross = (
        cross_prob
        * (grad_cross_prob - jnp.sum(cross_prob * grad_cross_prob, axis=-1, keepdims=True))
    ).astype(jnp.bfloat16)
    cross_query_grad = score_scale * jnp.einsum(
        "hqk,khd->qhd", grad_cross, caption_keys, preferred_element_type=jnp.float32
    )
    caption_key_grad = score_scale * jnp.einsum(
        "hqk,qhd->khd", grad_cross, queries3, preferred_element_type=jnp.float32
    )
    caption_value_grad = jnp.einsum(
        "hqk,qhd->khd",
        cross_prob.astype(jnp.bfloat16),
        grad_other,
        preferred_element_type=jnp.float32,
    )
    row_delta = jnp.sum(grad_own * own, axis=-1).T
    row_log = second_pass["row_log"]
    keys_whole = second_pass["keys_whole"]

    def grad_piece(query_grad, piece_index, with_keys):
        first_row = piece_index * slice_rows
        key_rows = block_size(slice_rows)
        steps_count = slice_rows // key_rows
        key_blocks = lax.dynamic_slice_in_dim(keys_whole[0], first_row, slice_rows, 0).reshape(
            steps_count, key_rows, local_heads, HD
        )
        value_blocks = lax.dynamic_slice_in_dim(keys_whole[1], first_row, slice_rows, 0).reshape(
            steps_count, key_rows, local_heads, HD
        )
        usable = key_usable(first_row, slice_rows).reshape(steps_count, key_rows)

        def grad_visit(accum, item):
            key_block, value_block, usable_block = item

            def grad_include(inner):
                scores = (
                    jnp.einsum(
                        "qhd,khd->hqk", queries3, key_block, preferred_element_type=jnp.float32
                    )
                    * score_scale
                )
                scores = jnp.where(usable_block[None, None, :], scores, MASKED)
                probability = jnp.exp(scores - row_log[..., None])
                grad_prob = jnp.einsum(
                    "qhd,khd->hqk", grad_own16, value_block, preferred_element_type=jnp.float32
                )
                grad_scores = (probability * (grad_prob - row_delta[..., None])).astype(
                    jnp.bfloat16
                )
                updated = inner + score_scale * jnp.einsum(
                    "hqk,khd->qhd", grad_scores, key_block, preferred_element_type=jnp.float32
                )
                key_grad = score_scale * jnp.einsum(
                    "hqk,qhd->khd", grad_scores, queries3, preferred_element_type=jnp.float32
                )
                value_grad = jnp.einsum(
                    "hqk,qhd->khd",
                    probability.astype(jnp.bfloat16),
                    grad_own16,
                    preferred_element_type=jnp.float32,
                )
                return (updated, key_grad, value_grad)

            def skip(inner):
                empty = jnp.zeros((key_rows, local_heads, HD), jnp.float32)
                return (inner, empty, empty)

            updated, key_grad, value_grad = lax.cond(
                jnp.any(usable_block), grad_include, skip, accum
            )
            return (updated, (key_grad, value_grad))

        query_grad, (key_grads, value_grads) = lax.scan(
            grad_visit, query_grad, (key_blocks, value_blocks, usable)
        )
        return (
            query_grad,
            (
                key_grads.reshape(slice_rows, local_width),
                value_grads.reshape(slice_rows, local_width),
            ),
        )

    query_start = jnp.zeros((slice_rows, local_heads, HD), jnp.float32)
    piece_order = jnp.arange(bucket_count, dtype=jnp.int32)
    self_query_grad, (key_terms, value_terms) = lax.scan(
        functools.partial(grad_piece, with_keys=True), query_start, piece_order
    )
    key_sum, value_sum = (
        lax.psum_scatter(
            key_terms.reshape(total_rows, local_width).astype(jnp.bfloat16),
            "bucket",
            scatter_dimension=0,
            tiled=True,
        ).astype(jnp.float32),
        lax.psum_scatter(
            value_terms.reshape(total_rows, local_width).astype(jnp.bfloat16),
            "bucket",
            scatter_dimension=0,
            tiled=True,
        ).astype(jnp.float32),
    )
    query_grad16 = (
        (self_query_grad + cross_query_grad).reshape(slice_rows, local_width).astype(jnp.bfloat16)
    )
    tok_query_grad, tok_key_grad, tok_value_grad = (
        lax.all_to_all(query_grad16, "seq", split_axis=0, concat_axis=1, tiled=True),
        lax.all_to_all(
            key_sum.astype(jnp.bfloat16), "seq", split_axis=0, concat_axis=1, tiled=True
        ),
        lax.all_to_all(
            value_sum.astype(jnp.bfloat16), "seq", split_axis=0, concat_axis=1, tiled=True
        ),
    )
    query_raw_grad, q_gain_grad = head_norm_back(
        rotate(tok_query_grad.astype(jnp.float32), -positions, H),
        q_gain,
        second_pass["query_unit"],
        second_pass["query_inverse"],
    )
    key_raw_grad, k_gain_grad = head_norm_back(
        rotate(tok_key_grad.astype(jnp.float32), -positions, H),
        k_gain,
        second_pass["key_unit"],
        second_pass["key_inverse"],
    )
    projected_grad = jnp.concatenate(
        [query_raw_grad, key_raw_grad, tok_value_grad.astype(jnp.float32)], axis=1
    ).astype(jnp.bfloat16)
    hidden = second_pass["hidden"]
    out_each = D // seq_count
    qkv_each = 3 * D // seq_count
    gate_up_each = 2 * FF // seq_count
    down_each = FF // seq_count
    rows_each = out_each + qkv_each + gate_up_each + down_each
    device_count = rows_each * lax.axis_size("seq") // rows_each
    first_device = jnp.int32(0) // rows_each

    def part(operand, partner, each):
        picked = lax.dynamic_slice_in_dim(operand, first_device * each, device_count * each, 1)
        term = lax.dot_general(
            picked, partner, (((0,), (0,)), ((), ())), preferred_element_type=jnp.float32
        )
        return term.reshape(device_count, each, D)

    terms = [
        part(grad_branch, attention, out_each),
        part(projected_grad, hidden, qkv_each),
        part(grad_gate_up, mlp_in, gate_up_each),
        part(inner, grad_mlp, down_each),
    ]
    weight_grad_seq = lax.psum_scatter(
        jnp.concatenate(terms, axis=1)
        .reshape(rows_each * lax.axis_size("seq"), D)
        .astype(jnp.bfloat16),
        "seq",
        scatter_dimension=0,
        tiled=True,
    )
    hidden_grad = jnp.dot(projected_grad, qkv_full, preferred_element_type=jnp.float32)
    unit_rows = second_pass["unit_rows"]
    scale_vec = second_pass["scale_vec"]
    inverse = second_pass["inverse"]
    norm_gain_grad = jnp.sum(hidden_grad * (1.0 + scale_vec) * unit_rows, axis=0)
    shift_grad = jnp.sum(hidden_grad, axis=0)
    scale_grad = jnp.sum(hidden_grad * unit_rows * norm_gain, axis=0)
    unit_grad = hidden_grad * norm_gain * (1.0 + scale_vec)
    token_grad = (
        inverse * (unit_grad - unit_rows * jnp.mean(unit_grad * unit_rows, axis=-1, keepdims=True))
        + residual_grad
    )
    modulation_grad = jnp.where(
        clip_mask[:, None],
        jnp.concatenate(
            [shift_grad, scale_grad, gate_grad, shift_mlp_grad, scale_mlp_grad, mlp_gate_grad]
        )[None, :],
        0.0,
    )
    ky_gain_part = jnp.sum(
        caption_key_grad.reshape(CAP, local_width) * caption_unit.reshape(CAP, local_width), axis=0
    )
    ky_gain_full = lax.dynamic_update_slice_in_dim(
        jnp.zeros((D,), jnp.float32), ky_gain_part, head_first, 0
    )
    gate_full = lax.dynamic_update_slice_in_dim(
        jnp.zeros((H,), jnp.float32), gate_grad_local, seq_id * local_heads, 0
    )
    caption_part = jnp.stack(
        [caption_key_grad.reshape(CAP, local_width), caption_value_grad.reshape(CAP, local_width)]
    )[None]
    zero_index = jnp.zeros((), jnp.int32)
    caption_full = lax.dynamic_update_slice(
        jnp.zeros((CLIPS, 2, CAP, D), jnp.float32),
        caption_part,
        (my_clip, zero_index, zero_index, head_first),
    )
    reduced = lax.psum(
        (
            norm_gain_grad,
            q_gain_grad,
            k_gain_grad,
            ky_gain_full,
            gate_full,
            modulation_grad,
            caption_full,
            ffn_gain_grad,
        ),
        ("bucket", "seq"),
    )
    modulation_total = reduced[5].astype(jnp.bfloat16)
    rows_local = 6 * D // seq_count
    cols_local = CD // bucket_count
    ada_grad = lax.dot_general(
        lax.dynamic_slice_in_dim(modulation_total, seq_id * rows_local, rows_local, 1),
        lax.dynamic_slice_in_dim(activation, bucket_id * cols_local, cols_local, 1),
        (((0,), (0,)), ((), ())),
        preferred_element_type=jnp.float32,
    )
    cond_sigmoid = jax.nn.sigmoid(cond)
    cond_grad = (
        jnp.dot(modulation_total, ada_full, preferred_element_type=jnp.float32)
        * cond_sigmoid
        * (1.0 + cond * (1.0 - cond_sigmoid))
    )
    caption_total = lax.dynamic_slice_in_dim(reduced[6], head_first, local_width, 3)
    raw_keys_all = jnp.einsum(
        "cty,dy->ctd", caption, w_caption[0], preferred_element_type=jnp.float32
    ).reshape(CLIPS * CAP, local_width)
    ignored, unit_all, inverse_all = head_norm(raw_keys_all, ky_gain_local, local_heads)
    raw_key_grad, unused_gain = head_norm_back(
        caption_total[:, 0].reshape(CLIPS * CAP, local_width), ky_gain_local, unit_all, inverse_all
    )
    raw_grad = jnp.stack(
        [raw_key_grad.reshape(CLIPS, CAP, local_width), caption_total[:, 1]], axis=1
    ).astype(jnp.bfloat16)
    caption_cols = lax.dynamic_slice_in_dim(
        caption, bucket_id * (YD // bucket_count), YD // bucket_count, 2
    )
    caption_w_grad = jnp.einsum(
        "cjtd,cty->jdy", raw_grad, caption_cols, preferred_element_type=jnp.float32
    )
    combined_grads = lax.psum_scatter(
        weight_grad_seq, "bucket", scatter_dimension=1, tiled=True
    ).astype(jnp.float32)
    out_grad_out = combined_grads[:out_each]
    qkv_grad_out = combined_grads[out_each : out_each + qkv_each]
    gate_up_grad_out = combined_grads[out_each + qkv_each : out_each + qkv_each + gate_up_each]
    down_grad_out = combined_grads[out_each + qkv_each + gate_up_each :]
    return (
        output,
        token_grad,
        cond_grad,
        ada_grad,
        reduced[0],
        qkv_grad_out,
        reduced[1],
        reduced[2],
        caption_w_grad,
        reduced[3],
        reduced[4],
        out_grad_out,
        reduced[7],
        gate_up_grad_out,
        down_grad_out,
    )


def solution(mesh):
    in_specs = (
        P(("bucket", "seq"), None),
        P(("bucket", "seq"), None),
        P(),
        P(),
        P(),
        P(),
        P("seq", None),
        P(),
        P("seq", None),
        P(),
        P(),
        P(None, "seq", None),
        P(),
        P(),
        P("seq", None),
        P(),
        P("seq", None),
        P("seq", None),
    )
    out_specs = (
        P(("bucket", "seq"), None),
        P(("bucket", "seq"), None),
        P(),
        P("seq", "bucket"),
        P(),
        P("seq", "bucket"),
        P(),
        P(),
        P(None, "seq", "bucket"),
        P(),
        P(),
        P("seq", "bucket"),
        P(),
        P("seq", "bucket"),
        P("seq", "bucket"),
    )
    return jax.shard_map(body, mesh=mesh, in_specs=in_specs, out_specs=out_specs, check_vma=False)
```

profile of v0, /device:TPU:0, one launch (start us, length us, event | category | flops | bytes accessed | tf_op | source)
XLA Modules:
  0.0 2727.8 jit_solution(18327724943892184735)
XLA Ops:
  15.3 221.4 %all-gather.8.cloned.1.call-done = bf16[9216,1024]{1,0:T(8,128)(2,1)} async-done(((bf16[4608,1024]{1,0:T(8,128)(2,1)}), bf16[9216,1024]{1,0:T(8,128)(2,1)}) %all-gather.8.cloned.1.call-update) | async-done | bytes 18874384 | tf_op jit(solution)/shard_map/all_gather | solution.py:274
  236.7 11.3 fusion.112
  248.6 159.4 %all-gather.10.cloned.1.call-done = bf16[4608,1536]{1,0:T(8,128)(2,1)} async-done(((bf16[2304,1536]{1,0:T(8,128)(2,1)}), bf16[4608,1536]{1,0:T(8,128)(2,1)}) %all-gather.10.cloned.1.call-update) | async-done | bytes 14155792 | tf_op jit(solution)/shard_map/all_gather | solution.py:275
  487.1 24.2 all-gather.12.cloned.1.call-done
  532.1 46.1 %all-gather.14.cloned.1.call-done = bf16[4096,768]{0,1:T(8,128)(2,1)} async-done(((bf16[256,768]{0,1:T(8,128)(2,1)}), bf16[4096,768]{0,1:T(8,128)(2,1)}) %all-gather.14.cloned.1.call-update) | async-done | bytes 6291472 | tf_op jit(solution)/shard_map/all_gather | solution.py:224
  585.2 17.2 copy.234
  602.5 17.5 while.39
  626.8 62.0 %while.40 = (s32[]{:T(128)}, f32[12,256]{1,0:T(8,128)S(1)}, f32[12,256]{1,0:T(8,128)S(1)}, f32[256,12,64]{0,2,1:T(8,128)S(1)}, s32[16]{0:T(128)S(1)}, /*index=5*...) while((s32[]{:T(128)}, f32[12,256]{1,0:T(8,128)S(1)}, ...), condition=%wide.region_26.27_spmd, body=%wide.region_19.26_spmd.sunk | while | flops 210383360 | bytes 13964625 | solution.py:184
  693.1 246.8 %all-gather.18.cloned.1.call-done = bf16[8192,1536]{1,0:T(8,128)(2,1)} async-done(((bf16[4096,1536]{1,0:T(8,128)(2,1)}), bf16[8192,1536]{1,0:T(8,128)(2,1)}) %all-gather.18.cloned.1.call-update) | async-done | bytes 25165840 | tf_op jit(solution)/shard_map/all_gather | solution.py:277
  939.9 15.5 fusion.128
  955.4 138.6 %all-gather.20.cloned.1.call-done = bf16[4096,1536]{1,0:T(8,128)(2,1)} async-done(((bf16[2048,1536]{1,0:T(8,128)(2,1)}), bf16[4096,1536]{1,0:T(8,128)(2,1)}) %all-gather.20.cloned.1.call-update) | async-done | bytes 12582928 | tf_op jit(solution)/shard_map/all_gather | solution.py:278
  1094.0 10.3 multiply_convert_fusion.2
  1104.3 12.4 multiply_reduce_fusion.3
  1142.8 110.3 %while.41 = (s32[]{:T(128)}, f32[256,12,64]{0,2,1:T(8,128)S(1)}, bf16[16,256,768]{2,1,0:T(8,128)(2,1)}, bf16[16,256,768]{2,1,0:T(8,128)(2,1)}, s32[16]{0:T(128)}...) while((s32[]{:T(128)}, f32[256,12,64]{0,2,1:T(8,128)S(1)}, ...), condition=%wide.region_34.35_spmd, body=%wide.region_29.34_spmd.sunk | while | flops 511970816 | bytes 24028244 | solution.py:429
  1273.9 14.0 convolution_convert_fusion
  1287.9 107.6 %reduce-scatter.7.cloned.1.call-done = bf16[256,768]{1,0:T(8,128)(2,1)} async-done(((bf16[4096,768]{1,0:T(8,128)(2,1)}), bf16[256,768]{1,0:T(8,128)(2,1)}) %reduce-scatter.7.cloned.1.call-update) | async-done | bytes 393232 | tf_op jit(solution)/shard_map/reduce_scatter | solution.py:439
  1407.7 76.6 %reduce-scatter.5.cloned.1.call-done = bf16[256,768]{1,0:T(8,128)(2,1)} async-done(((bf16[4096,768]{1,0:T(8,128)(2,1)}), bf16[256,768]{1,0:T(8,128)(2,1)}) %reduce-scatter.5.cloned.1.call-update) | async-done | bytes 393232 | tf_op jit(solution)/shard_map/reduce_scatter | solution.py:433
  1520.8 70.2 %pad_maximum_fusion = bf16[2,9216,1536]{2,1,0:T(8,128)(2,1)} fusion(bf16[2,2048,1536]{2,1,0:T(8,128)(2,1)} %bitcast.241, bf16[2,4096,1536]{2,1,0:T(8,128)(2,1)} %bitcast.237, bf16[2,2304,1536]{2,1,0:T(8,128)(2,1)} %bitcast.240, bf16[2,768,1536]{2,1,0:T(8,128)(2,1)S(1)} %bitcast.252), kind=kLoop, calls=%fused_computation.68 | loop fusion | flops 226492416 | bytes 113246208 | tf_op jit(solution)/shard_map/concatenate | solution.py:496
  1591.0 72.8 %copy.275 = bf16[18432,1536]{0,1:T(8,128)(2,1)} copy(bf16[18432,1536]{1,0:T(8,128)(2,1)} %bitcast.236) | data formatting | bytes 113246208 | tf_op jit(solution)/shard_map/convert_element_type | solution.py:498
  1672.5 606.7 %reduce-scatter.9.cloned.1.call-done = bf16[9216,1536]{0,1:T(8,128)(2,1)} async-done(((bf16[18432,1536]{0,1:T(8,128)(2,1)}), bf16[9216,1536]{0,1:T(8,128)(2,1)}) %reduce-scatter.9.cloned.1.call-update) | async-done | bytes 28311568 | tf_op jit(solution)/shard_map/reduce_scatter | solution.py:495
  2301.4 139.3 %all-reduce.4.cloned.1.call-done = f32[4,2,128,1536]{2,3,0,1:T(8,128)} async-done(((f32[4,2,128,1536]{2,3,0,1:T(8,128)}), f32[4,2,128,1536]{2,3,0,1:T(8,128)}) %all-reduce.4.cloned.1.call-update) | async-done | bytes 6291472 | tf_op jit(solution)/shard_map/psum | solution.py:540
  2456.1 10.6 fusion.85
  2467.1 46.4 %all-reduce.5 = (bf16[4,9216]{1,0:T(4,128)(2,1)S(1)}, f32[1536]{0:T(1024)}, f32[1536]{0:T(1024)}, f32[1536]{0:T(1024)}, f32[1536]{0:T(1024)}, /*index=5*/f32[24]{0:T(128)}, f32[1536]{0:T(1024)}) all-reduce(f32[4,9216]{1,0:T(4,128)S(1)} %broadcast_select_fusion, ...), channel_id=1, replica_groups=mesh['bucket'=16,'seq'=2] {'bucket','seq'}, use_global_device_ids=true, to_apply=%region_47.48 | all-reduce | flops 44568 | bytes 282816 | tf_op jit(solution)/shard_map/psum | solution.py:540
  2526.5 188.1 %reduce-scatter.11.cloned.1.call-done = bf16[9216,96]{0,1:T(8,128)(2,1)} async-done(((bf16[9216,1536]{0,1:T(8,128)(2,1)}), bf16[9216,96]{0,1:T(8,128)(2,1)}) %reduce-scatter.11.cloned.1.call-update) | async-done | bytes 1769488 | tf_op jit(solution)/shard_map/reduce_scatter | solution.py:585
  (674 shorter events, 456.1 us)
Async XLA Ops:
  7.2 229.5 %all-gather.8.cloned.1.call-start = ((), (), s32[]{:S(2)}) async-start(), calls=%async_computation.13 | async-start | bytes 28311552 | tf_op jit(solution)/shard_map/all_gather | solution.py:274
  7.9 400.1 %all-gather.10.cloned.1.call-start = ((), (), s32[]{:S(2)}) async-start(), calls=%async_computation.14 | async-start | bytes 21233664 | tf_op jit(solution)/shard_map/all_gather | solution.py:275
  8.7 502.6 %all-gather.12.cloned.1.call-start = ((), (), s32[]{:S(2)}) async-start(), calls=%async_computation.15 | async-start | bytes 6684672 | tf_op jit(solution)/shard_map/all_gather | solution.py:223
  14.4 393.6 %copy-start.81 = (f32[128]{0:T(128)}, f32[128]{0:T(128)S(1)}, u32[]{:S(2)}) copy-start(f32[128]{0:T(128)S(1)} %add_rsqrt_fusion.5) | copy-start | bytes 1540
  15.3 392.8 %copy-start.51 = (f32[1536]{0:T(1024)S(1)}, f32[1536]{0:T(1024)}, u32[]{:S(2)}) copy-start(f32[1536]{0:T(1024)} %param.37) | copy-start | bytes 18436
  449.3 128.9 %all-gather.14.cloned.1.call-start = ((), (), s32[]{:S(2)}) async-start(), calls=%async_computation.16 | async-start | bytes 6684672 | tf_op jit(solution)/shard_map/all_gather | solution.py:224
  458.8 230.1 %all-gather.16.cloned.1.call-start = ((), (), s32[]{:S(2)}) async-start(), calls=%async_computation.17 | async-start | bytes 7077888 | tf_op jit(solution)/shard_map/all_gather | solution.py:276
  459.4 480.5 %all-gather.18.cloned.1.call-start = ((), (), s32[]{:S(2)}) async-start(), calls=%async_computation.18 | async-start | bytes 37748736 | tf_op jit(solution)/shard_map/all_gather | solution.py:277
  459.9 634.1 %all-gather.20.cloned.1.call-start = ((), (), s32[]{:S(2)}) async-start(), calls=%async_computation.19 | async-start | bytes 18874368 | tf_op jit(solution)/shard_map/all_gather | solution.py:278
  475.6 9.3 all-to-all-start.1
  623.2 65.7 %all-to-all-start.3 = ((bf16[2,128,768]{1,2,0:T(8,128)(2,1)}), bf16[2,128,768]{1,2,0:T(8,128)(2,1)S(1)}, u32[]{:S(2)}, u32[]{:S(2)}) async-start(bf16[2,128,768]{1,2,0:T(8,128)(2,1)} %copy.238), calls=%async_computation.3 | async-start | bytes 786432 | tf_op jit(solution)/shard_map/all_to_all | solution.py:248
  688.9 250.9 %copy-start.39 = (f32[1536]{0:T(1024)S(1)}, f32[1536]{0:T(1024)}, u32[]{:S(2)}) copy-start(f32[1536]{0:T(1024)} %param.45) | copy-start | bytes 18436
  688.9 250.9 %copy-start.40 = (f32[1536]{0:T(1024)S(1)}, f32[1536]{0:T(1024)}, u32[]{:S(2)}) copy-start(f32[1536]{0:T(1024)} %get-tuple-element.811) | copy-start | bytes 18436
  693.1 423.7 %copy-start.76 = (f32[128]{0:T(128)}, f32[128]{0:T(128)S(1)}, u32[]{:S(2)}) copy-start(f32[128]{0:T(128)S(1)} %add_rsqrt_fusion.4) | copy-start | bytes 1540
  1127.6 10.3 all-to-all-start.4
  1131.0 264.4 %reduce-scatter.7.cloned.1.call-start = ((), (), s32[]{:S(2)}) async-start(), calls=%async_computation.21 | async-start | bytes 6684672 | tf_op jit(solution)/shard_map/reduce_scatter | solution.py:439
  1253.2 231.2 %reduce-scatter.5.cloned.1.call-start = ((), (), s32[]{:S(2)}) async-start(), calls=%async_computation.20 | async-start | bytes 6684672 | tf_op jit(solution)/shard_map/reduce_scatter | solution.py:433
  1260.2 9.4 all-to-all-start.5
  1270.4 17.5 all-to-all-start.8
  1395.5 88.9 %all-to-all-start.7 = ((bf16[2,128,768]{2,1,0:T(8,128)(2,1)}), bf16[2,128,768]{2,1,0:T(8,128)(2,1)S(1)}, u32[]{:S(2)}, u32[]{:S(2)}) async-start(bf16[2,128,768]{2,1,0:T(8,128)(2,1)} %bitcast.295), calls=%async_computation.9 | async-start | bytes 786432 | tf_op jit(solution)/shard_map/all_to_all | solution.py:454
  1484.3 9.6 all-to-all-start.6
  1487.8 791.4 %reduce-scatter.9.cloned.1.call-start = ((), (), s32[]{:S(2)}) async-start(), calls=%async_computation.22 | async-start | bytes 84934656 | tf_op jit(solution)/shard_map/reduce_scatter | solution.py:495
  1663.8 776.9 %all-reduce.4.cloned.1.call-start = ((), (), s32[]{:S(2)}) async-start(), calls=%async_computation.24 | async-start | bytes 12582912 | tf_op jit(solution)/shard_map/psum | solution.py:540
  1672.4 1042.1 %reduce-scatter.11.cloned.1.call-start = ((), (), s32[]{:S(2)}) async-start(), calls=%async_computation.23 | async-start | bytes 30081024 | tf_op jit(solution)/shard_map/reduce_scatter | solution.py:585
  (95 other events, 2320.0 us)
Sparse Core Ops, SparseCore 0:
  9.6 227.0 all-gather.7
  238.2 169.7 all-gather.9
  449.4 61.8 all-gather.11
  513.9 64.2 all-gather.13
  579.6 65.0 all-gather.15
  646.1 293.7 all-gather.17
  941.4 152.5 all-gather.19
  1253.3 142.1 reduce-scatter.6
  1399.9 84.3 reduce-scatter.4
  1663.9 615.2 reduce-scatter.8
  2284.9 155.8 all-reduce.3
  2445.4 269.1 reduce-scatter.10
where the time goes:
time: 2740 us; the launch traced here: 2730 us
  waiting for transfers between devices  1970 us (72%)
  local copies, waits for them, and re-layouts  247 us (9%)
  matrix products  182 us (7%)
  other arithmetic  168 us (6%)
  blocking collectives  64 us (2%)
  loops' own time  49.2 us (2%)
    reduce_scatter x1, waiting for transfers between devices, body(): lax.psum_scatter(jnp.concatenate(terms, axis=1).reshape(rows_each * lax.a...  607 us
    all_gather x1, waiting for transfers between devices, body(): lax.all_gather(w_gate_up, 'seq', axis=0, tiled=True)  247 us
    all_gather x1, waiting for transfers between devices, body(): lax.all_gather(ada_w, 'seq', axis=0, tiled=True)  221 us
    reduce_scatter x1, waiting for transfers between devices, body(): lax.psum_scatter(weight_grad_seq, 'bucket', scatter_dimension=1, tiled=True)  188 us
    all_gather x1, waiting for transfers between devices, body(): lax.all_gather(w_qkv, 'seq', axis=0, tiled=True)  159 us
    psum x1, waiting for transfers between devices, body(): lax.psum((norm_gain_grad, q_gain_grad, k_gain_grad, ky_gain_full, gate_fu...  139 us
    all_gather x1, waiting for transfers between devices, body(): lax.all_gather(w_down, 'seq', axis=0, tiled=True)  139 us
    reduce_scatter x1, waiting for transfers between devices, body(): lax.psum_scatter(value_terms.reshape(total_rows, local_width).astype(jnp....  108 us
  transfers between devices with their start and end apart: 19, of which 15 were waited for; matrix products, arithmetic and copies ran while one was open for 10% of the time, Pallas kernels for 0%

commit v1 on v0

--- a/solution.py
+++ b/solution.py
@@ -4,6 +4,8 @@
 import jax
 import jax.numpy as jnp
 from jax import lax
+from jax.experimental import pallas as pl
+from jax.experimental.pallas import tpu as pltpu
 from jax.sharding import PartitionSpec as P
 
 H = 24
@@ -15,9 +17,718 @@
 CAP = 128
 CLIPS = 4
 
-
 EPSILON = 1e-06
 MASKED = -1e30
+BF = jnp.bfloat16
+F32 = jnp.float32
+NN = (((1,), (0,)), ((), ()))
+NT = (((1,), (1,)), ((), ()))
+TN = (((0,), (0,)), ((), ()))
+
+
+def mm(a, b, dims):
+    return lax.dot_general(a, b, dims, preferred_element_type=F32)
+
+
+def norm_rope(raw, gain, cosine, sine):
+    inverse = lax.rsqrt(jnp.mean(raw * raw, axis=0, keepdims=True) + EPSILON)
+    normed = raw * inverse * gain
+    half = raw.shape[0] // 2
+    first, second = normed[:half], normed[half:]
+    return jnp.concatenate(
+        [first * cosine - second * sine, first * sine + second * cosine], axis=0
+    )
+
+
+def norm_rope_back(grad, raw, gain, cosine, sine):
+    inverse = lax.rsqrt(jnp.mean(raw * raw, axis=0, keepdims=True) + EPSILON)
+    unit = raw * inverse
+    half = raw.shape[0] // 2
+    first, second = grad[:half], grad[half:]
+    turned = jnp.concatenate(
+        [first * cosine + second * sine, second * cosine - first * sine], axis=0
+    )
+    gain_grad = jnp.sum(turned * unit, axis=1, keepdims=True)
+    unit_grad = turned * gain
+    raw_grad = inverse * (unit_grad - unit * jnp.mean(unit_grad * unit, axis=0, keepdims=True))
+    return raw_grad, gain_grad
+
+
+def attend_kernel(
+    heads, pieces, meta, gates, q_ref, *refs
+):
+    kv_refs = refs[:pieces]
+    (cap_ref, qg_ref, kg_ref, cos_ref, sin_ref) = refs[pieces : pieces + 5]
+    (comb_ref, own_ref, other_ref, stat_ref, qs_ref, ks_ref, vs_ref) = refs[pieces + 5 :]
+    width = heads * HD
+    count = q_ref.shape[0]
+    rows = q_ref.shape[2]
+    scale = HD**-0.5
+
+    for j, kv_ref in enumerate(kv_refs):
+        for k in range(kv_ref.shape[0]):
+            slot = meta[8 * count + j * kv_ref.shape[0] + k]
+            cosine, sine = cos_ref[slot], sin_ref[slot]
+            for h in range(heads):
+                at = slice(h * HD, h * HD + HD)
+                raw = kv_ref[k, at, :].astype(F32)
+                ks_ref[slot, at, :] = norm_rope(raw, kg_ref[at, :], cosine, sine).astype(BF)
+            vs_ref[slot] = kv_ref[k, width:, :]
+
+    def per_slice(i, carry):
+        slot = meta[8 * i + 4]
+        cosine, sine = cos_ref[slot], sin_ref[slot]
+        first, last = meta[8 * i], meta[8 * i + 1]
+        clip, length = meta[8 * i + 2], meta[8 * i + 3]
+        queries = []
+        for h in range(heads):
+            at = slice(h * HD, h * HD + HD)
+            raw = q_ref[i, at, :].astype(F32)
+            turned = norm_rope(raw, qg_ref[at, :], cosine, sine).astype(BF)
+            turned = (turned.astype(F32) * scale).astype(BF)
+            qs_ref[i, at, :] = turned
+            queries.append(turned)
+
+        def step(b, state):
+            totals, sums = state
+            new_totals, new_sums = [], []
+            for h in range(heads):
+                at = slice(h * HD, h * HD + HD)
+                weights = jnp.exp(mm(ks_ref[b, at, :], queries[h], TN))
+                new_totals.append(totals[h] + jnp.sum(weights, axis=0, keepdims=True))
+                new_sums.append(sums[h] + mm(vs_ref[b, at, :], weights.astype(BF), NN))
+            return tuple(new_totals), tuple(new_sums)
+
+        zero_total = tuple(jnp.zeros((1, rows), F32) for _ in range(heads))
+        zero_sum = tuple(jnp.zeros((HD, rows), F32) for _ in range(heads))
+        totals, sums = lax.fori_loop(first, last, step, (zero_total, zero_sum))
+        usable = lax.broadcasted_iota(jnp.int32, (CAP, rows), 0) < length
+        for h in range(heads):
+            at = slice(h * HD, h * HD + HD)
+            inverse = 1.0 / totals[h]
+            own = sums[h] * inverse
+            weights = jnp.where(usable, jnp.exp(mm(cap_ref[clip, at, :], queries[h], TN)), 0.0)
+            cap_inverse = 1.0 / jnp.sum(weights, axis=0, keepdims=True)
+            at_value = slice(width + h * HD, width + h * HD + HD)
+            other = mm(cap_ref[clip, at_value, :], weights.astype(BF), NN) * cap_inverse
+            own_ref[i, at, :] = own
+            other_ref[i, at, :] = other
+            comb_ref[i, at, :] = (own + gates[h] * other).astype(BF)
+            stat_ref[i, h : h + 1, :] = inverse
+            stat_ref[i, 4 + h : 5 + h, :] = cap_inverse
+        return carry
+
+    lax.fori_loop(0, count, per_slice, 0)
+
+
+def attend_back_kernel(heads, pieces, meta, gates, q_ref, *refs):
+    (g_ref, own_ref, other_ref, stat_ref, qs_ref, ks_ref, vs_ref) = refs[:7]
+    (cap_ref, qg_ref, cos_ref, sin_ref) = refs[7:11]
+    gq_ref, qgain_ref, dcap_ref, dgate_ref = refs[11:15]
+    dkv_refs = refs[15 : 15 + pieces]
+    acc_ref = refs[15 + pieces]
+    width = heads * HD
+    count = q_ref.shape[0]
+    rows = q_ref.shape[2]
+    scale = HD**-0.5
+    acc_ref[...] = jnp.zeros_like(acc_ref)
+    dcap_ref[...] = jnp.zeros_like(dcap_ref)
+    dgate_ref[...] = jnp.zeros_like(dgate_ref)
+    qgain_ref[...] = jnp.zeros_like(qgain_ref)
+
+    def per_slice(i, carry):
+        slot = meta[8 * i + 4]
+        first, last = meta[8 * i], meta[8 * i + 1]
+        clip, length = meta[8 * i + 2], meta[8 * i + 3]
+        queries, grads, deltas, inverses = [], [], [], []
+        for h in range(heads):
+            at = slice(h * HD, h * HD + HD)
+            grad = g_ref[i, at, :]
+            queries.append(qs_ref[i, at, :])
+            grads.append(grad)
+            deltas.append(jnp.sum(grad.astype(F32) * own_ref[i, at, :], axis=0, keepdims=True))
+            inverses.append(stat_ref[i, h : h + 1, :])
+
+        def step(b, state):
+            out = []
+            for h in range(heads):
+                at = slice(h * HD, h * HD + HD)
+                at_value = slice(width + h * HD, width + h * HD + HD)
+                keys, values = ks_ref[b, at, :], vs_ref[b, at, :]
+                prob = jnp.exp(mm(keys, queries[h], TN)) * inverses[h]
+                grad_prob = mm(values, grads[h], TN)
+                grad_score = (prob * (grad_prob - deltas[h])).astype(BF)
+                acc_ref[b, at_value, :] += mm(grads[h], prob.astype(BF), NT)
+                acc_ref[b, at, :] += mm(queries[h], grad_score, NT)
+                out.append(state[h] + mm(keys, grad_score, NN))
+            return tuple(out)
+
+        query_grads = lax.fori_loop(
+            first, last, step, tuple(jnp.zeros((HD, rows), F32) for _ in range(heads))
+        )
+        usable = lax.broadcasted_iota(jnp.int32, (CAP, rows), 0) < length
+        cosine, sine = cos_ref[slot], sin_ref[slot]
+        for h in range(heads):
+            at = slice(h * HD, h * HD + HD)
+            at_value = slice(width + h * HD, width + h * HD + HD)
+            cap_keys, cap_values = cap_ref[clip, at, :], cap_ref[clip, at_value, :]
+            grad = grads[h].astype(F32)
+            grad_other = (grad * gates[h]).astype(BF)
+            prob = (
+                jnp.where(usable, jnp.exp(mm(cap_keys, queries[h], TN)), 0.0)
+                * stat_ref[i, 4 + h : 5 + h, :]
+            )
+            grad_prob = mm(cap_values, grad_other, TN)
+            inner = jnp.sum(prob * grad_prob, axis=0, keepdims=True)
+            grad_score = (prob * (grad_prob - inner)).astype(BF)
+            query_grad = (query_grads[h] + mm(cap_keys, grad_score, NN)) * scale
+            dcap_ref[clip, at, :] += mm(queries[h], grad_score, NT)
+            dcap_ref[clip, at_value, :] += mm(grad_other, prob.astype(BF), NT)
+            part = jnp.sum(grad * other_ref[i, at, :], axis=0, keepdims=True)
+            dgate_ref[h : h + 1, :] += part
+            raw_grad, gain_grad = norm_rope_back(
+                query_grad.astype(BF).astype(F32), q_ref[i, at, :].astype(F32), qg_ref[at, :], cosine, sine
+            )
+            gq_ref[i, at, :] = raw_grad.astype(BF)
+            qgain_ref[at, :] += gain_grad
+        return carry
+
+    lax.fori_loop(0, count, per_slice, 0)
+    for j, dkv_ref in enumerate(dkv_refs):
+        for k in range(dkv_ref.shape[0]):
+            slot = meta[8 * count + j * dkv_ref.shape[0] + k]
+            dkv_ref[k] = acc_ref[slot].astype(BF)
+
+
+def vmem_specs(n):
+    return [pl.BlockSpec(memory_space=pltpu.VMEM) for _ in range(n)]
+
+
+SMEM = pl.BlockSpec(memory_space=pltpu.SMEM)
+
+
+def attend(heads, meta, gates, queries, kv_pieces, cap_kv, q_gain, k_gain, cosine, sine):
+    count, width, rows = queries.shape
+    slots = cosine.shape[0]
+    shape = jax.ShapeDtypeStruct
+    return pl.pallas_call(
+        functools.partial(attend_kernel, heads, len(kv_pieces)),
+        in_specs=[SMEM, SMEM] + vmem_specs(1 + len(kv_pieces) + 5),
+        out_specs=vmem_specs(7),
+        out_shape=[
+            shape((count, width, rows), BF),
+            shape((count, width, rows), F32),
+            shape((count, width, rows), F32),
+            shape((count, 8, rows), F32),
+            shape((count, width, rows), BF),
+            shape((slots, width, rows), BF),
+            shape((slots, width, rows), BF),
+        ],
+        name="attend",
+    )(meta, gates, queries, *kv_pieces, cap_kv, q_gain, k_gain, cosine, sine)
+
+
+def attend_back(heads, meta, gates, queries, grads, saved, cap_kv, q_gain, cosine, sine, kv_shapes):
+    count, width, rows = queries.shape
+    slots = cosine.shape[0]
+    shape = jax.ShapeDtypeStruct
+    own, other, stat, qs, ks, vs = saved
+    return pl.pallas_call(
+        functools.partial(attend_back_kernel, heads, len(kv_shapes)),
+        in_specs=[SMEM, SMEM] + vmem_specs(12),
+        out_specs=vmem_specs(4 + len(kv_shapes)),
+        out_shape=[
+            shape((count, width, rows), BF),
+            shape((width, 1), F32),
+            shape((CLIPS, 2 * width, CAP), F32),
+            shape((8, rows), F32),
+        ]
+        + [shape(s, BF) for s in kv_shapes],
+        scratch_shapes=[pltpu.VMEM((slots, 2 * width, rows), F32)],
+        name="attend_back",
+    )(meta, gates, queries, grads, own, other, stat, qs, ks, vs, cap_kv, q_gain, cosine, sine)
+
+
+def keys_back_kernel(heads, meta, a_ref, r_ref, kv_ref, kg_ref, cos_ref, sin_ref, out_ref, gain_ref):
+    width = heads * HD
+    gain_ref[...] = jnp.zeros_like(gain_ref)
+    for i in range(a_ref.shape[0]):
+        slot = meta[8 * i + 4]
+        cosine, sine = cos_ref[slot], sin_ref[slot]
+        total = (a_ref[i].astype(F32) + r_ref[i].astype(F32)).astype(BF)
+        for h in range(heads):
+            at = slice(h * HD, h * HD + HD)
+            raw_grad, gain_grad = norm_rope_back(
+                total[at, :].astype(F32), kv_ref[i, at, :].astype(F32), kg_ref[at, :], cosine, sine
+            )
+            out_ref[i, at, :] = raw_grad.astype(BF)
+            gain_ref[at, :] += gain_grad
+        out_ref[i, width:, :] = total[width:, :]
+
+
+def keys_back(heads, meta, part, received, kv, k_gain, cosine, sine):
+    shape = jax.ShapeDtypeStruct
+    return pl.pallas_call(
+        functools.partial(keys_back_kernel, heads),
+        in_specs=[SMEM] + vmem_specs(6),
+        out_specs=vmem_specs(2),
+        out_shape=[shape(kv.shape, BF), shape((heads * HD, 1), F32)],
+        name="keys_back",
+    )(meta, part, received, kv, k_gain, cosine, sine)
+
+
+def weight_kernel(count, dims, *refs):
+    left, right, out_ref = refs[:count], refs[count : 2 * count], refs[2 * count]
+    total = None
+    for a_ref, g_ref in zip(left, right):
+        part = mm(a_ref[0].reshape(-1, a_ref.shape[-1]), g_ref[...], dims)
+        total = part if total is None else total + part
+    out_ref[...] = total.reshape(out_ref.shape).astype(BF)
+
+
+def weight_grads(left, right, by_rows, tile, which):
+    kinds, chunks, columns, tokens = left[0].shape
+    rows = right[0].shape[0 if by_rows else 1]
+    left_spec = pl.BlockSpec((1, chunks, columns, tokens), lambda i: (which(i), 0, 0, 0))
+    if by_rows:
+        right_spec = pl.BlockSpec((tile, tokens), lambda i: (i, 0))
+    else:
+        right_spec = pl.BlockSpec((tokens, tile), lambda i: (0, i))
+    return pl.pallas_call(
+        functools.partial(weight_kernel, len(left), NT if by_rows else NN),
+        grid=(rows // tile,),
+        in_specs=[left_spec] * len(left) + [right_spec] * len(right),
+        out_specs=pl.BlockSpec((chunks, columns, tile), lambda i: (0, 0, i)),
+        out_shape=jax.ShapeDtypeStruct((chunks, columns, rows), BF),
+        name="weight_grads",
+    )(*left, *right)
+
+
+def fast_body(
+    tokens,
+    cotangent,
+    clip_slices,
+    caption_lengths,
+    caption,
+    cond,
+    ada_w,
+    norm_gain,
+    w_qkv,
+    q_gain,
+    k_gain,
+    w_caption,
+    ky_gain,
+    cross_gate,
+    w_out,
+    ffn_gain,
+    w_gate_up,
+    w_down,
+):
+    seq_count = lax.axis_size("seq")
+    bucket_count = lax.axis_size("bucket")
+    tok_rows = tokens.shape[0]
+    rows = tok_rows * seq_count
+    group = 4
+    line = bucket_count // group
+    local_width = D // seq_count
+    width = local_width // line
+    heads = width // HD
+    units = FF // seq_count
+    b = lax.axis_index("bucket")
+    s = lax.axis_index("seq")
+    z, g, c = b // group, b % group, b % 2
+    first = s == 0
+
+    def xswap(v):
+        return lax.ppermute(v, "seq", [(0, 1), (1, 0)])
+
+    def hop(v, to):
+        return lax.ppermute(v, "bucket", [(i, to(i)) for i in range(bucket_count)])
+
+    def cswap(v):
+        return hop(v, lambda i: i ^ 1)
+
+    def yswap(v):
+        return hop(v, lambda i: i ^ 2)
+
+    def zshift(v, k):
+        return hop(v, lambda i: (i + group * k) % bucket_count)
+
+    def join(own, other, axis):
+        return jnp.where(
+            first,
+            jnp.concatenate([own, other], axis),
+            jnp.concatenate([other, own], axis),
+        )
+
+    def take(v, index, size, axis):
+        return lax.dynamic_slice_in_dim(v, index * size, size, axis)
+
+    def pick(v, index):
+        return lax.dynamic_index_in_dim(v, index, 0, False)
+
+    ends_s = jnp.cumsum(clip_slices).astype(jnp.int32)
+    starts_s = ends_s - clip_slices
+    slot_ids = jnp.arange(bucket_count, dtype=jnp.int32)
+    slot_clip = jnp.sum((slot_ids[:, None] >= ends_s[None, :]).astype(jnp.int32), axis=1)
+    slot_start = starts_s[slot_clip]
+    my_clip = slot_clip[b]
+    clip_mask = jnp.arange(CLIPS) == my_clip
+    half = HD // 2
+    frequency = jnp.exp(
+        jnp.arange(half, dtype=F32) * (-2.0 * math.log(10000.0) / (2 * half))
+    )
+    positions = (
+        (slot_ids - slot_start)[:, None] * rows + jnp.arange(rows, dtype=jnp.int32)[None, :]
+    ).astype(F32)
+    angles = positions[:, None, :] * frequency[None, :, None]
+    cosine, sine = jnp.cos(angles), jnp.sin(angles)
+    line_ids = jnp.arange(line, dtype=jnp.int32)
+    my_slots = ((z - line_ids) % line) * group + g
+    my_clips = slot_clip[my_slots]
+    zeros = jnp.zeros_like(my_slots)
+    meta = jnp.stack(
+        [
+            starts_s[my_clips],
+            ends_s[my_clips],
+            my_clips,
+            caption_lengths[my_clips],
+            my_slots,
+            zeros,
+            zeros,
+            zeros,
+        ],
+        axis=1,
+    ).reshape(-1)
+    piece_slots = (
+        ((z - line_ids) % line)[None, :] * group
+        + (g ^ jnp.arange(group, dtype=jnp.int32))[:, None]
+    ).reshape(-1)
+    meta = jnp.concatenate([meta, piece_slots]).astype(jnp.int32)
+
+    tok_pair = join(tokens, xswap(tokens), 0).astype(F32)
+    activation = jax.nn.silu(cond).astype(BF)
+    cond_row = lax.dynamic_index_in_dim(activation, my_clip, 0, True)
+    mod_local = mm(cond_row, ada_w, NT)
+    modulation = join(mod_local, xswap(mod_local), 0).reshape(6, D)
+    shift_vec, scale_vec, gate_vec, shift_mlp, scale_mlp, gate_mlp = [
+        modulation[i : i + 1] for i in range(6)
+    ]
+    inverse = lax.rsqrt(jnp.mean(tok_pair * tok_pair, axis=-1, keepdims=True) + EPSILON)
+    hidden = (tok_pair * inverse * norm_gain * (1.0 + scale_vec) + shift_vec).astype(BF)
+    cot_pair = join(cotangent, xswap(cotangent), 0).astype(F32)
+
+    projected = mm(w_qkv, hidden, NT).astype(BF).reshape(3, local_width, rows)
+    swapped = xswap(projected[1])
+    raw_q = jnp.where(first, projected[0], swapped).reshape(line, width, rows)
+    raw_k = jnp.where(first, projected[2], projected[0]).reshape(line, width, rows)
+    raw_v = jnp.where(first, swapped, projected[2]).reshape(line, width, rows)
+
+    def spread(v):
+        parts = [pick(v, z)] + [zshift(pick(v, (z + k) % line), k) for k in range(1, line)]
+        return jnp.stack(parts)
+
+    def unspread(v):
+        parts = [v[0]] + [zshift(v[k], line - k) for k in range(1, line)]
+        twice = jnp.stack(parts + parts)
+        return lax.dynamic_slice_in_dim(twice, (line - z) % line, line, 0)
+
+    kv_own = spread(jnp.concatenate([raw_k, raw_v], axis=1))
+    queries = spread(raw_q)
+    kv_y = yswap(kv_own)
+    kv_c = cswap(kv_own)
+    kv_pieces = [kv_own, kv_c, kv_y, cswap(kv_y)]
+
+    w_cap = lax.dynamic_slice_in_dim(w_caption, z * width, width, 1)
+    cap_raw = mm(
+        w_cap.reshape(2 * width, YD), caption.reshape(CLIPS * CAP, YD), NT
+    )
+    head_first = s * local_width + z * width
+
+    def mine(gain):
+        return lax.dynamic_slice_in_dim(gain, head_first, width)[:, None]
+
+    q_gain_c, k_gain_c, ky_gain_c = mine(q_gain), mine(k_gain), mine(ky_gain)
+    cap_split = cap_raw[:width].reshape(heads, HD, CLIPS * CAP)
+    cap_inverse = lax.rsqrt(jnp.mean(cap_split * cap_split, axis=1, keepdims=True) + EPSILON)
+    cap_unit = (cap_split * cap_inverse).reshape(width, CLIPS * CAP)
+    cap_kv = jnp.concatenate([cap_unit * ky_gain_c, cap_raw[width:]], axis=0).astype(BF)
+    cap_kv = cap_kv.reshape(2 * width, CLIPS, CAP).transpose(1, 0, 2)
+    gates = jnp.tanh(lax.dynamic_slice_in_dim(cross_gate, s * (H // seq_count) + z * heads, heads))
+
+    combined, *saved = attend(
+        heads, meta, gates, queries, kv_pieces, cap_kv, q_gain_c, k_gain_c, cosine, sine
+    )
+    heads_back = unspread(combined).reshape(local_width, rows)
+    attention = join(heads_back, xswap(heads_back), 0)
+
+    branch_local = mm(attention, w_out, (((0,), (1,)), ((), ()))).astype(BF)
+    branch = join(branch_local, xswap(branch_local), 1).astype(F32)
+    middle = tok_pair + gate_vec * branch
+    mid_inverse = lax.rsqrt(jnp.mean(middle * middle, axis=-1, keepdims=True) + EPSILON)
+    mid_unit = middle * mid_inverse
+    mlp_gain = ffn_gain * (1.0 + scale_mlp)
+    mlp_in = (mid_unit * mlp_gain + shift_mlp).astype(BF)
+
+    quarter = units // 2
+    sent = lax.dynamic_slice_in_dim(w_gate_up, (1 - s) * units + c * quarter, quarter, 0)
+    came = xswap(sent)
+    came_too = cswap(came)
+    w_came = jnp.where(
+        c == 0, jnp.concatenate([came, came_too], 0), jnp.concatenate([came_too, came], 0)
+    )
+    w_kept = take(w_gate_up, s, units, 0)
+    kept = mm(mlp_in, w_kept, NT)
+    other = mm(mlp_in, w_came, NT)
+    gate_half = jnp.where(first, kept, other)
+    up_half = jnp.where(first, other, kept)
+    gate_sigmoid = jax.nn.sigmoid(gate_half)
+    silu_gate = gate_half * gate_sigmoid
+    inner = (silu_gate * up_half).astype(BF)
+    grad_mlp = (cot_pair * gate_mlp).astype(BF)
+    grad_inner = mm(grad_mlp, w_down, NT)
+    grad_gate = (
+        grad_inner * up_half * gate_sigmoid * (1.0 + gate_half * (1.0 - gate_sigmoid))
+    ).astype(BF)
+    grad_up = (grad_inner * silu_gate).astype(BF)
+    grad_kept = jnp.where(first, grad_gate, grad_up)
+    grad_came = jnp.where(first, grad_up, grad_gate)
+    mlp_in_part = mm(grad_kept, w_kept, NN) + mm(grad_came, w_came, NN)
+
+    mean_part = jnp.sum(mlp_in_part * mlp_gain * mid_unit, axis=-1, keepdims=True)
+    mean_all = (mean_part + xswap(mean_part)) * (1.0 / D)
+
+    def cols(v):
+        return take(v, s, local_width, v.ndim - 1)
+
+    def far(v, axis):
+        return take(v, 1 - s, v.shape[axis] // 2, axis)
+
+    def near(v, axis):
+        return take(v, s, v.shape[axis] // 2, axis)
+
+    mlp_in_grad = cols(mlp_in_part) + xswap(far(mlp_in_part, 1).astype(BF)).astype(F32)
+    unit_c = cols(mid_unit)
+    scale_mlp_c = cols(scale_mlp)
+    ffn_gain_c = cols(ffn_gain)
+    ffn_gain_grad = jnp.sum(mlp_in_grad * (1.0 + scale_mlp_c) * unit_c, axis=0)
+    shift_mlp_grad = jnp.sum(mlp_in_grad, axis=0)
+    scale_mlp_grad = jnp.sum(mlp_in_grad * unit_c * ffn_gain_c, axis=0)
+    grad_middle = cols(cot_pair) + mid_inverse * (
+        mlp_in_grad * ffn_gain_c * (1.0 + scale_mlp_c) - unit_c * mean_all
+    )
+    gate_grad = jnp.sum(grad_middle * cols(branch), axis=0)
+    grad_branch = (grad_middle * cols(gate_vec)).astype(BF)
+    attention_part = mm(w_out, grad_branch, (((0,), (1,)), ((), ())))
+    grad_heads = (near(attention_part, 0) + xswap(far(attention_part, 0).astype(BF)).astype(F32)).astype(BF)
+    grad_heads = spread(grad_heads.reshape(line, width, rows))
+
+    grad_q, q_gain_part, cap_part, gate_part, *grad_kv = attend_back(
+        heads,
+        meta,
+        gates,
+        queries,
+        grad_heads,
+        saved,
+        cap_kv,
+        q_gain_c,
+        cosine,
+        sine,
+        [kv_own.shape] * group,
+    )
+    here = (grad_kv[0].astype(F32) + cswap(grad_kv[1]).astype(F32)).astype(BF)
+    away = (grad_kv[2].astype(F32) + cswap(grad_kv[3]).astype(F32)).astype(BF)
+    grad_kv_raw, k_gain_part = keys_back(
+        heads, meta, here, yswap(away), kv_own, k_gain_c, cosine, sine
+    )
+    grad_qkv = unspread(jnp.concatenate([grad_q, grad_kv_raw], axis=1)).reshape(line, 3, width, rows)
+    back_q, back_k, back_v = [grad_qkv[:, i].reshape(local_width, rows) for i in range(3)]
+    back_swap = xswap(jnp.where(first, back_v, back_q))
+    grad_projected = jnp.concatenate(
+        [
+            jnp.where(first, back_q, back_k),
+            back_swap,
+            jnp.where(first, back_k, back_v),
+        ],
+        axis=0,
+    )
+    hidden_part = mm(grad_projected, w_qkv, TN)
+    hidden_grad = near(hidden_part, 0) + xswap(far(hidden_part, 0).astype(BF)).astype(F32)
+
+    middle_own = join(near(grad_middle, 0), xswap(far(grad_middle, 0)), 1)
+    tok_own = tokens.astype(F32)
+    inverse_own = near(inverse, 0)
+    unit_own = tok_own * inverse_own
+    unit_grad = hidden_grad * norm_gain * (1.0 + scale_vec)
+    token_grad = (
+        inverse_own
+        * (unit_grad - unit_own * jnp.mean(unit_grad * unit_own, axis=-1, keepdims=True))
+        + middle_own
+    )
+    norm_gain_grad = jnp.sum(hidden_grad * (1.0 + scale_vec) * unit_own, axis=0)
+    shift_grad = jnp.sum(hidden_grad, axis=0)
+    scale_grad = jnp.sum(hidden_grad * unit_own * norm_gain, axis=0)
+
+    mlp_part = mm(inner, w_down, NN)
+    mlp_branch = near(mlp_part, 0) + xswap(far(mlp_part, 0).astype(BF)).astype(F32)
+    output = (near(middle, 0) + gate_mlp * mlp_branch).astype(BF)
+    mlp_gate_grad = jnp.sum(cotangent.astype(F32) * mlp_branch, axis=0)
+
+    def gather_left(values):
+        cut = jnp.stack([v.reshape(line, group, D // bucket_count, rows) for v in values])
+
+        def of(index):
+            return lax.dynamic_index_in_dim(cut, index, 2, False)
+
+        came_y = yswap(jnp.stack([of(g ^ 2), of(g ^ 3)]))
+        came_c = cswap(jnp.stack([of(g ^ 1), came_y[1]]))
+        return [of(g), came_c[0], came_y[0], came_c[1]]
+
+    def gather_right(v):
+        far_v = yswap(v)
+        return [v, cswap(v), far_v, cswap(far_v)]
+
+    right_line = [(i, i + group) for i in range(bucket_count - group)]
+
+    def line_sum(parts):
+        parts_f = parts
+        left_in = right_in = None
+        for t in range(1, line):
+            to_right = lax.dynamic_index_in_dim(parts_f, jnp.clip(line - t + z, 0, line - 1), 0, False)
+            to_left = lax.dynamic_index_in_dim(parts_f, jnp.clip(t - 1 - (line - 1 - z), 0, line - 1), 0, False)
+            if t > 1:
+                to_right = (to_right.astype(F32) + right_in.astype(F32)).astype(BF)
+                to_left = (to_left.astype(F32) + left_in.astype(F32)).astype(BF)
+            pairs = [(i, i + group) for i in range(group * t)]
+            right_in = lax.ppermute(to_right, "bucket", pairs)
+            pairs = [
+                (bucket_count - 1 - i, bucket_count - 1 - i - group) for i in range(group * t)
+            ]
+            left_in = lax.ppermute(to_left, "bucket", pairs)
+        own = lax.dynamic_index_in_dim(parts_f, z, 0, False)
+        return own.astype(F32) + right_in.astype(F32) + left_in.astype(F32)
+
+    ffn_left = gather_left([grad_mlp.T, mlp_in.T])
+    ffn_right = gather_right(jnp.concatenate([inner, grad_kept, grad_came], axis=1))
+    tile = 512
+    down_tiles = units // tile
+    ffn_parts = weight_grads(
+        ffn_left, ffn_right, False, tile, lambda i: jnp.where(i < down_tiles, 0, 1)
+    )
+    ffn_sum = line_sum(ffn_parts)
+    down_grad_out = ffn_sum[:, :units].T
+    kept_grad = ffn_sum[:, units : 2 * units]
+    came_grad = xswap(ffn_sum[:, 2 * units :].astype(BF)).astype(F32)
+    gate_up_grad_out = join(kept_grad, came_grad, 1).T
+
+    out_left = gather_left([attention])
+    out_right = gather_right(grad_branch)
+    out_parts = weight_grads(out_left, out_right, False, 384, lambda i: 0)
+    out_grad_out = line_sum(out_parts).T
+    qkv_left = gather_left([hidden.T])
+    qkv_right = gather_right(grad_projected)
+    qkv_parts = weight_grads(qkv_left, qkv_right, True, 384, lambda i: 0)
+    qkv_grad_out = line_sum(qkv_parts).T
+
+    cap_c = cap_part.reshape(2, 2, 2 * width, CAP)
+    pair_sum = pick(cap_c.transpose(1, 0, 2, 3), c) + cswap(pick(cap_c.transpose(1, 0, 2, 3), 1 - c))
+    y = (b // 2) % 2
+    cap_sum = pick(pair_sum, y) + yswap(pick(pair_sum, 1 - y))
+    unit_g = lax.dynamic_slice_in_dim(cap_unit, g * CAP, CAP, 1)
+    cap_inverse_g = lax.dynamic_slice_in_dim(cap_inverse, g * CAP, CAP, 2)
+    key_sum = cap_sum[:width]
+    ky_gain_part = jnp.sum(key_sum * unit_g, axis=1)
+    key_unit_grad = (key_sum * ky_gain_c).reshape(heads, HD, CAP)
+    unit_g3 = unit_g.reshape(heads, HD, CAP)
+    raw_key_grad = cap_inverse_g * (
+        key_unit_grad - unit_g3 * jnp.mean(key_unit_grad * unit_g3, axis=1, keepdims=True)
+    )
+    raw_cap = jnp.concatenate([raw_key_grad.reshape(width, CAP), cap_sum[width:]], 0).astype(BF)
+    raw_all = lax.all_gather(raw_cap, "bucket", axis=0, tiled=False)
+    raw_all = raw_all.reshape(line, CLIPS, 2, width, CAP)
+    caption_cols = lax.dynamic_slice_in_dim(
+        caption, b * (YD // bucket_count), YD // bucket_count, 2
+    )
+    caption_w_grad = jnp.einsum(
+        "zcjwt,cty->jzwy", raw_all, caption_cols, preferred_element_type=F32
+    ).reshape(2, local_width, YD // bucket_count)
+
+    def place(v, size, at):
+        return lax.dynamic_update_slice_in_dim(jnp.zeros((size,), F32), v, at, 0)
+
+    def total(v):
+        v = v + cswap(v)
+        v = v + yswap(v)
+        v = v + hop(v, lambda i: i ^ group)
+        v = v + hop(v, lambda i: i ^ (2 * group))
+        return v + xswap(v)
+
+    early = jnp.concatenate(
+        [
+            place(gate_grad, D, s * local_width),
+            place(shift_mlp_grad, D, s * local_width),
+            place(scale_mlp_grad, D, s * local_width),
+            mlp_gate_grad,
+        ]
+    )
+    early_rows = jnp.where(clip_mask[:, None], early[None, :], 0.0).reshape(-1, 128)
+    early_all = jnp.concatenate(
+        [early_rows, place(ffn_gain_grad, D, s * local_width).reshape(-1, 128)], axis=0
+    )
+    early_sum = total(early_all)
+    early_mod = early_sum[: CLIPS * 4 * D // 128].reshape(CLIPS, 4 * D)
+    ffn_gain_out = early_sum[CLIPS * 4 * D // 128 :].reshape(-1)
+    late = jnp.concatenate([shift_grad, scale_grad])
+    late_rows = jnp.where(clip_mask[:, None], late[None, :], 0.0).reshape(-1, 128)
+    head_grads = lax.dynamic_update_slice_in_dim(
+        jnp.zeros((128,), F32),
+        jnp.sum(gate_part[:heads], axis=1) * (1.0 - gates * gates),
+        s * (H // seq_count) + z * heads,
+        0,
+    )
+    late_all = jnp.concatenate(
+        [
+            late_rows,
+            norm_gain_grad.reshape(-1, 128),
+            place(q_gain_part[:, 0], D, head_first).reshape(-1, 128),
+            place(k_gain_part[:, 0], D, head_first).reshape(-1, 128),
+            place(ky_gain_part, D, head_first).reshape(-1, 128),
+            head_grads.reshape(1, 128),
+        ],
+        axis=0,
+    )
+    late_sum = total(late_all)
+    n_late = CLIPS * 2 * D // 128
+    per = D // 128
+    late_mod = late_sum[:n_late].reshape(CLIPS, 2 * D)
+    gain_rows = late_sum[n_late : n_late + 4 * per].reshape(4, D)
+    cross_gate_out = late_sum[n_late + 4 * per, :H]
+    mod_total = jnp.concatenate([late_mod, early_mod], axis=1).astype(BF)
+    mod_mine = take(mod_total, s, 6 * D // seq_count, 1)
+    cols_local = CD // bucket_count
+    ada_grad = mm(mod_mine, take(activation, b, cols_local, 1), TN)
+    cond_part = mm(mod_mine, ada_w, NN)
+    cond_sigmoid = jax.nn.sigmoid(cond)
+    cond_grad = (
+        (cond_part + xswap(cond_part)) * cond_sigmoid * (1.0 + cond * (1.0 - cond_sigmoid))
+    )
+    return (
+        output,
+        token_grad,
+        cond_grad,
+        ada_grad,
+        gain_rows[0],
+        qkv_grad_out,
+        gain_rows[1],
+        gain_rows[2],
+        caption_w_grad,
+        gain_rows[3],
+        cross_gate_out,
+        out_grad_out,
+        ffn_gain_out,
+        gate_up_grad_out,
+        down_grad_out,
+    )
 
 
 def project(activations, weight):
@@ -71,7 +782,7 @@
     return 512 if row_count % 512 == 0 else row_count
 
 
-def body(
+def general_body(
     tokens,
     cotangent,
     clip_slices,
@@ -646,4 +1357,6 @@
         P("seq", "bucket"),
         P("seq", "bucket"),
     )
+    fits = mesh.shape["seq"] == 2 and mesh.shape["bucket"] == 16
+    body = fast_body if fits else general_body
     return jax.shard_map(body, mesh=mesh, in_specs=in_specs, out_specs=out_specs, check_vma=False)

time: 2740 us -> 768 us (0.28)
  waiting for transfers between devices: 1970 us -> 261 us
  local copies, waits for them, and re-layouts: 247 us -> 92.7 us
  starting transfers between devices: 25 us -> 149 us
  matrix products: 182 us -> 64 us
  Pallas kernels: 0 us -> 86 us
  other arithmetic: 168 us -> 86.5 us
  blocking collectives: 64 us -> 0 us
  loops' own time: 49.2 us -> 0 us
    reduce_scatter x4 -> x0, waiting for transfers between devices: 979 us -> none  [the longest x1 607 us: body(): lax.psum_scatter(jnp.concatenate(terms, axis=1).reshape(rows_each * lax.a...]
    all_gather x7 -> x1, waiting for transfers between devices: 837 us -> 0.01 us  [fast_body(): raw_all = lax.all_gather(raw_cap, 'bucket', axis=0, tiled=False)]
    ppermute x0 -> x83, waiting for transfers between devices: none -> 261 us  [the longest x47 153 us: hop(): return lax.ppermute(v, 'bucket', [(i, to(i)) for i in range(bucket_count)])]
    ppermute x0 -> x83, starting transfers between devices: none -> 149 us  [the longest x47 61.1 us: hop(): return lax.ppermute(v, 'bucket', [(i, to(i)) for i in range(bucket_count)])]
    psum x1 -> x0, waiting for transfers between devices: 139 us -> none  [body(): lax.psum((norm_gain_grad, q_gain_grad, k_gain_grad, ky_gain_full, gate_fu...]
    dot_general x40 -> x15, matrix products: 181 us -> 64 us  [the longest x14 61.9 us: mm(): return lax.dot_general(a, b, dims, preferred_element_type=F32)]
    pallas_call x0 -> x6, Pallas kernels: none -> 86 us  [the longest x1 31.5 us: attend_back(): pl.pallas_call(functools.partial(attend_back_kernel, heads, len(kv_shapes...]
    convert_element_type x9 -> x5, local copies, waits for them, and re-layouts: 80.4 us -> 3.6 us  [the longest x1 1.93 us: fast_body(): (near(attention_part, 0) + xswap(far(attention_part, 0).astype(BF)).astyp...]
  transfers between devices with their start and end apart: 19 -> 84, of which waited for: 15 -> 30; matrix products, arithmetic and copies ran while one was open for 10% -> 24% of each run, Pallas kernels for 0% -> 11%
where the time goes in v1:
time: 768 us; the launch traced here: 758 us
  waiting for transfers between devices  261 us (34%)
  starting transfers between devices  149 us (19%)
  local copies, waits for them, and re-layouts  92.7 us (12%)
  other arithmetic  86.5 us (11%)
  Pallas kernels  86 us (11%)
  matrix products  64 us (8%)
  between operations  18.3 us (2%)
    ppermute x47, waiting for transfers between devices, hop(): return lax.ppermute(v, 'bucket', [(i, to(i)) for i in range(bucket_count)])  153 us
    ppermute x18, waiting for transfers between devices, xswap(): return lax.ppermute(v, 'seq', [(0, 1), (1, 0)])  65.9 us
    dot_general x14, matrix products, mm(): return lax.dot_general(a, b, dims, preferred_element_type=F32)  61.9 us
    ppermute x47, starting transfers between devices, hop(): return lax.ppermute(v, 'bucket', [(i, to(i)) for i in range(bucket_count)])  61.1 us
    ppermute x9, starting transfers between devices, line_sum(): right_in = lax.ppermute(to_right, 'bucket', pairs)  54.2 us
    ppermute x9, waiting for transfers between devices, line_sum(): right_in = lax.ppermute(to_right, 'bucket', pairs)  34.1 us
    pallas_call x1, Pallas kernels, attend_back(): pl.pallas_call(functools.partial(attend_back_kernel, heads, len(kv_shapes...  31.5 us
    pallas_call x1, Pallas kernels, attend(): pl.pallas_call(functools.partial(attend_kernel, heads, len(kv_pieces)), i...  26.5 us
  transfers between devices with their start and end apart: 84, of which 30 were waited for; matrix products, arithmetic and copies ran while one was open for 24% of the time, Pallas kernels for 11%

profile of v1, /device:TPU:0, one launch (start us, length us, event | category | flops | bytes accessed | tf_op | source)
XLA Modules:
  0.0 757.9 jit_solution(1869960331075332009)
XLA Ops:
  11.6 6.3 fusion.69
  49.4 7.0 collective-permute-done.2
  71.5 8.5 %collective-permute-done.7 = bf16[384,256]{1,0:T(8,128)(2,1)S(1)} collective-permute-done((bf16[384,256]{1,0:T(8,128)(2,1)}, bf16[384,256]{1,0:T(8,128)(2,1)S(1)}, u32[]{:S(2)}, u32[]{:S(2)}) %collective-permute-start.7) | collective-permute-done | bytes 196640 | tf_op jit(solution)/shard_map/ppermute | solution.py:346
  86.5 13.7 %collective-permute-done.10.refs_2_ = bf16[4,384,256]{2,1,0:T(8,128)(2,1)} collective-permute-done((bf16[4,384,256]{2,1,0:T(8,128)(2,1)S(1)}, bf16[4,384,256]{2,1,0:T(8,128)(2,1)}, u32[]{:S(2)}, u32[]{:S(2)}) %collective-permute-start.10) | collective-permute-done | bytes 786464 | tf_op jit(solution)/shard_map/ppermute | solution.py:346
  122.1 26.5 %attend.1 = (bf16[4,192,256]{2,1,0:T(8,128)(2,1)}, f32[4,192,256]{2,1,0:T(8,128)}, f32[4,192,256]{2,1,0:T(8,128)}, f32[4,8,256]{2,1,0:T(8,128)}, bf16[4,192,256]...) custom-call(s32[48]{0:T(128)} %pad_add_fusion.meta, f32[3]{0:T(128)} %dynamic-slice_tanh_fusion.gates, ...), custom_call_target="tpu_custom_call" | custom-call | tf_op jit(solution)/shard_map/attend/pallas_call | solution.py:214
  155.2 8.3 %collective-permute-done.13 = bf16[192,256]{1,0:T(8,128)(2,1)S(1)} collective-permute-done((bf16[192,256]{1,0:T(8,128)(2,1)S(1)}, bf16[192,256]{1,0:T(8,128)(2,1)S(1)}, u32[]{:S(2)}, u32[]{:S(2)}) %collective-permute-start.13) | collective-permute-done | bytes 98336 | tf_op jit(solution)/shard_map/ppermute | solution.py:346
  165.2 28.4 %collective-permute-done.20 = bf16[128,1536]{1,0:T(8,128)(2,1)} collective-permute-done((bf16[128,1536]{1,0:T(8,128)(2,1)}, bf16[128,1536]{1,0:T(8,128)(2,1)}, u32[]{:S(2)}, u32[]{:S(2)}) %collective-permute-start.20) | collective-permute-done | bytes 393248 | tf_op jit(solution)/shard_map/ppermute | solution.py:343
  239.0 8.7 %collective-permute-done.71 = bf16[2,2,4,96,256]{4,3,2,1,0:T(8,128)(2,1)S(1)} collective-permute-done((bf16[2,2,4,96,256]{4,3,2,1,0:T(8,128)(2,1)S(1)}, bf16[2,2,4,96,256]{4,3,2,1,0:T(8,128)(2,1)S(1)}, u32[]{:S(2)}, u32[]{:S(2)}) %collective-permute-start.71) | collective-permute-done | bytes 786464 | tf_op jit(solution)/shard_map/ppermute | solution.py:346
  253.4 8.4 %multiply_convert_fusion.2 = (bf16[256,2048]{1,0:T(8,128)(2,1)S(1)}, f32[256,2048]{1,0:T(8,128)}) fusion(f32[256,2048]{1,0:T(8,128)S(1)} %fusion.2, pred[]{:T(512)S(6)} %eq.34, bf16[256,1536]{1,0:T(8,128)(2,1)S(1)} %copy-done.13, bf16[1024,1536]{1,0:T(8,128)(2,1)} %collective-permute-done.18, bf16[1024,1536]{1,0:T(8,128)(2,1)} %collective-permute-done.17, ...), kind=kOutput, calls=%fused_computation.37 | convolution fusion | flops 1643118592 | bytes 12320770 | tf_op jit(solution)/shard_map/dot_general | solution.py:30
  266.8 7.2 broadcast_select_fusion
  287.0 7.8 %collective-permute-done.22 = f32[256,1]{0,1:T(1,128)S(1)} collective-permute-done((f32[256,1]{0,1:T(1,128)S(1)}, f32[256,1]{0,1:T(1,128)S(1)}, u32[]{:S(2)}, u32[]{:S(2)}) %collective-permute-start.22) | collective-permute-done | bytes 1056 | tf_op jit(solution)/shard_map/ppermute | solution.py:343
  340.4 31.5 %attend_back.1 = (bf16[4,192,256]{2,1,0:T(8,128)(2,1)}, f32[192,1]{1,0:T(8,128)}, f32[4,384,128]{2,1,0:T(8,128)}, f32[8,256]{1,0:T(8,128)}, bf16[4,384,256]{2,1,...) custom-call(s32[48]{0:T(128)} %pad_add_fusion.meta, ...), custom_call_target="tpu_custom_call" | custom-call | tf_op jit(solution)/shard_map/attend_back/pallas_call | solution.py:236
  379.1 8.7 %collective-permute-start.74 = (bf16[256,6144]{1,0:T(8,128)(2,1)}, bf16[256,6144]{1,0:T(8,128)(2,1)}, u32[]{:S(2)}, u32[]{:S(2)}) collective-permute-start(bf16[256,6144]{1,0:T(8,128)(2,1)} %pad_maximum_fusion.refs_4_), channel_id=1, source_target_pairs={{0,4},{2,6},{4,0},{6,2},{8,12},{10,14},{12,8},{14,10},{16,20},{18,... | collective-permute-start | bytes 9437192 | tf_op jit(solution)/shard_map/ppermute | solution.py:346
  409.9 63.7 %collective-permute-done.29.r_ref = bf16[4,384,256]{2,1,0:T(8,128)(2,1)} collective-permute-done((bf16[4,384,256]{2,1,0:T(8,128)(2,1)S(1)}, bf16[4,384,256]{2,1,0:T(8,128)(2,1)}, u32[]{:S(2)}, u32[]{:S(2)}) %collective-permute-start.29) | collective-permute-done | bytes 786464 | tf_op jit(solution)/shard_map/ppermute | solution.py:346
  490.6 12.2 %collective-permute-start.32 = (bf16[576,256]{1,0:T(8,128)(2,1)S(1)}, bf16[576,256]{1,0:T(8,128)(2,1)S(1)}, u32[]{:S(2)}, u32[]{:S(2)}) collective-permute-start(bf16[576,256]{1,0:T(8,128)(2,1)S(1)} %get-tuple-element.99), channel_id=1, source_target_pairs={{0,8},{2,10},{4,12},{6,14},{8,16},{10,18},{12,20},{14,22},{16,24},... | collective-permute-start | bytes 884744 | tf_op jit(solution)/shard_map/ppermute | solution.py:346
  515.3 7.6 %collective-permute-done.33 = bf16[768,256]{1,0:T(8,128)(2,1)} collective-permute-done((bf16[768,256]{1,0:T(8,128)(2,1)}, bf16[768,256]{1,0:T(8,128)(2,1)}, u32[]{:S(2)}, u32[]{:S(2)}) %collective-permute-start.33) | collective-permute-done | bytes 393248 | tf_op jit(solution)/shard_map/ppermute | solution.py:343
  563.8 13.6 %weight_grads.5 = bf16[4,96,6144]{2,1,0:T(8,128)(2,1)} custom-call(bf16[2,4,96,256]{3,2,1,0:T(8,128)(2,1)} %get-tuple-element.91.refs_0_, bf16[2,4,96,256]{3,2,1,0:T(8,128)(2,1)} %get-tuple-element.105.refs_1_, bf16[2,4,96,256]{3,2,1,0:T(8,128)(2,1)} %get-tuple-element.106.refs_2_, bf16[2,4,96,256]{3,2,1,0:T(8,128)(2,1)} %get-tuple-element.104.refs_3_, ...), custom_call_target="tpu_custom_call" | custom-call | tf_op jit(solution)/shard_map/weight_grads/pallas_call | solution.py:297
  590.3 23.8 %collective-permute-done.41 = f32[145,128]{1,0:T(8,128)S(1)} collective-permute-done((f32[145,128]{1,0:T(8,128)S(1)}, f32[145,128]{1,0:T(8,128)S(1)}, u32[]{:S(2)}, u32[]{:S(2)}) %collective-permute-start.41) | collective-permute-done | bytes 74272 | tf_op jit(solution)/shard_map/ppermute | solution.py:346
  618.7 7.4 weight_grads.3
  640.8 6.3 collective-permute-start.55
  647.1 17.4 %collective-permute-done.77 = bf16[96,6144]{1,0:T(8,128)(2,1)S(1)} collective-permute-done((bf16[96,6144]{1,0:T(8,128)(2,1)S(1)}, bf16[96,6144]{1,0:T(8,128)(2,1)S(1)}, u32[]{:S(2)}, u32[]{:S(2)}) %collective-permute-start.77) | collective-permute-done | bytes 1179680 | tf_op jit(solution)/shard_map/ppermute | solution.py:603
  682.8 26.4 %collective-permute-start.78 = (bf16[96,6144]{1,0:T(8,128)(2,1)}, bf16[96,6144]{1,0:T(8,128)(2,1)S(1)}, u32[]{:S(2)}, u32[]{:S(2)}) collective-permute-start(bf16[96,6144]{1,0:T(8,128)(2,1)} %get-tuple-element.76), channel_id=1, source_target_pairs={{0,8},{2,10},{4,12},{6,14},{8,16},{10,18},{12,20},{14,22},{16,24},... | collective-permute-start | bytes 3538952 | tf_op jit(solution)/shard_map/ppermute | solution.py:603
  720.3 10.0 %collective-permute-done.78 = bf16[96,6144]{1,0:T(8,128)(2,1)S(1)} collective-permute-done((bf16[96,6144]{1,0:T(8,128)(2,1)}, bf16[96,6144]{1,0:T(8,128)(2,1)S(1)}, u32[]{:S(2)}, u32[]{:S(2)}) %collective-permute-start.78) | collective-permute-done | bytes 1179680 | tf_op jit(solution)/shard_map/ppermute | solution.py:603
  730.4 8.7 %collective-permute-done.81 = bf16[96,6144]{1,0:T(8,128)(2,1)} collective-permute-done((bf16[96,6144]{1,0:T(8,128)(2,1)}, bf16[96,6144]{1,0:T(8,128)(2,1)}, u32[]{:S(2)}, u32[]{:S(2)}) %collective-permute-start.81) | collective-permute-done | bytes 1179680 | tf_op jit(solution)/shard_map/ppermute | solution.py:607
  (572 shorter events, 371.7 us)
Async XLA Ops:
  7.2 707.5 %all-gather.2.cloned.1.call-start = ((), (), s32[]{:S(2)}) async-start(), calls=%async_computation | async-start | bytes 1671168 | tf_op jit(solution)/shard_map/all_gather | solution.py:647
  113.8 96.2 %collective-permute-start.17 = (bf16[1024,1536]{1,0:T(8,128)(2,1)}, bf16[1024,1536]{1,0:T(8,128)(2,1)}, u32[]{:S(2)}, u32[]{:S(2)}) collective-permute-start(bf16[1024,1536]{1,0:T(8,128)(2,1)} %constant_dynamic-slice_fusion.8), channel_id=1, source_target_pairs={{0,1},{1,0},{2,3},{3,2},{4,5},{5,4},{6,7},{7,6},{8,9},{9,8},{10,11... | collective-permute-start | bytes 9437192 | tf_op jit(solution)/shard_map/ppermute | solution.py:343
  119.8 73.7 %collective-permute-start.20 = (bf16[128,1536]{1,0:T(8,128)(2,1)}, bf16[128,1536]{1,0:T(8,128)(2,1)}, u32[]{:S(2)}, u32[]{:S(2)}) collective-permute-start(bf16[128,1536]{1,0:T(8,128)(2,1)} %param.19), channel_id=1, source_target_pairs={{0,1},{1,0},{2,3},{3,2},{4,5},{5,4},{6,7},{7,6},{8,9},{9,8},{10,11... | collective-permute-start | bytes 1179656 | tf_op jit(solution)/shard_map/ppermute | solution.py:343
  210.0 43.4 %collective-permute-start.18 = (bf16[1024,1536]{1,0:T(8,128)(2,1)}, bf16[1024,1536]{1,0:T(8,128)(2,1)}, u32[]{:S(2)}, u32[]{:S(2)}) collective-permute-start(bf16[1024,1536]{1,0:T(8,128)(2,1)} %collective-permute-done.17), channel_id=1, source_target_pairs={{0,2},{2,0},{4,6},{6,4},{8,10},{10,8},{12,14},{14,12},{16,18},{18,... | collective-permute-start | bytes 9437192 | tf_op jit(solution)/shard_map/ppermute | solution.py:346
  330.9 230.9 %collective-permute-start.73 = (bf16[256,6144]{1,0:T(8,128)(2,1)}, bf16[256,6144]{1,0:T(8,128)(2,1)}, u32[]{:S(2)}, u32[]{:S(2)}) collective-permute-start(bf16[256,6144]{1,0:T(8,128)(2,1)} %pad_maximum_fusion.refs_4_), channel_id=1, source_target_pairs={{0,2},{2,0},{4,6},{6,4},{8,10},{10,8},{12,14},{14,12},{16,18},{18,... | collective-permute-start | bytes 9437192 | tf_op jit(solution)/shard_map/ppermute | solution.py:346
  331.9 57.1 %collective-permute-start.62 = (bf16[256,768]{1,0:T(8,128)(2,1)}, bf16[256,768]{1,0:T(8,128)(2,1)S(1)}, u32[]{:S(2)}, u32[]{:S(2)}) collective-permute-start(bf16[256,768]{1,0:T(8,128)(2,1)} %multiply_convert_fusion.4.refs_4_), channel_id=1, source_target_pairs={{0,2},{2,0},{4,6},{6,4},{8,10},{10,8},{12,14},{14,12},{16,18},{18,... | collective-permute-start | bytes 1179656 | tf_op jit(solution)/shard_map/ppermute | solution.py:346
  332.6 56.6 %collective-permute-start.64 = (bf16[256,768]{1,0:T(8,128)(2,1)}, bf16[256,768]{1,0:T(8,128)(2,1)}, u32[]{:S(2)}, u32[]{:S(2)}) collective-permute-start(bf16[256,768]{1,0:T(8,128)(2,1)} %collective-permute-done.63.refs_6_), channel_id=1, source_target_pairs={{0,2},{2,0},{4,6},{6,4},{8,10},{10,8},{12,14},{14,12},{16,18},{18,... | collective-permute-start | bytes 1179656 | tf_op jit(solution)/shard_map/ppermute | solution.py:346
  338.1 40.9 %collective-permute-start.47 = (f32[204,128]{1,0:T(8,128)S(1)}, f32[204,128]{1,0:T(8,128)S(1)}, u32[]{:S(2)}, u32[]{:S(2)}) collective-permute-start(f32[204,128]{1,0:T(8,128)S(1)} %add.636), channel_id=1, source_target_pairs={{0,1},{1,0},{2,3},{3,2},{4,5},{5,4},{6,7},{7,6},{8,9},{9,8},{10,11... | collective-permute-start | bytes 313352 | tf_op jit(solution)/shard_map/ppermute | solution.py:343
  379.1 130.9 %collective-permute-start.74 = (bf16[256,6144]{1,0:T(8,128)(2,1)}, bf16[256,6144]{1,0:T(8,128)(2,1)}, u32[]{:S(2)}, u32[]{:S(2)}) collective-permute-start(bf16[256,6144]{1,0:T(8,128)(2,1)} %pad_maximum_fusion.refs_4_), channel_id=1, source_target_pairs={{0,4},{2,6},{4,0},{6,2},{8,12},{10,14},{12,8},{14,10},{16,20},{18,... | collective-permute-start | bytes 9437192 | tf_op jit(solution)/shard_map/ppermute | solution.py:346
  394.9 78.8 %collective-permute-start.29 = (bf16[4,384,256]{2,1,0:T(8,128)(2,1)S(1)}, bf16[4,384,256]{2,1,0:T(8,128)(2,1)}, u32[]{:S(2)}, u32[]{:S(2)}) collective-permute-start(bf16[4,384,256]{2,1,0:T(8,128)(2,1)S(1)} %add_convert_fusion), channel_id=1, source_target_pairs={{0,4},{2,6},{4,0},{6,2},{8,12},{10,14},{12,8},{14,10},{16,20},{18,... | collective-permute-start | bytes 2359304 | tf_op jit(solution)/shard_map/ppermute | solution.py:346
  400.7 81.5 %collective-permute-start.68 = (bf16[96,768]{1,0:T(8,128)(2,1)}, bf16[96,768]{1,0:T(8,128)(2,1)}, u32[]{:S(2)}, u32[]{:S(2)}) collective-permute-start(bf16[96,768]{1,0:T(8,128)(2,1)} %get-tuple-element.126), channel_id=1, source_target_pairs={{30,22},{28,20},{26,18},{24,16},{31,23},{29,21},{27,19},{25,17}} | collective-permute-start | bytes 442376 | tf_op jit(solution)/shard_map/ppermute | solution.py:607
  402.7 81.3 %collective-permute-start.66 = (bf16[96,768]{1,0:T(8,128)(2,1)}, bf16[96,768]{1,0:T(8,128)(2,1)}, u32[]{:S(2)}, u32[]{:S(2)}) collective-permute-start(bf16[96,768]{1,0:T(8,128)(2,1)} %fusion.41), channel_id=1, source_target_pairs={{0,8},{2,10},{4,12},{6,14},{8,16},{10,18},{12,20},{14,22},{1,9},{3... | collective-permute-start | bytes 442376 | tf_op jit(solution)/shard_map/ppermute | solution.py:603
  507.4 46.9 %collective-permute-start.69 = (bf16[96,768]{1,0:T(8,128)(2,1)}, bf16[96,768]{1,0:T(8,128)(2,1)}, u32[]{:S(2)}, u32[]{:S(2)}) collective-permute-start(bf16[96,768]{1,0:T(8,128)(2,1)} %get-tuple-element.124), channel_id=1, source_target_pairs={{30,22},{28,20},{26,18},{24,16},{22,14},{20,12},{18,10},{16,8},{31... | collective-permute-start | bytes 442376 | tf_op jit(solution)/shard_map/ppermute | solution.py:607
  509.9 53.3 %collective-permute-start.75 = (bf16[256,6144]{1,0:T(8,128)(2,1)}, bf16[256,6144]{1,0:T(8,128)(2,1)}, u32[]{:S(2)}, u32[]{:S(2)}) collective-permute-start(bf16[256,6144]{1,0:T(8,128)(2,1)} %collective-permute-done.74.refs_6_), channel_id=1, source_target_pairs={{0,2},{2,0},{4,6},{6,4},{8,10},{10,8},{12,14},{14,12},{16,18},{18,... | collective-permute-start | bytes 9437192 | tf_op jit(solution)/shard_map/ppermute | solution.py:346
  525.2 37.9 %collective-permute-start.52 = (bf16[2304,256]{1,0:T(8,128)(2,1)}, bf16[2304,256]{1,0:T(8,128)(2,1)}, u32[]{:S(2)}, u32[]{:S(2)}) collective-permute-start(bf16[2304,256]{1,0:T(8,128)(2,1)} %pad_maximum_fusion.1.refs_4_), channel_id=1, source_target_pairs={{0,4},{2,6},{4,0},{6,2},{8,12},{10,14},{12,8},{14,10},{16,20},{18,... | collective-permute-start | bytes 3538952 | tf_op jit(solution)/shard_map/ppermute | solution.py:346
  552.1 63.6 %collective-permute-start.35 = (f32[128,768]{1,0:T(8,128)}, f32[128,768]{1,0:T(8,128)}, u32[]{:S(2)}, u32[]{:S(2)}) collective-permute-start(f32[128,768]{1,0:T(8,128)} %get-tuple-element.118), channel_id=1, source_target_pairs={{0,1},{1,0},{2,3},{3,2},{4,5},{5,4},{6,7},{7,6},{8,9},{9,8},{10,11... | collective-permute-start | bytes 1179656 | tf_op jit(solution)/shard_map/ppermute | solution.py:343
  563.2 55.5 %collective-permute-start.51 = (bf16[2304,256]{1,0:T(8,128)(2,1)}, bf16[2304,256]{1,0:T(8,128)(2,1)}, u32[]{:S(2)}, u32[]{:S(2)}) collective-permute-start(bf16[2304,256]{1,0:T(8,128)(2,1)} %pad_maximum_fusion.1.refs_4_), channel_id=1, source_target_pairs={{0,2},{2,0},{4,6},{6,4},{8,10},{10,8},{12,14},{14,12},{16,18},{18,... | collective-permute-start | bytes 3538952 | tf_op jit(solution)/shard_map/ppermute | solution.py:346
  563.3 55.4 %collective-permute-start.53 = (bf16[2304,256]{1,0:T(8,128)(2,1)}, bf16[2304,256]{1,0:T(8,128)(2,1)}, u32[]{:S(2)}, u32[]{:S(2)}) collective-permute-start(bf16[2304,256]{1,0:T(8,128)(2,1)} %collective-permute-done.52.refs_6_), channel_id=1, source_target_pairs={{0,2},{2,0},{4,6},{6,4},{8,10},{10,8},{12,14},{14,12},{16,18},{18,... | collective-permute-start | bytes 3538952 | tf_op jit(solution)/shard_map/ppermute | solution.py:346
  583.5 46.3 %collective-permute-start.76 = (bf16[96,6144]{1,0:T(8,128)(2,1)}, bf16[96,6144]{1,0:T(8,128)(2,1)}, u32[]{:S(2)}, u32[]{:S(2)}) collective-permute-start(bf16[96,6144]{1,0:T(8,128)(2,1)} %get-tuple-element.78), channel_id=1, source_target_pairs={{0,8},{2,10},{4,12},{6,14},{1,9},{3,11},{5,13},{7,15}} | collective-permute-start | bytes 3538952 | tf_op jit(solution)/shard_map/ppermute | solution.py:603
  638.5 75.6 %collective-permute-start.48 = (f32[4,1024]{1,0:T(4,128)S(1)}, f32[4,1024]{1,0:T(4,128)S(1)}, u32[]{:S(2)}, u32[]{:S(2)}) collective-permute-start(f32[4,1024]{1,0:T(4,128)S(1)} %fusion.86), channel_id=1, source_target_pairs={{0,1},{1,0},{2,3},{3,2},{4,5},{5,4},{6,7},{7,6},{8,9},{9,8},{10,11... | collective-permute-start | bytes 49160 | tf_op jit(solution)/shard_map/ppermute | solution.py:343
  666.4 42.9 %collective-permute-start.80 = (bf16[96,6144]{1,0:T(8,128)(2,1)S(1)}, bf16[96,6144]{1,0:T(8,128)(2,1)S(1)}, u32[]{:S(2)}, u32[]{:S(2)}) collective-permute-start(bf16[96,6144]{1,0:T(8,128)(2,1)S(1)} %get-tuple-element.77), channel_id=1, source_target_pairs={{30,22},{28,20},{26,18},{24,16},{22,14},{20,12},{18,10},{16,8},{31... | collective-permute-start | bytes 3538952 | tf_op jit(solution)/shard_map/ppermute | solution.py:607
  674.9 43.1 %collective-permute-start.56 = (bf16[96,2304]{1,0:T(8,128)(2,1)}, bf16[96,2304]{1,0:T(8,128)(2,1)}, u32[]{:S(2)}, u32[]{:S(2)}) collective-permute-start(bf16[96,2304]{1,0:T(8,128)(2,1)} %get-tuple-element.86), channel_id=1, source_target_pairs={{0,8},{2,10},{4,12},{6,14},{8,16},{10,18},{12,20},{14,22},{16,24},... | collective-permute-start | bytes 1327112 | tf_op jit(solution)/shard_map/ppermute | solution.py:603
  681.5 36.5 %collective-permute-start.59 = (bf16[96,2304]{1,0:T(8,128)(2,1)}, bf16[96,2304]{1,0:T(8,128)(2,1)}, u32[]{:S(2)}, u32[]{:S(2)}) collective-permute-start(bf16[96,2304]{1,0:T(8,128)(2,1)} %fusion.19), channel_id=1, source_target_pairs={{30,22},{28,20},{26,18},{24,16},{22,14},{20,12},{18,10},{16,8},{14... | collective-permute-start | bytes 1327112 | tf_op jit(solution)/shard_map/ppermute | solution.py:607
  682.8 47.5 %collective-permute-start.78 = (bf16[96,6144]{1,0:T(8,128)(2,1)}, bf16[96,6144]{1,0:T(8,128)(2,1)S(1)}, u32[]{:S(2)}, u32[]{:S(2)}) collective-permute-start(bf16[96,6144]{1,0:T(8,128)(2,1)} %get-tuple-element.76), channel_id=1, source_target_pairs={{0,8},{2,10},{4,12},{6,14},{8,16},{10,18},{12,20},{14,22},{16,24},... | collective-permute-start | bytes 3538952 | tf_op jit(solution)/shard_map/ppermute | solution.py:603
  (156 other events, 2151.5 us)
Sparse Core Ops, SparseCore 0:
  552.2 39.8 all-gather.1

commit v2 on v0

--- a/solution.py
+++ b/solution.py
@@ -4,7 +4,9 @@
 import jax
 import jax.numpy as jnp
 from jax import lax
-from jax.sharding import PartitionSpec as P
+from jax.experimental import pallas as pl
+from jax.experimental.pallas import tpu as pltpu
+from jax.sharding import Mesh, PartitionSpec as P
 
 H = 24
 HD = 64
@@ -15,9 +17,1324 @@
 CAP = 128
 CLIPS = 4
 
-
 EPSILON = 1e-06
 MASKED = -1e30
+BF = jnp.bfloat16
+F32 = jnp.float32
+NN = (((1,), (0,)), ((), ()))
+NT = (((1,), (1,)), ((), ()))
+TN = (((0,), (0,)), ((), ()))
+GROUP = 4
+LINE = 4
+BUCKET = ("z", "y", "c")
+SMEM = pl.BlockSpec(memory_space=pltpu.SMEM)
+VMEM = pl.BlockSpec(memory_space=pltpu.VMEM)
+shape = jax.ShapeDtypeStruct
+
+
+def cost(microseconds):
+    return pl.CostEstimate(
+        flops=0, transcendentals=0, bytes_accessed=int(microseconds * 3_000_000)
+    )
+
+
+def mm(a, b, dims):
+    return lax.dot_general(a, b, dims, preferred_element_type=F32)
+
+
+def clip_at(slices, slot):
+    ends = [slices[0]]
+    for i in range(1, CLIPS):
+        ends.append(ends[-1] + slices[i])
+    clip = jnp.int32(0)
+    first, last = jnp.int32(0), ends[0]
+    for i in range(CLIPS - 1):
+        later = slot >= ends[i]
+        clip = jnp.where(later, i + 1, clip)
+        first = jnp.where(later, ends[i], first)
+        last = jnp.where(later, ends[i + 1], last)
+    return clip, first, last
+
+
+def slot_of(bucket, k, j):
+    return lax.rem(bucket // GROUP - k + LINE, LINE) * GROUP + jnp.bitwise_xor(
+        lax.rem(bucket, GROUP), j
+    )
+
+
+def chunk_at(bucket, k, width):
+    return pl.multiple_of(lax.rem(bucket // GROUP + k, LINE) * width, HD)
+
+
+def norm_rope(raw, gain, cosine, sine):
+    inverse = lax.rsqrt(jnp.mean(raw * raw, axis=0, keepdims=True) + EPSILON)
+    normed = raw * inverse * gain
+    half = raw.shape[0] // 2
+    first, second = normed[:half], normed[half:]
+    return jnp.concatenate(
+        [first * cosine - second * sine, first * sine + second * cosine], axis=0
+    )
+
+
+def norm_rope_back(grad, raw, gain, cosine, sine):
+    inverse = lax.rsqrt(jnp.mean(raw * raw, axis=0, keepdims=True) + EPSILON)
+    unit = raw * inverse
+    half = raw.shape[0] // 2
+    first, second = grad[:half], grad[half:]
+    turned = jnp.concatenate(
+        [first * cosine + second * sine, second * cosine - first * sine], axis=0
+    )
+    gain_grad = jnp.sum(turned * unit, axis=1, keepdims=True)
+    unit_grad = turned * gain
+    raw_grad = inverse * (unit_grad - unit * jnp.mean(unit_grad * unit, axis=0, keepdims=True))
+    return raw_grad, gain_grad
+
+
+def row_inverse(values):
+    return lax.rsqrt(jnp.mean(values * values, axis=-1, keepdims=True) + EPSILON)
+
+
+def pre_kernel(ids, slices, tok_a, tok_b, mod_a, mod_b, gain_ref, w_ref, p_ref, hid_ref, mod_ref):
+    @pl.when(pl.program_id(0) == 0)
+    def _():
+        s = ids[1]
+        clip, _, _ = clip_at(slices, ids[0])
+        row_a, row_b = mod_a[pl.ds(clip, 1), :], mod_b[pl.ds(clip, 1), :]
+        low, high = jnp.where(s == 0, row_a, row_b), jnp.where(s == 0, row_b, row_a)
+        mod_ref[...] = jnp.zeros_like(mod_ref)
+        for i in range(3):
+            mod_ref[i : i + 1, :] = low[:, i * D : (i + 1) * D]
+            mod_ref[3 + i : 4 + i, :] = high[:, i * D : (i + 1) * D]
+        shift, scale = mod_ref[0:1, :], mod_ref[1:2, :]
+        count = tok_a.shape[0]
+        for place, ref in ((s, tok_a), (1 - s, tok_b)):
+            values = ref[...].astype(F32)
+            hidden = values * row_inverse(values) * gain_ref[...] * (1.0 + scale) + shift
+            hid_ref[pl.ds(pl.multiple_of(place * count, count), count), :] = hidden.astype(BF)
+
+    p_ref[...] = mm(w_ref[...], hid_ref[...], NT).astype(BF)
+
+
+def pre(ids, slices, tok_a, tok_b, mod_a, mod_b, gain, w_qkv):
+    rows = 2 * tok_a.shape[0]
+    tile = w_qkv.shape[0] // 3
+    full = lambda v: pl.BlockSpec(v.shape, lambda i: (0,) * v.ndim)
+    return pl.pallas_call(
+        pre_kernel,
+        grid=(w_qkv.shape[0] // tile,),
+        in_specs=[SMEM, SMEM]
+        + [full(v) for v in (tok_a, tok_b, mod_a, mod_b, gain)]
+        + [pl.BlockSpec((tile, D), lambda i: (i, 0))],
+        out_specs=[
+            pl.BlockSpec((tile, rows), lambda i: (i, 0)),
+            pl.BlockSpec((rows, D), lambda i: (0, 0)),
+            pl.BlockSpec((8, D), lambda i: (0, 0)),
+        ],
+        out_shape=[shape((w_qkv.shape[0], rows), BF), shape((rows, D), BF), shape((8, D), F32)],
+        name="pre",
+        cost_estimate=cost(6),
+    )(ids, slices, tok_a, tok_b, mod_a, mod_b, gain, w_qkv)
+
+
+def route_kernel(ids, p_ref, r_ref, *outs):
+    b, s = ids[0], ids[1]
+    local = r_ref.shape[0]
+    width = local // LINE
+    for k in range(LINE):
+        at = chunk_at(b, k, width)
+        kv_ref, q_ref = outs[k], outs[LINE + k]
+
+        @pl.when(s == 0)
+        def _():
+            q_ref[...] = p_ref[pl.ds(at, width), :]
+            kv_ref[:width, :] = p_ref[pl.ds(2 * local + at, width), :]
+            kv_ref[width:, :] = r_ref[pl.ds(at, width), :]
+
+        @pl.when(s == 1)
+        def _():
+            q_ref[...] = r_ref[pl.ds(at, width), :]
+            kv_ref[:width, :] = p_ref[pl.ds(at, width), :]
+            kv_ref[width:, :] = p_ref[pl.ds(2 * local + at, width), :]
+
+
+def route(ids, projected, received):
+    local, rows = received.shape
+    width = local // LINE
+    outs = pl.pallas_call(
+        route_kernel,
+        in_specs=[SMEM, VMEM, VMEM],
+        out_specs=[VMEM] * (2 * LINE),
+        out_shape=[shape((2 * width, rows), BF)] * LINE + [shape((width, rows), BF)] * LINE,
+        name="route",
+        cost_estimate=cost(2.5),
+    )(ids, projected, received)
+    return outs[:LINE], outs[LINE:]
+
+
+def caption_kernel(ids, w_ref, cap_ref, gains_ref, raw_ref, kv_ref):
+    step = pl.program_id(0)
+    width = w_ref.shape[1]
+
+    @pl.when(step == 0)
+    def _():
+        raw_ref[...] = jnp.zeros_like(raw_ref)
+
+    for j in range(2):
+        raw_ref[j * width : (j + 1) * width, :] += mm(w_ref[j], cap_ref[...], NT)
+
+    @pl.when(step == pl.num_programs(0) - 1)
+    def _():
+        base = ids[1] * LINE * width + ids[0] // GROUP * width
+        for h in range(width // HD):
+            at = slice(h * HD, h * HD + HD)
+            raw = raw_ref[at, :]
+            inverse = lax.rsqrt(jnp.mean(raw * raw, axis=0, keepdims=True) + EPSILON)
+            gain = gains_ref[pl.ds(pl.multiple_of(base + h * HD, HD), HD), 2:3]
+            keys = (raw * inverse * gain).astype(BF)
+            for c in range(CLIPS):
+                kv_ref[c, at, :] = keys[:, c * CAP : (c + 1) * CAP]
+        for c in range(CLIPS):
+            kv_ref[c, width:, :] = raw_ref[width:, c * CAP : (c + 1) * CAP].astype(BF)
+
+
+def caption_keys(ids, w_caption, caption, gains):
+    width = w_caption.shape[1] // LINE
+    tile = 1024
+    count = caption.shape[0]
+    return pl.pallas_call(
+        caption_kernel,
+        grid_spec=pltpu.PrefetchScalarGridSpec(
+            num_scalar_prefetch=1,
+            grid=(YD // tile,),
+            in_specs=[
+                pl.BlockSpec((2, width, tile), lambda i, ids: (0, ids[0] // GROUP, i)),
+                pl.BlockSpec((count, tile), lambda i, ids: (0, i)),
+                pl.BlockSpec(gains.shape, lambda i, ids: (0, 0)),
+            ],
+            out_specs=[
+                pl.BlockSpec((2 * width, count), lambda i, ids: (0, 0)),
+                pl.BlockSpec((CLIPS, 2 * width, CAP), lambda i, ids: (0, 0, 0)),
+            ],
+        ),
+        out_shape=[shape((2 * width, count), F32), shape((CLIPS, 2 * width, CAP), BF)],
+        name="caption_keys",
+        cost_estimate=cost(8),
+    )(ids, w_caption, caption, gains)
+
+
+def attend_kernel(ids, slices, lengths, gates, *refs):
+    q_refs = refs[:LINE]
+    kv_refs = refs[LINE : LINE + GROUP]
+    cap_ref, gains_ref, cos_ref, sin_ref = refs[LINE + GROUP : LINE + GROUP + 4]
+    outs = refs[LINE + GROUP + 4 :]
+    comb_refs = outs[:LINE]
+    own_ref, other_ref, stat_ref, qs_ref, ks_ref, vs_ref = outs[LINE:]
+    b, s = ids[0], ids[1]
+    width, rows = q_refs[0].shape
+    heads = width // HD
+    scale = HD**-0.5
+    base = s * LINE * width + b // GROUP * width
+
+    def gain_of(h, column):
+        return gains_ref[pl.ds(pl.multiple_of(base + h * HD, HD), HD), column : column + 1]
+
+    key_gains = [gain_of(h, 1) for h in range(heads)]
+    query_gains = [gain_of(h, 0) for h in range(heads)]
+    for j, kv_ref in enumerate(kv_refs):
+        for k in range(LINE):
+            slot = slot_of(b, k, j)
+            _, start, _ = clip_at(slices, slot)
+            cosine, sine = cos_ref[slot - start], sin_ref[slot - start]
+            for h in range(heads):
+                at = slice(h * HD, h * HD + HD)
+                raw = kv_ref[k, at, :].astype(F32)
+                ks_ref[slot, at, :] = norm_rope(raw, key_gains[h], cosine, sine).astype(BF)
+            vs_ref[slot] = kv_ref[k, width:, :]
+
+    for i in range(LINE):
+        slot = slot_of(b, i, 0)
+        clip, first, last = clip_at(slices, slot)
+        cosine, sine = cos_ref[slot - first], sin_ref[slot - first]
+        queries = []
+        for h in range(heads):
+            at = slice(h * HD, h * HD + HD)
+            raw = q_refs[i][at, :].astype(F32)
+            turned = norm_rope(raw, query_gains[h], cosine, sine).astype(BF)
+            turned = (turned.astype(F32) * scale).astype(BF)
+            qs_ref[i, at, :] = turned
+            queries.append(turned)
+
+        def step(n, state):
+            totals, sums = state
+            new_totals, new_sums = [], []
+            for h in range(heads):
+                at = slice(h * HD, h * HD + HD)
+                weights = jnp.exp(mm(ks_ref[n, at, :], queries[h], TN))
+                new_totals.append(totals[h] + jnp.sum(weights, axis=0, keepdims=True))
+                new_sums.append(sums[h] + mm(vs_ref[n, at, :], weights.astype(BF), NN))
+            return tuple(new_totals), tuple(new_sums)
+
+        zero_total = tuple(jnp.zeros((1, rows), F32) for _ in range(heads))
+        zero_sum = tuple(jnp.zeros((HD, rows), F32) for _ in range(heads))
+        totals, sums = lax.fori_loop(first, last, step, (zero_total, zero_sum))
+        usable = lax.broadcasted_iota(jnp.int32, (CAP, rows), 0) < lengths[clip]
+        for h in range(heads):
+            at = slice(h * HD, h * HD + HD)
+            inverse = 1.0 / totals[h]
+            own = sums[h] * inverse
+            weights = jnp.where(usable, jnp.exp(mm(cap_ref[clip, at, :], queries[h], TN)), 0.0)
+            cap_inverse = 1.0 / jnp.sum(weights, axis=0, keepdims=True)
+            at_value = slice(width + h * HD, width + h * HD + HD)
+            other = mm(cap_ref[clip, at_value, :], weights.astype(BF), NN) * cap_inverse
+            own_ref[i, at, :] = own
+            other_ref[i, at, :] = other
+            gate = gates[(s * LINE + b // GROUP) * heads + h]
+            comb_refs[i][at, :] = (own + gate * other).astype(BF)
+            stat_ref[i, h : h + 1, :] = inverse
+            stat_ref[i, 4 + h : 5 + h, :] = cap_inverse
+
+
+def attend(ids, slices, lengths, gates, queries, kv_pieces, cap_kv, gains, cosine, sine):
+    width, rows = queries[0].shape
+    slots = LINE * GROUP
+    outs = pl.pallas_call(
+        attend_kernel,
+        in_specs=[SMEM] * 4 + [VMEM] * (LINE + GROUP + 4),
+        out_specs=[VMEM] * (LINE + 6),
+        out_shape=[shape((width, rows), BF)] * LINE
+        + [
+            shape((LINE, width, rows), F32),
+            shape((LINE, width, rows), F32),
+            shape((LINE, 8, rows), F32),
+            shape((LINE, width, rows), BF),
+            shape((slots, width, rows), BF),
+            shape((slots, width, rows), BF),
+        ],
+        name="attend",
+        cost_estimate=cost(33),
+    )(ids, slices, lengths, gates, *queries, *kv_pieces, cap_kv, gains, cosine, sine)
+    return outs[:LINE], outs[LINE:]
+
+
+def out_kernel(ids, *refs):
+    own, other = refs[:LINE], refs[LINE : 2 * LINE]
+    w_ref, att_ref, branch_ref = refs[2 * LINE :]
+    b, s = ids[0], ids[1]
+    width = own[0].shape[0]
+    for k in range(LINE):
+        at = chunk_at(b, k, width)
+        att_ref[pl.ds(pl.multiple_of(s * LINE * width + at, HD), width), :] = own[k][...]
+        att_ref[pl.ds(pl.multiple_of((1 - s) * LINE * width + at, HD), width), :] = other[k][...]
+    branch_ref[...] = mm(w_ref[...], att_ref[...], NN).T.astype(BF)
+
+
+def out_proj(ids, own, other, w_out):
+    rows = own[0].shape[1]
+    return pl.pallas_call(
+        out_kernel,
+        in_specs=[SMEM] + [VMEM] * (2 * LINE + 1),
+        out_specs=[VMEM, VMEM],
+        out_shape=[shape((D, rows), BF), shape((rows, w_out.shape[0]), BF)],
+        name="out_proj",
+        cost_estimate=cost(3.5),
+    )(ids, *own, *other, w_out)
+
+
+def cut_kernel(turned, ids, *refs):
+    count = len(turned)
+    ins = refs[:count]
+    own_ref, c_ref, y_ref, scratch = refs[count:]
+    place = lax.rem(ids[0], GROUP)
+    columns = own_ref.shape[3]
+    for n in range(count):
+        if turned[n]:
+            source = ins[n]
+        else:
+            scratch[...] = ins[n][...].astype(F32).T
+            source = scratch
+        for k in range(LINE):
+            for j, (ref, i) in enumerate(((own_ref, 0), (c_ref, 0), (y_ref, 0), (y_ref, 1))):
+                at = (k * GROUP + jnp.bitwise_xor(place, j)) * columns
+                ref[i, n, k] = source[pl.ds(pl.multiple_of(at, 32), columns), :].astype(BF)
+
+
+def cut(ids, values, turned):
+    rows = values[0].shape[1 if turned[0] else 0]
+    columns = D // (LINE * GROUP)
+    count = len(values)
+    return pl.pallas_call(
+        functools.partial(cut_kernel, tuple(turned)),
+        in_specs=[SMEM] + [VMEM] * count,
+        out_specs=[VMEM] * 3,
+        out_shape=[shape((n, count, LINE, columns, rows), BF) for n in (1, 1, 2)],
+        scratch_shapes=[pltpu.VMEM((D, rows), F32)],
+        name="cut",
+        cost_estimate=cost(2.4),
+    )(ids, *values)
+
+
+def ffn_kernel(
+    ids,
+    tok_a,
+    tok_b,
+    br_a,
+    br_b,
+    out16_ref,
+    mod_ref,
+    gain_ref,
+    kept_ref,
+    came_ref,
+    down_ref,
+    inner_ref,
+    gkept_ref,
+    gcame_ref,
+    in16_ref,
+    mid_ref,
+    near_ref,
+    far_ref,
+    mean_ref,
+    near_out_ref,
+    far_out_ref,
+    acc_in,
+    acc_out,
+):
+    step = pl.program_id(0)
+    steps = pl.num_programs(0)
+    s = ids[1]
+    count = tok_a.shape[0]
+    half = br_a.shape[1]
+    gate, shift2, scale2 = [mod_ref[i : i + 1, :] for i in (2, 3, 4)]
+    mlp_gain = gain_ref[...] * (1.0 + scale2)
+
+    @pl.when(step == 0)
+    def _():
+        for place, tok in ((s, tok_a), (1 - s, tok_b)):
+            at = pl.ds(pl.multiple_of(place * count, count), count)
+            mid_ref[at, :] = tok[...].astype(F32)
+        low = jnp.where(s == 0, br_a[...].astype(F32), br_b[...].astype(F32))
+        high = jnp.where(s == 0, br_b[...].astype(F32), br_a[...].astype(F32))
+        mid_ref[:, :half] += gate[:, :half] * low
+        mid_ref[:, half:] += gate[:, half:] * high
+        middle = mid_ref[...]
+        in16_ref[...] = (middle * row_inverse(middle) * mlp_gain + shift2).astype(BF)
+        acc_in[...] = jnp.zeros_like(acc_in)
+        acc_out[...] = jnp.zeros_like(acc_out)
+
+    w_kept, w_came, w_down = kept_ref[...], came_ref[...], down_ref[...]
+    kept = mm(in16_ref[...], w_kept, NT)
+    other = mm(in16_ref[...], w_came, NT)
+    grad_inner = mm(out16_ref[...], w_down, NT)
+    gate_half = jnp.where(s == 0, kept, other)
+    up_half = jnp.where(s == 0, other, kept)
+    sigmoid = jax.nn.sigmoid(gate_half)
+    silu = gate_half * sigmoid
+    inner = (silu * up_half).astype(BF)
+    grad_gate = grad_inner * up_half * sigmoid * (1.0 + gate_half * (1.0 - sigmoid))
+    grad_up = grad_inner * silu
+    grad_kept = jnp.where(s == 0, grad_gate, grad_up).astype(BF)
+    grad_came = jnp.where(s == 0, grad_up, grad_gate).astype(BF)
+    inner_ref[...] = inner
+    gkept_ref[...] = grad_kept
+    gcame_ref[...] = grad_came
+    acc_in[...] += mm(grad_kept, w_kept, NN) + mm(grad_came, w_came, NN)
+    acc_out[...] += mm(inner, w_down, NN)
+
+    @pl.when(step == steps - 1)
+    def _():
+        middle = mid_ref[...]
+        part = jnp.sum(
+            acc_in[...] * mlp_gain * (middle * row_inverse(middle)), axis=-1, keepdims=True
+        )
+        mean_ref[...] = jnp.broadcast_to(part, (part.shape[0], 128)).T[:8]
+        near_ref[...] = acc_in[:, pl.ds(pl.multiple_of(s * half, half), half)]
+        far_ref[...] = acc_in[:, pl.ds(pl.multiple_of((1 - s) * half, half), half)].astype(BF)
+        near_out_ref[...] = acc_out[pl.ds(pl.multiple_of(s * count, count), count), :]
+        far_out_ref[...] = acc_out[pl.ds(pl.multiple_of((1 - s) * count, count), count), :].astype(BF)
+
+
+def ffn(ids, toks, branches, grad_mlp, mod, gain, w_gate_up, came, w_down):
+    count = toks[0].shape[0]
+    rows = 2 * count
+    half = D // 2
+    units = w_down.shape[0]
+    tile = 512
+    steps = units // tile
+    full = lambda v: pl.BlockSpec(v.shape, lambda i, ids: (0,) * v.ndim)
+
+    def fixed(r, c):
+        return pl.BlockSpec((r, c), lambda i, ids: (0, 0))
+
+    small = [*toks, *branches, grad_mlp, mod, gain]
+    return pl.pallas_call(
+        ffn_kernel,
+        grid_spec=pltpu.PrefetchScalarGridSpec(
+            num_scalar_prefetch=1,
+            grid=(steps,),
+            in_specs=[full(v) for v in small]
+            + [
+                pl.BlockSpec((tile, D), lambda i, ids: (ids[1] * steps + i, 0)),
+                pl.BlockSpec((tile, D), lambda i, ids: ((1 - ids[1]) * steps + i, 0)),
+                pl.BlockSpec((tile, D), lambda i, ids: (i, 0)),
+            ],
+            out_specs=[pl.BlockSpec((rows, tile), lambda i, ids: (0, i))] * 3
+            + [
+                fixed(rows, D),
+                fixed(rows, D),
+                fixed(rows, half),
+                fixed(rows, half),
+                fixed(8, rows),
+                fixed(count, D),
+                fixed(count, D),
+            ],
+            scratch_shapes=[pltpu.VMEM((rows, D), F32), pltpu.VMEM((rows, D), F32)],
+        ),
+        out_shape=[shape((rows, units), BF)] * 3
+        + [
+            shape((rows, D), BF),
+            shape((rows, D), F32),
+            shape((rows, half), F32),
+            shape((rows, half), BF),
+            shape((8, rows), F32),
+            shape((count, D), F32),
+            shape((count, D), BF),
+        ],
+        name="ffn",
+        cost_estimate=cost(18),
+    )(ids, *small, w_gate_up, came, w_down)
+
+
+def mid_kernel(
+    ids,
+    near_ref,
+    recv_ref,
+    mean_a,
+    mean_b,
+    mid_ref,
+    cot_a,
+    cot_b,
+    br_ref,
+    mod_ref,
+    gain_ref,
+    w_ref,
+    sums_ref,
+    gbr_ref,
+    near_mid_ref,
+    far_mid_ref,
+    *refs,
+):
+    near_refs, far_refs, scratch = refs[:LINE], refs[LINE : 2 * LINE], refs[2 * LINE]
+    b, s = ids[0], ids[1]
+    half = near_ref.shape[1]
+    count = cot_a.shape[0]
+    cols = pl.ds(pl.multiple_of(s * half, half), half)
+    gate, scale2 = mod_ref[2:3, cols], mod_ref[4:5, cols]
+    gain = gain_ref[:, cols]
+    middle = mid_ref[...]
+    inverse = row_inverse(middle)
+    unit = mid_ref[:, cols] * inverse
+    means = (mean_a[...] + mean_b[...]) * (1.0 / D)
+    mean = jnp.concatenate([means] * 16, axis=0).T[:, 0:1]
+    grad_in = near_ref[...] + recv_ref[...].astype(F32)
+    cot_own, cot_far = cot_a[:, cols].astype(F32), cot_b[:, cols].astype(F32)
+    cot = jnp.concatenate(
+        [jnp.where(s == 0, cot_own, cot_far), jnp.where(s == 0, cot_far, cot_own)], axis=0
+    )
+    scaled = grad_in * (1.0 + scale2)
+    grad_mid = cot + inverse * (scaled * gain - unit * mean)
+    sums_ref[...] = jnp.zeros_like(sums_ref)
+    sums_ref[0:1, :] = jnp.sum(grad_mid * br_ref[...].astype(F32), axis=0, keepdims=True)
+    sums_ref[1:2, :] = jnp.sum(grad_in, axis=0, keepdims=True)
+    sums_ref[2:3, :] = jnp.sum(grad_in * unit, axis=0, keepdims=True) * gain
+    sums_ref[3:4, :] = jnp.sum(scaled * unit, axis=0, keepdims=True)
+    grad_branch = (grad_mid * gate).astype(BF)
+    gbr_ref[...] = grad_branch
+    top, low = grad_mid[:count], grad_mid[count:]
+    near_mid_ref[...] = jnp.where(s == 0, top, low)
+    far_mid_ref[...] = jnp.where(s == 0, low, top).astype(BF)
+    scratch[...] = mm(grad_branch, w_ref[...], NN).T
+    width = near_refs[0].shape[0]
+    for k in range(LINE):
+        at = chunk_at(b, k, width)
+        near_refs[k][...] = scratch[pl.ds(pl.multiple_of(s * half + at, HD), width), :]
+        far_refs[k][...] = scratch[pl.ds(pl.multiple_of((1 - s) * half + at, HD), width), :].astype(BF)
+
+
+def mid_back(ids, near, received, mean_a, mean_b, middle, cots, branch, mod, gain, w_out):
+    rows, half = near.shape
+    width = half // LINE
+    count = cots[0].shape[0]
+    outs = pl.pallas_call(
+        mid_kernel,
+        in_specs=[SMEM] + [VMEM] * 11,
+        out_specs=[VMEM] * (4 + 2 * LINE),
+        out_shape=[
+            shape((8, half), F32),
+            shape((rows, half), BF),
+            shape((count, half), F32),
+            shape((count, half), BF),
+        ]
+        + [shape((width, rows), F32)] * LINE
+        + [shape((width, rows), BF)] * LINE,
+        scratch_shapes=[pltpu.VMEM((D, rows), F32)],
+        name="mid_back",
+        cost_estimate=cost(5.5),
+    )(ids, near, received, mean_a, mean_b, middle, *cots, branch, mod, gain, w_out)
+    return outs[:4], outs[4 : 4 + LINE], outs[4 + LINE :]
+
+
+def place_row(b, column):
+    width = column.shape[0]
+    row = jnp.broadcast_to(column, (width, 128)).T[0:1]
+    z = b // GROUP
+    return jnp.concatenate([jnp.where(z == k, row, 0.0) for k in range(LINE)], axis=1)
+
+
+def output_kernel(ids, slices, near_ref, recv_ref, mid_ref, cot_ref, mod_ref, sums_ref, out_ref, early_ref):
+    s = ids[1]
+    count, half = near_ref.shape[0], sums_ref.shape[1]
+    clip, _, _ = clip_at(slices, ids[0])
+    branch = near_ref[...] + recv_ref[...].astype(F32)
+    middle = mid_ref[pl.ds(pl.multiple_of(s * count, count), count), :]
+    out_ref[...] = (middle + mod_ref[5:6, :] * branch).astype(BF)
+    gate2 = jnp.sum(cot_ref[...].astype(F32) * branch, axis=0, keepdims=True)
+    rows = [sums_ref[i : i + 1, :] for i in range(3)] + [gate2[:, :half], gate2[:, half:]]
+    early_ref[...] = jnp.zeros_like(early_ref)
+    for c in range(CLIPS):
+        for i, row in enumerate(rows):
+            early_ref[5 * c + i : 5 * c + i + 1, :] = jnp.where(clip == c, row, 0.0)
+    early_ref[20:21, :] = sums_ref[3:4, :]
+
+
+def output_sums(ids, slices, near, received, middle, cot, mod, sums):
+    count = near.shape[0]
+    return pl.pallas_call(
+        output_kernel,
+        in_specs=[SMEM, SMEM] + [VMEM] * 6,
+        out_specs=[VMEM, VMEM],
+        out_shape=[shape((count, D), BF), shape((24, D // 2), F32)],
+        name="output_sums",
+        cost_estimate=cost(3),
+    )(ids, slices, near, received, middle, cot, mod, sums)
+
+
+def attend_back_kernel(ids, slices, lengths, gates, *refs):
+    q_refs, g_refs = refs[:LINE], refs[LINE : 2 * LINE]
+    (own_ref, other_ref, stat_ref, qs_ref, ks_ref, vs_ref, cap_ref, gains_ref, cos_ref, sin_ref) = refs[
+        2 * LINE : 2 * LINE + 10
+    ]
+    outs = refs[2 * LINE + 10 :]
+    gq_refs = outs[:LINE]
+    qgain_ref, keep_ref, send_ref, dgate_ref = outs[LINE : LINE + 4]
+    dkv_refs = outs[LINE + 4 : LINE + 4 + GROUP]
+    acc_ref, dcap_ref = outs[LINE + 4 + GROUP :]
+    b, s = ids[0], ids[1]
+    width, rows = q_refs[0].shape
+    heads = width // HD
+    scale = HD**-0.5
+    base = s * LINE * width + b // GROUP * width
+    acc_ref[...] = jnp.zeros_like(acc_ref)
+    dcap_ref[...] = jnp.zeros_like(dcap_ref)
+    dgate_ref[...] = jnp.zeros_like(dgate_ref)
+    qgain_ref[...] = jnp.zeros_like(qgain_ref)
+
+    for i in range(LINE):
+        slot = slot_of(b, i, 0)
+        clip, first, last = clip_at(slices, slot)
+        queries, grads, deltas, inverses = [], [], [], []
+        for h in range(heads):
+            at = slice(h * HD, h * HD + HD)
+            grad = g_refs[i][at, :]
+            queries.append(qs_ref[i, at, :])
+            grads.append(grad)
+            deltas.append(jnp.sum(grad.astype(F32) * own_ref[i, at, :], axis=0, keepdims=True))
+            inverses.append(stat_ref[i, h : h + 1, :])
+
+        def step(n, state):
+            out = []
+            for h in range(heads):
+                at = slice(h * HD, h * HD + HD)
+                at_value = slice(width + h * HD, width + h * HD + HD)
+                keys, values = ks_ref[n, at, :], vs_ref[n, at, :]
+                prob = jnp.exp(mm(keys, queries[h], TN)) * inverses[h]
+                grad_prob = mm(values, grads[h], TN)
+                grad_score = (prob * (grad_prob - deltas[h])).astype(BF)
+                acc_ref[n, at_value, :] += mm(grads[h], prob.astype(BF), NT)
+                acc_ref[n, at, :] += mm(queries[h], grad_score, NT)
+                out.append(state[h] + mm(keys, grad_score, NN))
+            return tuple(out)
+
+        query_grads = lax.fori_loop(
+            first, last, step, tuple(jnp.zeros((HD, rows), F32) for _ in range(heads))
+        )
+        usable = lax.broadcasted_iota(jnp.int32, (CAP, rows), 0) < lengths[clip]
+        cosine, sine = cos_ref[slot - first], sin_ref[slot - first]
+        for h in range(heads):
+            at = slice(h * HD, h * HD + HD)
+            at_value = slice(width + h * HD, width + h * HD + HD)
+            gate = gates[(s * LINE + b // GROUP) * heads + h]
+            cap_keys, cap_values = cap_ref[clip, at, :], cap_ref[clip, at_value, :]
+            grad = grads[h].astype(F32)
+            grad_other = (grad * gate).astype(BF)
+            prob = (
+                jnp.where(usable, jnp.exp(mm(cap_keys, queries[h], TN)), 0.0)
+                * stat_ref[i, 4 + h : 5 + h, :]
+            )
+            grad_prob = mm(cap_values, grad_other, TN)
+            inner = jnp.sum(prob * grad_prob, axis=0, keepdims=True)
+            grad_score = (prob * (grad_prob - inner)).astype(BF)
+            query_grad = (query_grads[h] + mm(cap_keys, grad_score, NN)) * scale
+            dcap_ref[clip, at, :] += mm(queries[h], grad_score, NT)
+            dcap_ref[clip, at_value, :] += mm(grad_other, prob.astype(BF), NT)
+            part = jnp.sum(grad * other_ref[i, at, :], axis=0, keepdims=True)
+            dgate_ref[h : h + 1, :] += part * (1.0 - gate * gate)
+            gain = gains_ref[pl.ds(pl.multiple_of(base + h * HD, HD), HD), 0:1]
+            raw_grad, gain_grad = norm_rope_back(
+                query_grad.astype(BF).astype(F32), q_refs[i][at, :].astype(F32), gain, cosine, sine
+            )
+            gq_refs[i][at, :] = raw_grad.astype(BF)
+            qgain_ref[at, :] += gain_grad
+
+    for j, dkv_ref in enumerate(dkv_refs):
+        for k in range(LINE):
+            dkv_ref[k] = acc_ref[slot_of(b, k, j)].astype(BF)
+    core = lax.rem(b, 2)
+    for i in range(2):
+        keep_ref[i] = dcap_ref[2 * i + core]
+        send_ref[i] = dcap_ref[2 * i + 1 - core]
+
+
+def attend_back(ids, slices, lengths, gates, queries, grads, saved, cap_kv, gains, cosine, sine):
+    width, rows = queries[0].shape
+    outs = pl.pallas_call(
+        attend_back_kernel,
+        in_specs=[SMEM] * 4 + [VMEM] * (2 * LINE + 10),
+        out_specs=[VMEM] * (LINE + 4 + GROUP),
+        out_shape=[shape((width, rows), BF)] * LINE
+        + [
+            shape((width, 1), F32),
+            shape((2, 2 * width, CAP), F32),
+            shape((2, 2 * width, CAP), F32),
+            shape((8, rows), F32),
+        ]
+        + [shape((LINE, 2 * width, rows), BF)] * GROUP,
+        scratch_shapes=[
+            pltpu.VMEM((LINE * GROUP, 2 * width, rows), F32),
+            pltpu.VMEM((CLIPS, 2 * width, CAP), F32),
+        ],
+        name="attend_back",
+        cost_estimate=cost(40),
+    )(ids, slices, lengths, gates, *queries, *grads, *saved, cap_kv, gains, cosine, sine)
+    return outs[:LINE], outs[LINE : LINE + 4], outs[LINE + 4 :]
+
+
+def keys_back_kernel(ids, slices, a_ref, r_ref, kv_ref, gains_ref, cos_ref, sin_ref, *outs):
+    out_refs, gain_ref = outs[:LINE], outs[LINE]
+    b, s = ids[0], ids[1]
+    width = gain_ref.shape[0]
+    base = s * LINE * width + b // GROUP * width
+    gain_ref[...] = jnp.zeros_like(gain_ref)
+    for i in range(LINE):
+        slot = slot_of(b, i, 0)
+        _, first, _ = clip_at(slices, slot)
+        cosine, sine = cos_ref[slot - first], sin_ref[slot - first]
+        total = (a_ref[i].astype(F32) + r_ref[i].astype(F32)).astype(BF)
+        for h in range(width // HD):
+            at = slice(h * HD, h * HD + HD)
+            gain = gains_ref[pl.ds(pl.multiple_of(base + h * HD, HD), HD), 1:2]
+            raw_grad, gain_grad = norm_rope_back(
+                total[at, :].astype(F32), kv_ref[i, at, :].astype(F32), gain, cosine, sine
+            )
+            out_refs[i][at, :] = raw_grad.astype(BF)
+            gain_ref[at, :] += gain_grad
+        out_refs[i][width:, :] = total[width:, :]
+
+
+def keys_back(ids, slices, part, received, kv, gains, cosine, sine):
+    _, both, rows = kv.shape
+    outs = pl.pallas_call(
+        keys_back_kernel,
+        in_specs=[SMEM, SMEM] + [VMEM] * 6,
+        out_specs=[VMEM] * (LINE + 1),
+        out_shape=[shape((both, rows), BF)] * LINE + [shape((both // 2, 1), F32)],
+        name="keys_back",
+        cost_estimate=cost(3.7),
+    )(ids, slices, part, received, kv, gains, cosine, sine)
+    return outs[:LINE], outs[LINE]
+
+
+def pack_kernel(ids, *refs):
+    q_refs, kv_refs = refs[:LINE], refs[LINE : 2 * LINE]
+    own_ref, send_ref = refs[2 * LINE :]
+    b, s = ids[0], ids[1]
+    width = q_refs[0].shape[0]
+    local = LINE * width
+    for k in range(LINE):
+        at = chunk_at(b, k, width)
+
+        @pl.when(s == 0)
+        def _():
+            own_ref[pl.ds(at, width), :] = q_refs[k][...]
+            own_ref[pl.ds(local + at, width), :] = kv_refs[k][:width, :]
+            send_ref[pl.ds(at, width), :] = kv_refs[k][width:, :]
+
+        @pl.when(s == 1)
+        def _():
+            own_ref[pl.ds(at, width), :] = kv_refs[k][:width, :]
+            own_ref[pl.ds(local + at, width), :] = kv_refs[k][width:, :]
+            send_ref[pl.ds(at, width), :] = q_refs[k][...]
+
+
+def pack(ids, grads_q, grads_kv):
+    width, rows = grads_q[0].shape
+    return pl.pallas_call(
+        pack_kernel,
+        in_specs=[SMEM] + [VMEM] * (2 * LINE),
+        out_specs=[VMEM, VMEM],
+        out_shape=[shape((2 * LINE * width, rows), BF), shape((LINE * width, rows), BF)],
+        name="pack",
+        cost_estimate=cost(2.5),
+    )(ids, *grads_q, *grads_kv)
+
+
+def qkv_back_kernel(ids, own_ref, recv_ref, w_ref, near_ref, far_ref, acc_ref):
+    step = pl.program_id(0)
+    third = pl.num_programs(0) // 3
+    count = near_ref.shape[0]
+    s = ids[1]
+
+    @pl.when(step == 0)
+    def _():
+        acc_ref[...] = jnp.zeros_like(acc_ref)
+
+    middle = jnp.logical_and(step >= third, step < 2 * third)
+    grads = jnp.where(middle, recv_ref[...], own_ref[...])
+    acc_ref[...] += mm(grads, w_ref[...], TN)
+
+    @pl.when(step == pl.num_programs(0) - 1)
+    def _():
+        near_ref[...] = acc_ref[pl.ds(pl.multiple_of(s * count, count), count), :]
+        far_ref[...] = acc_ref[pl.ds(pl.multiple_of((1 - s) * count, count), count), :].astype(BF)
+
+
+def qkv_back(ids, own, received, w_qkv):
+    local, rows = received.shape
+    count = rows // 2
+    tile = local
+    third = local // tile
+
+    def own_at(i, ids):
+        return (jnp.where(i < third, i, jnp.clip(i - third, third - 1, 2 * third - 1)), 0)
+
+    return pl.pallas_call(
+        qkv_back_kernel,
+        grid_spec=pltpu.PrefetchScalarGridSpec(
+            num_scalar_prefetch=1,
+            grid=(3 * third,),
+            in_specs=[
+                pl.BlockSpec((tile, rows), own_at),
+                pl.BlockSpec((tile, rows), lambda i, ids: (jnp.clip(i - third, 0, third - 1), 0)),
+                pl.BlockSpec((tile, D), lambda i, ids: (i, 0)),
+            ],
+            out_specs=[pl.BlockSpec((count, D), lambda i, ids: (0, 0))] * 2,
+            scratch_shapes=[pltpu.VMEM((rows, D), F32)],
+        ),
+        out_shape=[shape((count, D), F32), shape((count, D), BF)],
+        name="qkv_back",
+        cost_estimate=cost(6),
+    )(ids, own, received, w_qkv)
+
+
+def tokens_kernel(
+    ids, slices, tok_ref, near_ref, recv_ref, mid_near, mid_far, mod_ref, gain_ref, *refs
+):
+    qgain_ref, kgain_ref, cgain_ref, dgate_ref, early_ref, out_ref, late_ref = refs
+    b, s = ids[0], ids[1]
+    half = mid_near.shape[1]
+    clip, _, _ = clip_at(slices, b)
+    values = tok_ref[...].astype(F32)
+    inverse = row_inverse(values)
+    unit = values * inverse
+    scale = 1.0 + mod_ref[1:2, :]
+    gain = gain_ref[...]
+    grad = near_ref[...] + recv_ref[...].astype(F32)
+    scaled = grad * scale
+    unit_grad = scaled * gain
+    mean = jnp.mean(unit_grad * unit, axis=-1, keepdims=True)
+    mid_own, mid_other = mid_near[...], mid_far[...].astype(F32)
+    middle = jnp.concatenate(
+        [jnp.where(s == 0, mid_own, mid_other), jnp.where(s == 0, mid_other, mid_own)], axis=1
+    )
+    out_ref[...] = inverse * (unit_grad - unit * mean) + middle
+    shift_row = jnp.sum(grad, axis=0, keepdims=True)
+    with_unit = grad * unit
+    scale_row = jnp.sum(with_unit, axis=0, keepdims=True) * gain
+    norm_row = jnp.sum(scaled * unit, axis=0, keepdims=True)
+    rows = [shift_row[:, :half], shift_row[:, half:], scale_row[:, :half], scale_row[:, half:]]
+    late_ref[...] = jnp.zeros_like(late_ref)
+    for c in range(CLIPS):
+        for i, row in enumerate(rows):
+            late_ref[4 * c + i : 4 * c + i + 1, :] = jnp.where(clip == c, row, 0.0)
+    late_ref[16:17, :] = norm_row[:, :half]
+    late_ref[17:18, :] = norm_row[:, half:]
+    for i, ref in enumerate((qgain_ref, kgain_ref, cgain_ref)):
+        late_ref[18 + i : 19 + i, :] = place_row(b, ref[...])
+    heads = qgain_ref.shape[0] // HD
+    lane = lax.broadcasted_iota(jnp.int32, (1, half), 1)
+    gate_row = jnp.zeros((1, half), F32)
+    for h in range(heads):
+        value = jnp.sum(dgate_ref[h : h + 1, :], axis=1, keepdims=True)
+        gate_row = gate_row + jnp.where(lane == b // GROUP * heads + h, value, 0.0)
+    late_ref[21:22, :] = gate_row
+    late_ref[24:, :] = early_ref[...]
+
+
+def tokens_back(ids, slices, tok, near, received, mid_near, mid_far, mod, gain, parts):
+    return pl.pallas_call(
+        tokens_kernel,
+        in_specs=[SMEM, SMEM] + [VMEM] * 12,
+        out_specs=[VMEM, VMEM],
+        out_shape=[shape(tok.shape, F32), shape((48, D // 2), F32)],
+        name="tokens_back",
+        cost_estimate=cost(3.5),
+    )(ids, slices, tok, near, received, mid_near, mid_far, mod, gain, *parts)
+
+
+def finish_kernel(ids, late_a, late_b, mod_ref, gains_ref):
+    s = ids[1]
+    early_a, early_b = late_a.at[pl.ds(24, 24)], late_b.at[pl.ds(24, 24)]
+
+    def joined(a, b, i):
+        own, other = a[i : i + 1, :], b[i : i + 1, :]
+        return jnp.concatenate(
+            [jnp.where(s == 0, own, other), jnp.where(s == 0, other, own)], axis=1
+        )
+
+    def added(a, b, i):
+        both = a[i : i + 2, :] + b[i : i + 2, :]
+        return jnp.concatenate([both[0:1], both[1:2]], axis=1)
+
+    for c in range(CLIPS):
+        low = [added(late_a, late_b, 4 * c), added(late_a, late_b, 4 * c + 2), joined(early_a, early_b, 5 * c)]
+        high = [
+            joined(early_a, early_b, 5 * c + 1),
+            joined(early_a, early_b, 5 * c + 2),
+            added(early_a, early_b, 5 * c + 3),
+        ]
+        for i in range(3):
+            mod_ref[c : c + 1, i * D : (i + 1) * D] = jnp.where(s == 0, low[i], high[i])
+    gains_ref[...] = jnp.zeros_like(gains_ref)
+    gains_ref[0:1, :] = added(late_a, late_b, 16)
+    for i in range(3):
+        gains_ref[1 + i : 2 + i, :] = joined(late_a, late_b, 18 + i)
+    gains_ref[4:5, :] = joined(early_a, early_b, 20)
+    gains_ref[5:6, :] = joined(late_a, late_b, 21)
+
+
+def finish(ids, late_a, late_b):
+    return pl.pallas_call(
+        finish_kernel,
+        in_specs=[SMEM] + [VMEM] * 2,
+        out_specs=[VMEM, VMEM],
+        out_shape=[shape((CLIPS, 3 * D), F32), shape((8, D), F32)],
+        name="finish",
+        cost_estimate=cost(1.7),
+    )(ids, late_a, late_b)
+
+
+def caption_back_kernel(ids, sum_ref, raw_ref, gains_ref, out_ref, gain_ref):
+    b, s = ids[0], ids[1]
+    width = gain_ref.shape[0]
+    base = s * LINE * width + b // GROUP * width
+    cols = pl.ds(pl.multiple_of(lax.rem(b, GROUP) * CAP, CAP), CAP)
+    for h in range(width // HD):
+        at = slice(h * HD, h * HD + HD)
+        gain = gains_ref[pl.ds(pl.multiple_of(base + h * HD, HD), HD), 2:3]
+        raw = raw_ref[at, cols]
+        inverse = lax.rsqrt(jnp.mean(raw * raw, axis=0, keepdims=True) + EPSILON)
+        unit = raw * inverse
+        grad = sum_ref[at, :]
+        gain_ref[at, :] = jnp.sum(grad * unit, axis=1, keepdims=True)
+        unit_grad = grad * gain
+        out_ref[at, :] = (
+            inverse * (unit_grad - unit * jnp.mean(unit_grad * unit, axis=0, keepdims=True))
+        ).astype(BF)
+    out_ref[width:, :] = sum_ref[width:, :].astype(BF)
+
+
+def caption_back(ids, total, raw, gains):
+    return pl.pallas_call(
+        caption_back_kernel,
+        in_specs=[SMEM] + [VMEM] * 3,
+        out_specs=[VMEM, VMEM],
+        out_shape=[shape(total.shape, BF), shape((total.shape[0] // 2, 1), F32)],
+        name="caption_back",
+        cost_estimate=cost(2.3),
+    )(ids, total, raw, gains)
+
+
+def caption_weight_kernel(ids, *refs):
+    raw_refs, cap_ref, out_refs = refs[:GROUP], refs[GROUP], refs[GROUP + 1 :]
+    b = ids[0]
+    each = out_refs[0].shape[1]
+    place = lax.rem(b, GROUP)
+    for k in range(LINE):
+        at = pl.multiple_of((lax.rem(b // GROUP - k + LINE, LINE) * GROUP + place) * each, each)
+        total = None
+        for j in range(GROUP):
+            rows = pl.ds(pl.multiple_of(jnp.bitwise_xor(place, j) * CAP, CAP), CAP)
+            part = mm(raw_refs[j][...], cap_ref[rows, pl.ds(at, each)], NN)
+            total = part if total is None else total + part
+        out_refs[k][...] = total.astype(BF)
+
+
+def caption_weights(ids, raws, caption):
+    rows = raws[0].shape[0]
+    return pl.pallas_call(
+        caption_weight_kernel,
+        in_specs=[SMEM] + [VMEM] * (GROUP + 1),
+        out_specs=[VMEM] * LINE,
+        out_shape=[shape((rows, YD // (LINE * GROUP)), BF)] * LINE,
+        name="caption_weights",
+        cost_estimate=cost(4),
+    )(ids, *raws, caption)
+
+
+def caption_join_kernel(ids, *refs):
+    parts, out_ref = refs[:LINE], refs[LINE]
+    width = parts[0].shape[0] // 2
+    for k in range(LINE):
+        at = chunk_at(ids[0], k, width)
+        for j in range(2):
+            out_ref[j, pl.ds(at, width), :] = parts[k][j * width : (j + 1) * width, :].astype(F32)
+
+
+def caption_join(ids, parts):
+    both, each = parts[0].shape
+    return pl.pallas_call(
+        caption_join_kernel,
+        in_specs=[SMEM] + [VMEM] * LINE,
+        out_specs=VMEM,
+        out_shape=shape((2, both // 2 * LINE, each), F32),
+        name="caption_join",
+        cost_estimate=cost(2),
+    )(ids, *parts)
+
+
+def weight_kernel(count, dims, *refs):
+    left, right, out_ref = refs[:count], refs[count : 2 * count], refs[-1]
+    total = None
+    for a_ref, g_ref in zip(left, right):
+        part = mm(a_ref[0, 0].reshape(-1, a_ref.shape[-1]), g_ref[...], dims)
+        total = part if total is None else total + part
+    out_ref[...] = total.reshape(out_ref.shape).astype(BF)
+
+
+def weight_grads(left, right, by_rows, tile, kind, total, place, into=None):
+    _, _, chunks, columns, tokens = left[0][0].shape
+    rows = right[0].shape[0 if by_rows else 1]
+    left_specs = [
+        pl.BlockSpec((1, 1, chunks, columns, tokens), lambda i, n=n: (n, kind, 0, 0, 0))
+        for _, n in left
+    ]
+    if by_rows:
+        right_spec = pl.BlockSpec((tile, tokens), lambda i: (i, 0))
+    else:
+        right_spec = pl.BlockSpec((tokens, tile), lambda i: (0, i))
+    args = [a for a, _ in left] + list(right)
+    specs = left_specs + [right_spec] * len(right)
+    aliases = {}
+    if into is not None:
+        aliases = {len(args): 0}
+        args.append(into)
+        specs.append(pl.BlockSpec(memory_space=pl.ANY))
+    return pl.pallas_call(
+        functools.partial(weight_kernel, len(left), NT if by_rows else NN),
+        grid=(rows // tile,),
+        in_specs=specs,
+        out_specs=pl.BlockSpec((chunks, columns, tile), lambda i: (0, 0, place(i))),
+        out_shape=shape((chunks, columns, total), BF),
+        input_output_aliases=aliases,
+        name="weight_grads",
+        cost_estimate=cost(5),
+    )(*args)
+
+
+def fast_body(
+    tokens,
+    cotangent,
+    clip_slices,
+    caption_lengths,
+    caption,
+    cond,
+    ada_w,
+    norm_gain,
+    w_qkv,
+    q_gain,
+    k_gain,
+    w_caption,
+    ky_gain,
+    cross_gate,
+    w_out,
+    ffn_gain,
+    w_gate_up,
+    w_down,
+):
+    bucket_count = LINE * GROUP
+    seq_count = lax.axis_size("seq")
+    local_width = D // seq_count
+    units = FF // seq_count
+    b = lax.axis_index(BUCKET)
+    s = lax.axis_index("seq")
+    z, g, c, y = b // GROUP, b % GROUP, b % 2, (b // 2) % 2
+    ids = jnp.stack([b, s]).astype(jnp.int32)
+
+    def xswap(v):
+        return lax.ppermute(v, "seq", [(0, 1), (1, 0)])
+
+    def hop(v, to):
+        return lax.ppermute(v, BUCKET, [(i, to(i)) for i in range(bucket_count)])
+
+    def cswap(v):
+        return hop(v, lambda i: i ^ 1)
+
+    def yswap(v):
+        return hop(v, lambda i: i ^ 2)
+
+    def zshift(v, k):
+        return hop(v, lambda i: (i + GROUP * k) % bucket_count)
+
+    def after(v, *others):
+        return lax.optimization_barrier((v, *others))[0]
+
+    def pick(v, index):
+        return lax.dynamic_index_in_dim(v, index, 0, False)
+
+    def spread(parts):
+        return [parts[0]] + [zshift(parts[k], k) for k in range(1, LINE)]
+
+    def unspread(parts):
+        return [parts[0]] + [zshift(parts[k], LINE - k) for k in range(1, LINE)]
+
+    half = HD // 2
+    rows = tokens.shape[0] * seq_count
+    frequency = jnp.exp(jnp.arange(half, dtype=F32) * (-2.0 * math.log(10000.0) / (2 * half)))
+    positions = jnp.arange(bucket_count * rows, dtype=F32).reshape(bucket_count, 1, rows)
+    angles = positions * frequency[None, :, None]
+    cosine, sine = jnp.cos(angles), jnp.sin(angles)
+    gains = jnp.stack([q_gain, k_gain, ky_gain], axis=1)
+    gates = jnp.tanh(cross_gate)
+    norm_row, ffn_row = norm_gain[None], ffn_gain[None]
+
+    tok_far = xswap(tokens)
+    activation = jax.nn.silu(cond).astype(BF)
+    mod_near = mm(activation, ada_w, NT)
+    mod_far = xswap(mod_near)
+    each = units // 2
+    sent = lax.dynamic_slice_in_dim(w_gate_up, (1 - s) * units + c * each, each, 0)
+    tok_far, sent = lax.optimization_barrier((tok_far, sent))
+    projected, hidden, mod = pre(
+        ids, clip_slices, tokens, tok_far, mod_near, mod_far, norm_row, w_qkv
+    )
+    local = lax.slice_in_dim(projected, local_width, 2 * local_width, axis=0)
+    swapped = xswap(local)
+    hid_own, hid_c, hid_y = cut(ids, [hidden], [False])
+    came = lax.all_gather(after(sent, swapped), ("seq", "c"), axis=0, tiled=True)
+    swapped = after(swapped, hid_own)
+    kv_parts, q_parts = route(ids, projected, swapped)
+    kv_here = spread(kv_parts)
+    q_here = spread(q_parts)
+    caption_rows = caption.reshape(CLIPS * CAP, YD)
+    cap_raw, cap_kv = caption_keys(ids, w_caption, after(caption_rows, kv_parts[0]), gains)
+    kv_here[1] = after(kv_here[1], cap_kv, cosine, sine)
+    cot_far = xswap(after(cotangent, cap_kv))
+    kv_own = jnp.stack(kv_here)
+    kv_y = yswap(kv_own)
+    kv_c = cswap(kv_own)
+    kv_cy = cswap(kv_y)
+    kv_pieces = [kv_own, kv_c, kv_y, kv_cy]
+    grad_mlp = (
+        jnp.where(
+            s == 0,
+            jnp.concatenate([cotangent, cot_far], 0),
+            jnp.concatenate([cot_far, cotangent], 0),
+        ).astype(F32)
+        * mod[5:6]
+    ).astype(BF)
+    q_here[0] = after(q_here[0], grad_mlp)
+    combined, saved = attend(
+        ids, clip_slices, caption_lengths, gates, q_here, kv_pieces, cap_kv, gains, cosine, sine
+    )
+    heads_own = unspread(combined)
+    heads_far = [xswap(v) for v in heads_own]
+    attention, branch = out_proj(ids, heads_own, heads_far, w_out)
+    branch_far = xswap(branch)
+    att_own, att_c, att_y = cut(ids, [attention, grad_mlp], [True, False])
+    branch_far = after(branch_far, att_own)
+    (
+        inner,
+        grad_kept,
+        grad_came,
+        mlp_in,
+        middle,
+        near,
+        far,
+        mean_near,
+        near_out,
+        far_out,
+    ) = ffn(ids, [tokens, tok_far], [branch, branch_far], grad_mlp, mod, ffn_row, w_gate_up, came, w_down)
+    received = xswap(far)
+    mean_far = xswap(mean_near)
+    ffn_own, ffn_c, ffn_y = cut(ids, [mlp_in], [False])
+    received = after(received, ffn_own)
+
+    def left_of(own, c_part, y_part):
+        came_y = yswap(y_part)
+        return [(own, 0), (cswap(c_part), 0), (came_y, 0), (cswap(came_y), 1)]
+
+    def right_of(v):
+        far_v = yswap(v)
+        return [v, cswap(v), far_v, cswap(far_v)]
+
+    def line_sum(parts):
+        right_in = left_in = None
+        for t in range(1, LINE):
+            to_right = pick(parts, jnp.clip(LINE - t + z, 0, LINE - 1))
+            to_left = pick(parts, jnp.clip(t - LINE + z, 0, LINE - 1))
+            if t > 1:
+                to_right = (to_right.astype(F32) + right_in.astype(F32)).astype(BF)
+                to_left = (to_left.astype(F32) + left_in.astype(F32)).astype(BF)
+            ends = range(GROUP * t)
+            right_in = lax.ppermute(to_right, BUCKET, [(i, i + GROUP) for i in ends])
+            last = bucket_count - 1
+            left_in = lax.ppermute(to_left, BUCKET, [(last - i, last - i - GROUP) for i in ends])
+        return pick(parts, z).astype(F32) + right_in.astype(F32) + left_in.astype(F32)
+
+    def scatter(parts):
+        return lax.psum_scatter(parts, "z", scatter_dimension=0, tiled=False)
+
+    att_left = left_of(att_own, att_c, att_y)
+    inner_all = right_of(inner)
+    tile = 512
+    per = units // tile
+    (sums, grad_branch, mid_near, mid_far), near_heads, far_heads = mid_back(
+        ids, near, received, mean_near, mean_far, middle, [cotangent, cot_far], branch, mod, ffn_row, w_out
+    )
+    grad_heads = [
+        (near_heads[k] + xswap(far_heads[k]).astype(F32)).astype(BF) for k in range(LINE)
+    ]
+    grad_here = spread(grad_heads)
+    parts_inner = weight_grads(att_left, inner_all, False, tile, 1, units, lambda i: i)
+    sum_inner = scatter(parts_inner)
+    ffn_left = left_of(*[after(v, inner_all[2]) for v in (ffn_own, ffn_c, ffn_y)])
+    kept_all = right_of(after(grad_kept, inner_all[2]))
+    out_recv = xswap(after(far_out, grad_heads[0]))
+    output, early = output_sums(ids, clip_slices, near_out, out_recv, middle, cotangent, mod, sums)
+    grad_here[0] = after(grad_here[0], parts_inner)
+    grads_q, (q_gain_part, cap_keep, cap_send, gate_part), grads_kv = attend_back(
+        ids, clip_slices, caption_lengths, gates, q_here, grad_here, saved, cap_kv, gains, cosine, sine
+    )
+    came_all = right_of(after(grad_came, kept_all[2]))
+    here = (grads_kv[0].astype(F32) + cswap(grads_kv[1]).astype(F32)).astype(BF)
+    away = (grads_kv[2].astype(F32) + cswap(grads_kv[3]).astype(F32)).astype(BF)
+    away_here = yswap(away)
+    back_q = unspread(grads_q)
+    pair = cap_keep + cswap(cap_send)
+    mid_came = xswap(after(mid_far, away))
+
+    kept_all[0] = after(kept_all[0], away)
+    parts_a = weight_grads(ffn_left, kept_all, False, tile, 0, 2 * units, lambda i: i)
+    parts_a = weight_grads(ffn_left, came_all, False, tile, 0, 2 * units, lambda i: i + per, parts_a)
+    sum_a = scatter(parts_a)
+    away_here = after(away_here, parts_a)
+    back_kv, k_gain_part = keys_back(ids, clip_slices, here, away_here, kv_own, gains, cosine, sine)
+    back_kv = unspread(back_kv)
+    branch_all = right_of(after(grad_branch, away_here))
+    hid_left = left_of(hid_own, hid_c, hid_y)
+
+    cap_total = pick(pair, y) + yswap(after(pick(pair, 1 - y), away_here))
+    raw_cap, cap_gain_part = caption_back(ids, cap_total, cap_raw, gains)
+    raw_y = yswap(raw_cap)
+    cap_parts = caption_weights(ids, [raw_cap, cswap(raw_cap), raw_y, cswap(raw_y)], caption_rows)
+    parts_out = weight_grads(att_left, branch_all, False, 384, 0, local_width, lambda i: i)
+    sum_out = scatter(parts_out)
+    back_kv[1] = after(back_kv[1], parts_out, cap_parts[0])
+
+    packed, send = pack(ids, back_q, back_kv)
+    packed_recv = xswap(send)
+    packed_all = right_of(packed)
+    recv_all = right_of(packed_recv)
+    cap_parts = unspread([after(v, packed) for v in cap_parts])
+    tok_near, tok_send = qkv_back(ids, packed, packed_recv, w_qkv)
+    tok_recv = xswap(tok_send)
+    token_grad, late = tokens_back(
+        ids,
+        clip_slices,
+        tokens,
+        tok_near,
+        tok_recv,
+        mid_near,
+        mid_came,
+        mod,
+        norm_row,
+        [q_gain_part, k_gain_part, cap_gain_part, gate_part, early],
+    )
+    tile = 384
+    parts_c = weight_grads(
+        hid_left, packed_all, True, tile, 0, 3 * local_width, lambda i: jnp.where(i < 2, i, i + 2)
+    )
+    parts_c = weight_grads(
+        hid_left, recv_all, True, tile, 0, 3 * local_width, lambda i: i + 2, parts_c
+    )
+    sum_c = line_sum(parts_c)
+    caption_w_grad = caption_join(ids, cap_parts)
+    def bucket_sum(v):
+        v = v + cswap(v)
+        v = v + yswap(v)
+        v = v + hop(v, lambda i: i ^ GROUP)
+        return v + hop(v, lambda i: i ^ (2 * GROUP))
+
+    late_sum = bucket_sum(late)
+    late_far = xswap(late_sum)
+    mod_grad, gain_rows = finish(ids, late_sum, late_far)
+    mod_mine = mod_grad.astype(BF)
+    cols_local = CD // bucket_count
+    act_cols = lax.dynamic_slice_in_dim(activation, b * cols_local, cols_local, 1)
+    ada_grad = mm(mod_mine, act_cols, TN)
+    cond_part = mm(mod_mine, ada_w, NN)
+    cond_sigmoid = jax.nn.sigmoid(cond)
+    cond_grad = (
+        (cond_part + xswap(cond_part)) * cond_sigmoid * (1.0 + cond * (1.0 - cond_sigmoid))
+    )
+    heads_each = H // seq_count
+    cross_out = jnp.concatenate(
+        [gain_rows[5, :heads_each], gain_rows[5, local_width : local_width + heads_each]]
+    )
+
+    down_out = sum_inner.astype(F32).T
+    kept_out = sum_a[:, :units].astype(F32)
+    came_out = xswap(sum_a[:, units:]).astype(F32)
+    gate_up_out = jnp.where(
+        s == 0,
+        jnp.concatenate([kept_out, came_out], 1),
+        jnp.concatenate([came_out, kept_out], 1),
+    ).T
+    return (
+        output,
+        token_grad,
+        cond_grad,
+        ada_grad,
+        gain_rows[0],
+        sum_c.T,
+        gain_rows[1],
+        gain_rows[2],
+        caption_w_grad,
+        gain_rows[3],
+        cross_out,
+        sum_out.astype(F32).T,
+        gain_rows[4],
+        gate_up_out,
+        down_out,
+    )
 
 
 def project(activations, weight):
@@ -71,7 +1388,7 @@
     return 512 if row_count % 512 == 0 else row_count
 
 
-def body(
+def general_body(
     tokens,
     cotangent,
     clip_slices,
@@ -609,9 +1926,14 @@
 
 
 def solution(mesh):
+    fits = mesh.shape["seq"] == 2 and mesh.shape["bucket"] == LINE * GROUP
+    bucket = ("bucket",)
+    if fits:
+        bucket = BUCKET
+        mesh = Mesh(mesh.devices.reshape(LINE, 2, GROUP // 2, 2), (*BUCKET, "seq"))
     in_specs = (
-        P(("bucket", "seq"), None),
-        P(("bucket", "seq"), None),
+        P((*bucket, "seq"), None),
+        P((*bucket, "seq"), None),
         P(),
         P(),
         P(),
@@ -630,20 +1952,21 @@
         P("seq", None),
     )
     out_specs = (
-        P(("bucket", "seq"), None),
-        P(("bucket", "seq"), None),
+        P((*bucket, "seq"), None),
+        P((*bucket, "seq"), None),
         P(),
-        P("seq", "bucket"),
+        P("seq", bucket),
         P(),
-        P("seq", "bucket"),
+        P("seq", bucket),
         P(),
         P(),
-        P(None, "seq", "bucket"),
+        P(None, "seq", bucket),
         P(),
         P(),
-        P("seq", "bucket"),
+        P("seq", bucket),
         P(),
-        P("seq", "bucket"),
-        P("seq", "bucket"),
-    )
+        P("seq", bucket),
+        P("seq", bucket),
+    )
+    body = fast_body if fits else general_body
     return jax.shard_map(body, mesh=mesh, in_specs=in_specs, out_specs=out_specs, check_vma=False)

time: 2740 us -> 594 us (0.22)
  waiting for transfers between devices: 1970 us -> 228 us
  local copies, waits for them, and re-layouts: 247 us -> 22.4 us
  Pallas kernels: 0 us -> 189 us
  matrix products: 182 us -> 12.8 us
  other arithmetic: 168 us -> 24.8 us
  starting transfers between devices: 25 us -> 92.8 us
  blocking collectives: 64 us -> 0 us
  loops' own time: 49.2 us -> 0 us
    reduce_scatter x4 -> x3, waiting for transfers between devices: 979 us -> 0.04 us  [scatter(): return lax.psum_scatter(parts, 'z', scatter_dimension=0, tiled=False)]
    all_gather x7 -> x1, waiting for transfers between devices: 837 us -> 0.01 us  [fast_body(): lax.all_gather(after(sent, swapped), ('seq', 'c'), axis=0, tiled=True)]
    ppermute x0 -> x91, waiting for transfers between devices: none -> 228 us  [the longest x63 162 us: hop(): return lax.ppermute(v, BUCKET, [(i, to(i)) for i in range(bucket_count)])]
    pallas_call x0 -> x26, Pallas kernels: none -> 189 us  [the longest x1 40.7 us: attend_back(): pl.pallas_call(attend_back_kernel, in_specs=[SMEM] * 4 + [VMEM] * (2 * LI...]
    dot_general x40 -> x3, matrix products: 181 us -> 12.8 us  [mm(): return lax.dot_general(a, b, dims, preferred_element_type=F32)]
    psum x1 -> x0, waiting for transfers between devices: 139 us -> none  [body(): lax.psum((norm_gain_grad, q_gain_grad, k_gain_grad, ky_gain_full, gate_fu...]
    ppermute x0 -> x91, starting transfers between devices: none -> 92.6 us  [the longest x63 49.5 us: hop(): return lax.ppermute(v, BUCKET, [(i, to(i)) for i in range(bucket_count)])]
    convert_element_type x9 -> x0, local copies, waits for them, and re-layouts: 80.4 us -> none  [the longest x1 72.8 us: body(): weight_grad_seq = lax.psum_scatter(jnp.concatenate(terms, axis=1).reshape...]
  transfers between devices with their start and end apart: 19 -> 95, of which waited for: 15 -> 36; matrix products, arithmetic and copies ran while one was open for 10% -> 8% of each run, Pallas kernels for 0% -> 28%
where the time goes in v2:
time: 594 us; the launch traced here: 585 us
  waiting for transfers between devices  228 us (38%)
  Pallas kernels  189 us (32%)
  starting transfers between devices  92.8 us (16%)
  other arithmetic  24.8 us (4%)
  local copies, waits for them, and re-layouts  22.4 us (4%)
  between operations  15.2 us (3%)
  matrix products  12.8 us (2%)
    ppermute x63, waiting for transfers between devices, hop(): return lax.ppermute(v, BUCKET, [(i, to(i)) for i in range(bucket_count)])  162 us
    ppermute x63, starting transfers between devices, hop(): return lax.ppermute(v, BUCKET, [(i, to(i)) for i in range(bucket_count)])  49.5 us
    ppermute x22, waiting for transfers between devices, xswap(): return lax.ppermute(v, 'seq', [(0, 1), (1, 0)])  42.8 us
    pallas_call x1, Pallas kernels, attend_back(): pl.pallas_call(attend_back_kernel, in_specs=[SMEM] * 4 + [VMEM] * (2 * LI...  40.7 us
    pallas_call x1, Pallas kernels, attend(): pl.pallas_call(attend_kernel, in_specs=[SMEM] * 4 + [VMEM] * (LINE + GROU...  34 us
    pallas_call x6, Pallas kernels, weight_grads(): pl.pallas_call(functools.partial(weight_kernel, len(left), NT if by_rows...  29.1 us
    ppermute x22, starting transfers between devices, xswap(): return lax.ppermute(v, 'seq', [(0, 1), (1, 0)])  28.6 us
    pallas_call x1, Pallas kernels, ffn(): pl.pallas_call(ffn_kernel, grid_spec=pltpu.PrefetchScalarGridSpec(num_sca...  19.9 us
  transfers between devices with their start and end apart: 95, of which 36 were waited for; matrix products, arithmetic and copies ran while one was open for 8% of the time, Pallas kernels for 28%

profile of v2, /device:TPU:0, one launch (start us, length us, event | category | flops | bytes accessed | tf_op | source)
XLA Modules:
  0.0 585.1 jit_solution(11093329479103464021)
XLA Ops:
  11.0 6.2 %fusion.11.mod_a = f32[4,4608]{1,0:T(4,128)S(1)} fusion(bf16[4,1024]{1,0:T(4,128)(2,1)S(1)} %multiply_convert_fusion.1, bf16[4608,1024]{1,0:T(8,128)(2,1)} %param.24), kind=kOutput, calls=%fused_computation.53 | convolution fusion | flops 37748736 | bytes 9519104 | tf_op jit(solution)/shard_map/dot_general | solution.py:42
  23.5 6.6 %pre.1 = (bf16[2304,256]{1,0:T(8,128)(2,1)}, bf16[256,1536]{1,0:T(8,128)(2,1)}, f32[8,1536]{1,0:T(8,128)}) custom-call(s32[2]{0:T(128)} %pad_add_fusion.ids, s32[4]{0:T(128)} %slices.11, bf16[128,1536]{1,0:T(8,128)(2,1)} %tok_ref.1, bf16[128,1536]{1,0:T(8,128)(2,1)} %copy-done.6, f32[4,4608]{1,0:T(4,128)} %copy-done.40, f32[4,4608]{1,0:T(4,128)} %copy-done.66, ...), custom_call_target="tpu_custom_call" | custom-call | bytes 18000000 | tf_op jit(solution)/shard_map/pre/pallas_call | solution.py:122
  33.3 8.6 %collective-permute-done.2.r_ref = bf16[768,256]{1,0:T(8,128)(2,1)S(1)} collective-permute-done((bf16[768,256]{1,0:T(8,128)(2,1)S(1)}, bf16[768,256]{1,0:T(8,128)(2,1)S(1)}, u32[]{:S(2)}, u32[]{:S(2)}) %collective-permute-start.2) | collective-permute-done | bytes 393248 | tf_op jit(solution)/shard_map/ppermute | solution.py:1092
  57.4 8.1 %caption_keys.1 = (f32[384,512]{1,0:T(8,128)}, bf16[4,384,128]{2,1,0:T(8,128)(2,1)}) custom-call(s32[2]{0:T(128)} %pad_add_fusion.ids, bf16[2,768,4096]{2,1,0:T(8,128)(2,1)} %w_ref.5, bf16[512,4096]{1,0:T(8,128)(2,1)} %bitcast.52, f32[1536,3]{1,0:T(8,128)} %copy.38.gains_ref.refs_9_.refs_15_), custom_call_target="tpu_custom_call" | custom-call | bytes 24000000 | tf_op jit(solution)/shard_map/caption_keys/pallas_call | solution.py:204
  68.7 15.6 %collective-permute-done.11.refs_6_ = bf16[4,384,256]{2,1,0:T(8,128)(2,1)S(1)} collective-permute-done((bf16[4,384,256]{2,1,0:T(8,128)(2,1)S(1)}, bf16[4,384,256]{2,1,0:T(8,128)(2,1)S(1)}, u32[]{:S(2)}, u32[]{:S(2)}) %collective-permute-start.11) | collective-permute-done | bytes 786464 | tf_op jit(solution)/shard_map/ppermute | solution.py:1095
  99.6 34.0 %attend.1 = (bf16[192,256]{1,0:T(8,128)(2,1)}, bf16[192,256]{1,0:T(8,128)(2,1)}, bf16[192,256]{1,0:T(8,128)(2,1)}, bf16[192,256]{1,0:T(8,128)(2,1)}, f32[4,192,2...) custom-call(s32[2]{0:T(128)} %pad_add_fusion.ids, ...), custom_call_target="tpu_custom_call" | custom-call | bytes 99000000 | tf_op jit(solution)/shard_map/attend/pallas_call | solution.py:300
  169.1 19.9 %ffn.1 = (bf16[256,2048]{1,0:T(8,128)(2,1)}, bf16[256,2048]{1,0:T(8,128)(2,1)}, bf16[256,2048]{1,0:T(8,128)(2,1)}, bf16[256,1536]{1,0:T(8,128)(2,1)}, f32[256,15...) custom-call(s32[2]{0:T(128)} %pad_add_fusion.ids, ...), custom_call_target="tpu_custom_call" | custom-call | bytes 54000000 | tf_op jit(solution)/shard_map/ffn/pallas_call | solution.py:468
  192.3 23.2 %collective-permute-done.29.refs_6_ = bf16[256,2048]{1,0:T(8,128)(2,1)} collective-permute-done((bf16[256,2048]{1,0:T(8,128)(2,1)}, bf16[256,2048]{1,0:T(8,128)(2,1)}, u32[]{:S(2)}, u32[]{:S(2)}) %collective-permute-start.29) | collective-permute-done | bytes 1048608 | tf_op jit(solution)/shard_map/ppermute | solution.py:1095
  215.5 16.7 %collective-permute-done.26.refs_2_ = bf16[2,2,4,96,256]{4,3,2,1,0:T(8,128)(2,1)S(1)} collective-permute-done((bf16[2,2,4,96,256]{4,3,2,1,0:T(8,128)(2,1)S(1)}, bf16[2,2,4,96,256]{4,3,2,1,0:T(8,128)(2,1)S(1)}, u32[]{:S(2)}, u32[]{:S(2)}) %collective-permute-start.26) | collective-permute-done | bytes 786464 | tf_op jit(solution)/shard_map/ppermute | solution.py:1095
  239.0 5.6 mid_back.1
  254.6 5.6 weight_grads.6
  273.9 40.7 %attend_back.1 = (bf16[192,256]{1,0:T(8,128)(2,1)}, bf16[192,256]{1,0:T(8,128)(2,1)}, bf16[192,256]{1,0:T(8,128)(2,1)}, bf16[192,256]{1,0:T(8,128)(2,1)}, f32[19...) custom-call(s32[2]{0:T(128)} %pad_add_fusion.ids, ...), custom_call_target="tpu_custom_call" | custom-call | bytes 120000000 | tf_op jit(solution)/shard_map/attend_back/pallas_call | solution.py:708
  315.2 11.0 %collective-permute-done.44.refs_2_ = bf16[2,1,4,96,256]{4,3,2,1,0:T(8,128)(2,1)S(1)} collective-permute-done((bf16[2,1,4,96,256]{4,3,2,1,0:T(8,128)(2,1)S(1)}, bf16[2,1,4,96,256]{4,3,2,1,0:T(8,128)(2,1)S(1)}, u32[]{:S(2)}, u32[]{:S(2)}) %collective-permute-start.44) | collective-permute-done | bytes 393248 | tf_op jit(solution)/shard_map/ppermute | solution.py:1095
  333.7 5.5 weight_grads.7.refs_8_
  339.3 5.6 weight_grads.8
  350.5 9.5 %collective-permute-done.54.refs_6_ = bf16[256,768]{1,0:T(8,128)(2,1)S(1)} collective-permute-done((bf16[256,768]{1,0:T(8,128)(2,1)S(1)}, bf16[256,768]{1,0:T(8,128)(2,1)S(1)}, u32[]{:S(2)}, u32[]{:S(2)}) %collective-permute-start.54) | collective-permute-done | bytes 393248 | tf_op jit(solution)/shard_map/ppermute | solution.py:1095
  397.6 12.2 %collective-permute-done.38.refs_2_ = bf16[192,256]{1,0:T(8,128)(2,1)S(1)} collective-permute-done((bf16[192,256]{1,0:T(8,128)(2,1)S(1)}, bf16[192,256]{1,0:T(8,128)(2,1)S(1)}, u32[]{:S(2)}, u32[]{:S(2)}) %collective-permute-start.38) | collective-permute-done | bytes 98336 | tf_op jit(solution)/shard_map/ppermute | solution.py:1095
  416.0 9.5 %collective-permute-done.63.recv_ref.refs_4_ = bf16[768,256]{1,0:T(8,128)(2,1)S(1)} collective-permute-done((bf16[768,256]{1,0:T(8,128)(2,1)}, bf16[768,256]{1,0:T(8,128)(2,1)S(1)}, u32[]{:S(2)}, u32[]{:S(2)}) %collective-permute-start.63) | collective-permute-done | bytes 393248 | tf_op jit(solution)/shard_map/ppermute | solution.py:1092
  426.3 7.4 %qkv_back.1 = (f32[128,1536]{1,0:T(8,128)}, bf16[128,1536]{1,0:T(8,128)(2,1)}) custom-call(s32[2]{0:T(128)} %pad_add_fusion.ids, bf16[1536,256]{1,0:T(8,128)(2,1)} %get-tuple-element.222.own_ref.refs_4_, bf16[768,256]{1,0:T(8,128)(2,1)} %copy-done.9, bf16[2304,1536]{1,0:T(8,128)(2,1)} %w_ref.7), custom_call_target="tpu_custom_call" | custom-call | bytes 18000000 | tf_op jit(solution)/shard_map/qkv_back/pallas_call | solution.py:828
  439.4 8.3 %collective-permute-done.65.mid_far = bf16[128,768]{1,0:T(8,128)(2,1)S(1)} collective-permute-done((bf16[128,768]{1,0:T(8,128)(2,1)S(1)}, bf16[128,768]{1,0:T(8,128)(2,1)S(1)}, u32[]{:S(2)}, u32[]{:S(2)}) %collective-permute-start.65) | collective-permute-done | bytes 196640 | tf_op jit(solution)/shard_map/ppermute | solution.py:1092
  456.1 19.1 %collective-permute-done.67 = f32[48,768]{1,0:T(8,128)S(1)} collective-permute-done((f32[48,768]{1,0:T(8,128)S(1)}, f32[48,768]{1,0:T(8,128)S(1)}, u32[]{:S(2)}, u32[]{:S(2)}) %collective-permute-start.67) | collective-permute-done | bytes 147488 | tf_op jit(solution)/shard_map/ppermute | solution.py:1095
  487.0 8.7 %collective-permute-done.69 = f32[48,768]{1,0:T(8,128)S(1)} collective-permute-done((f32[48,768]{1,0:T(8,128)S(1)}, f32[48,768]{1,0:T(8,128)S(1)}, u32[]{:S(2)}, u32[]{:S(2)}) %collective-permute-start.69) | collective-permute-done | bytes 147488 | tf_op jit(solution)/shard_map/ppermute | solution.py:1095
  542.9 7.6 %collective-permute-done.82 = bf16[96,2304]{1,0:T(8,128)(2,1)S(1)} collective-permute-done((bf16[96,2304]{1,0:T(8,128)(2,1)S(1)}, bf16[96,2304]{1,0:T(8,128)(2,1)S(1)}, u32[]{:S(2)}, u32[]{:S(2)}) %collective-permute-start.82) | collective-permute-done | bytes 442400 | tf_op jit(solution)/shard_map/ppermute | solution.py:1207
  566.4 9.3 %collective-permute-done.86 = bf16[96,2304]{1,0:T(8,128)(2,1)S(1)} collective-permute-done((bf16[96,2304]{1,0:T(8,128)(2,1)S(1)}, bf16[96,2304]{1,0:T(8,128)(2,1)S(1)}, u32[]{:S(2)}, u32[]{:S(2)}) %collective-permute-start.86) | collective-permute-done | bytes 442400 | tf_op jit(solution)/shard_map/ppermute | solution.py:1209
  (416 shorter events, 265.4 us)
Async XLA Ops:
  7.2 161.2 %all-gather.2.cloned.1.call-start = ((), (), s32[]{:S(2)}) async-start(), calls=%async_computation.3 | async-start | bytes 15728640 | tf_op jit(solution)/shard_map/all_gather | solution.py:1141
  41.9 466.3 %reduce-scatter.8.cloned.1.call-start = ((), (), s32[]{:S(2)}) async-start(), calls=%async_computation.6 | async-start | bytes 1966080 | tf_op jit(solution)/shard_map/reduce_scatter | solution.py:1213
  67.2 23.5 %collective-permute-start.3 = (bf16[128,1536]{1,0:T(8,128)(2,1)S(1)}, bf16[128,1536]{1,0:T(8,128)(2,1)S(1)}, u32[]{:S(2)}, u32[]{:S(2)}) collective-permute-start(bf16[128,1536]{1,0:T(8,128)(2,1)S(1)} %copy-done.2), channel_id=1, source_target_pairs={{0,1},{1,0},{2,3},{3,2},{4,5},{5,4},{6,7},{7,6},{8,9},{9,8},{10,11... | collective-permute-start | bytes 1179656 | tf_op jit(solution)/shard_map/ppermute | solution.py:1092
  68.7 30.0 %collective-permute-start.10 = (bf16[4,384,256]{2,1,0:T(8,128)(2,1)S(1)}, bf16[4,384,256]{2,1,0:T(8,128)(2,1)S(1)}, u32[]{:S(2)}, u32[]{:S(2)}) collective-permute-start(bf16[4,384,256]{2,1,0:T(8,128)(2,1)S(1)} %pad_maximum_fusion.refs_4_.kv_ref), channel_id=1, source_target_pairs={{0,2},{2,0},{4,6},{6,4},{8,10},{10,8},{12,14},{14,12},{16,18},{18,... | collective-permute-start | bytes 2359304 | tf_op jit(solution)/shard_map/ppermute | solution.py:1095
  189.0 26.5 %collective-permute-start.29 = (bf16[256,2048]{1,0:T(8,128)(2,1)}, bf16[256,2048]{1,0:T(8,128)(2,1)}, u32[]{:S(2)}, u32[]{:S(2)}) collective-permute-start(bf16[256,2048]{1,0:T(8,128)(2,1)} %get-tuple-element.176.refs_4_), channel_id=1, source_target_pairs={{0,4},{2,6},{4,0},{6,2},{8,12},{10,14},{12,8},{14,10},{16,20},{18,... | collective-permute-start | bytes 3145736 | tf_op jit(solution)/shard_map/ppermute | solution.py:1095
  189.1 43.1 %collective-permute-start.26 = (bf16[2,2,4,96,256]{4,3,2,1,0:T(8,128)(2,1)S(1)}, bf16[2,2,4,96,256]{4,3,2,1,0:T(8,128)(2,1)S(1)}, u32[]{:S(2)}, u32[]{:S(2)}) collective-permute-start(bf16[2,2,4,96,256]{4,3,2,1,0:T(8,128)(2,1)S(1)} %copy-done.75), channel_id=1, source_target_pairs={{0,4},{2,6},{4,0},{6,2},{8,12},{10,14},{12,8},{14,10},{16,20},{18,... | collective-permute-start | bytes 2359304 | tf_op jit(solution)/shard_map/ppermute | solution.py:1095
  191.1 45.0 %collective-permute-start.21 = (bf16[256,768]{1,0:T(8,128)(2,1)}, bf16[256,768]{1,0:T(8,128)(2,1)S(1)}, u32[]{:S(2)}, u32[]{:S(2)}) collective-permute-start(bf16[256,768]{1,0:T(8,128)(2,1)} %get-tuple-element.163), channel_id=1, source_target_pairs={{0,1},{1,0},{2,3},{3,2},{4,5},{5,4},{6,7},{7,6},{8,9},{9,8},{10,11... | collective-permute-start | bytes 1179656 | tf_op jit(solution)/shard_map/ppermute | solution.py:1092
  192.3 61.1 %collective-permute-start.28 = (bf16[256,2048]{1,0:T(8,128)(2,1)}, bf16[256,2048]{1,0:T(8,128)(2,1)}, u32[]{:S(2)}, u32[]{:S(2)}) collective-permute-start(bf16[256,2048]{1,0:T(8,128)(2,1)} %get-tuple-element.176.refs_4_), channel_id=1, source_target_pairs={{0,2},{2,0},{4,6},{6,4},{8,10},{10,8},{12,14},{14,12},{16,18},{18,... | collective-permute-start | bytes 3145736 | tf_op jit(solution)/shard_map/ppermute | solution.py:1095
  215.4 39.2 %collective-permute-start.30 = (bf16[256,2048]{1,0:T(8,128)(2,1)}, bf16[256,2048]{1,0:T(8,128)(2,1)}, u32[]{:S(2)}, u32[]{:S(2)}) collective-permute-start(bf16[256,2048]{1,0:T(8,128)(2,1)} %collective-permute-done.29.refs_6_), channel_id=1, source_target_pairs={{0,2},{2,0},{4,6},{6,4},{8,10},{10,8},{12,14},{14,12},{16,18},{18,... | collective-permute-start | bytes 3145736 | tf_op jit(solution)/shard_map/ppermute | solution.py:1095
  215.5 46.0 %collective-permute-start.46 = (bf16[256,2048]{1,0:T(8,128)(2,1)}, bf16[256,2048]{1,0:T(8,128)(2,1)S(1)}, u32[]{:S(2)}, u32[]{:S(2)}) collective-permute-start(bf16[256,2048]{1,0:T(8,128)(2,1)} %get-tuple-element.207.refs_4_), channel_id=1, source_target_pairs={{0,4},{2,6},{4,0},{6,2},{8,12},{10,14},{12,8},{14,10},{16,20},{18,... | collective-permute-start | bytes 3145736 | tf_op jit(solution)/shard_map/ppermute | solution.py:1095
  260.2 249.9 %reduce-scatter.4.cloned.1.call-start = ((), (), s32[]{:S(2)}) async-start(), calls=%async_computation.4 | async-start | bytes 737280 | tf_op jit(solution)/shard_map/reduce_scatter | solution.py:1213
  262.6 64.7 %collective-permute-start.48 = (bf16[256,2048]{1,0:T(8,128)(2,1)S(1)}, bf16[256,2048]{1,0:T(8,128)(2,1)S(1)}, u32[]{:S(2)}, u32[]{:S(2)}) collective-permute-start(bf16[256,2048]{1,0:T(8,128)(2,1)S(1)} %copy-done.15), channel_id=1, source_target_pairs={{0,4},{2,6},{4,0},{6,2},{8,12},{10,14},{12,8},{14,10},{16,20},{18,... | collective-permute-start | bytes 3145736 | tf_op jit(solution)/shard_map/ppermute | solution.py:1095
  366.0 193.8 %reduce-scatter.6.cloned.1.call-start = ((), (), s32[]{:S(2)}) async-start(), calls=%async_computation.5 | async-start | bytes 3932160 | tf_op jit(solution)/shard_map/reduce_scatter | solution.py:1213
  383.8 26.0 %collective-permute-start.61 = (bf16[384,256]{1,0:T(8,128)(2,1)S(1)}, bf16[384,256]{1,0:T(8,128)(2,1)S(1)}, u32[]{:S(2)}, u32[]{:S(2)}) collective-permute-start(bf16[384,256]{1,0:T(8,128)(2,1)S(1)} %copy-done.81), channel_id=1, source_target_pairs={{0,16},{2,18},{4,20},{6,22},{8,24},{10,26},{12,28},{14,30},{16,0},... | collective-permute-start | bytes 589832 | tf_op jit(solution)/shard_map/ppermute | solution.py:1095
  384.2 25.7 %collective-permute-start.62 = (bf16[384,256]{1,0:T(8,128)(2,1)S(1)}, bf16[384,256]{1,0:T(8,128)(2,1)S(1)}, u32[]{:S(2)}, u32[]{:S(2)}) collective-permute-start(bf16[384,256]{1,0:T(8,128)(2,1)S(1)} %copy-done.80), channel_id=1, source_target_pairs={{0,8},{2,10},{4,12},{6,14},{8,16},{10,18},{12,20},{14,22},{16,24},... | collective-permute-start | bytes 589832 | tf_op jit(solution)/shard_map/ppermute | solution.py:1095
  389.4 20.4 %collective-permute-start.38 = (bf16[192,256]{1,0:T(8,128)(2,1)S(1)}, bf16[192,256]{1,0:T(8,128)(2,1)S(1)}, u32[]{:S(2)}, u32[]{:S(2)}) collective-permute-start(bf16[192,256]{1,0:T(8,128)(2,1)S(1)} %copy-done.83), channel_id=1, source_target_pairs={{0,16},{2,18},{4,20},{6,22},{8,24},{10,26},{12,28},{14,30},{16,0},... | collective-permute-start | bytes 294920 | tf_op jit(solution)/shard_map/ppermute | solution.py:1095
  389.5 20.3 %collective-permute-start.39 = (bf16[192,256]{1,0:T(8,128)(2,1)S(1)}, bf16[192,256]{1,0:T(8,128)(2,1)S(1)}, u32[]{:S(2)}, u32[]{:S(2)}) collective-permute-start(bf16[192,256]{1,0:T(8,128)(2,1)S(1)} %copy-done.82), channel_id=1, source_target_pairs={{0,8},{2,10},{4,12},{6,14},{8,16},{10,18},{12,20},{14,22},{16,24},... | collective-permute-start | bytes 294920 | tf_op jit(solution)/shard_map/ppermute | solution.py:1095
  415.1 20.7 %collective-permute-start.24 = (bf16[128,1536]{1,0:T(8,128)(2,1)S(1)}, bf16[128,1536]{1,0:T(8,128)(2,1)S(1)}, u32[]{:S(2)}, u32[]{:S(2)}) collective-permute-start(bf16[128,1536]{1,0:T(8,128)(2,1)S(1)} %copy-done.76), channel_id=1, source_target_pairs={{0,1},{1,0},{2,3},{3,2},{4,5},{5,4},{6,7},{7,6},{8,9},{9,8},{10,11... | collective-permute-start | bytes 1179656 | tf_op jit(solution)/shard_map/ppermute | solution.py:1092
  452.1 52.0 %collective-permute-start.79 = (bf16[1536,256]{1,0:T(8,128)(2,1)S(1)}, bf16[1536,256]{1,0:T(8,128)(2,1)S(1)}, u32[]{:S(2)}, u32[]{:S(2)}) collective-permute-start(bf16[1536,256]{1,0:T(8,128)(2,1)S(1)} %copy-done.3), channel_id=1, source_target_pairs={{0,4},{2,6},{4,0},{6,2},{8,12},{10,14},{12,8},{14,10},{16,20},{18,... | collective-permute-start | bytes 2359304 | tf_op jit(solution)/shard_map/ppermute | solution.py:1095
  454.6 20.6 %collective-permute-start.67 = (f32[48,768]{1,0:T(8,128)S(1)}, f32[48,768]{1,0:T(8,128)S(1)}, u32[]{:S(2)}, u32[]{:S(2)}) collective-permute-start(f32[48,768]{1,0:T(8,128)S(1)} %add.148), channel_id=1, source_target_pairs={{0,4},{2,6},{4,0},{6,2},{8,12},{10,14},{12,8},{14,10},{16,20},{18,... | collective-permute-start | bytes 442376 | tf_op jit(solution)/shard_map/ppermute | solution.py:1095
  456.1 28.0 %collective-permute-start.72 = (bf16[1,1,4,96,256]{4,3,2,1,0:T(8,128)(2,1)S(1)}, bf16[1,1,4,96,256]{4,3,2,1,0:T(8,128)(2,1)S(1)}, u32[]{:S(2)}, u32[]{:S(2)}) collective-permute-start(bf16[1,1,4,96,256]{4,3,2,1,0:T(8,128)(2,1)S(1)} %copy-done.78), channel_id=1, source_target_pairs={{0,2},{2,0},{4,6},{6,4},{8,10},{10,8},{12,14},{14,12},{16,18},{18,... | collective-permute-start | bytes 589832 | tf_op jit(solution)/shard_map/ppermute | solution.py:1095
  482.7 24.8 %collective-permute-start.73 = (bf16[2,1,4,96,256]{4,3,2,1,0:T(8,128)(2,1)}, bf16[2,1,4,96,256]{4,3,2,1,0:T(8,128)(2,1)S(1)}, u32[]{:S(2)}, u32[]{:S(2)}) collective-permute-start(bf16[2,1,4,96,256]{4,3,2,1,0:T(8,128)(2,1)} %get-tuple-element.239), channel_id=1, source_target_pairs={{0,4},{2,6},{4,0},{6,2},{8,12},{10,14},{12,8},{14,10},{16,20},{18,... | collective-permute-start | bytes 1179656 | tf_op jit(solution)/shard_map/ppermute | solution.py:1095
  484.1 23.6 %collective-permute-start.76 = (bf16[768,256]{1,0:T(8,128)(2,1)S(1)}, bf16[768,256]{1,0:T(8,128)(2,1)S(1)}, u32[]{:S(2)}, u32[]{:S(2)}) collective-permute-start(bf16[768,256]{1,0:T(8,128)(2,1)S(1)} %copy-done.10), channel_id=1, source_target_pairs={{0,4},{2,6},{4,0},{6,2},{8,12},{10,14},{12,8},{14,10},{16,20},{18,... | collective-permute-start | bytes 1179656 | tf_op jit(solution)/shard_map/ppermute | solution.py:1095
  532.3 20.4 %collective-permute-start.71 = (f32[4,1024]{1,0:T(4,128)S(1)}, f32[4,1024]{1,0:T(4,128)S(1)}, u32[]{:S(2)}, u32[]{:S(2)}) collective-permute-start(f32[4,1024]{1,0:T(4,128)S(1)} %fusion.9), channel_id=1, source_target_pairs={{0,1},{1,0},{2,3},{3,2},{4,5},{5,4},{6,7},{7,6},{8,9},{9,8},{10,11... | collective-permute-start | bytes 49160 | tf_op jit(solution)/shard_map/ppermute | solution.py:1092
  (157 other events, 1430.9 us)
Sparse Core Ops, SparseCore 0:
  42.0 91.9 all-gather.1
  260.3 35.2 reduce-scatter.7
  366.1 26.8 reduce-scatter.3
  415.2 57.3 reduce-scatter.5

commit v3 on v2

--- a/solution.py
+++ b/solution.py
@@ -27,6 +27,7 @@
 GROUP = 4
 LINE = 4
 BUCKET = ("z", "y", "c")
+SENDS = (1, 2, 3, 0)
 SMEM = pl.BlockSpec(memory_space=pltpu.SMEM)
 VMEM = pl.BlockSpec(memory_space=pltpu.VMEM)
 shape = jax.ShapeDtypeStruct
@@ -34,7 +35,7 @@
 
 def cost(microseconds):
     return pl.CostEstimate(
-        flops=0, transcendentals=0, bytes_accessed=int(microseconds * 3_000_000)
+        flops=0, transcendentals=0, bytes_accessed=int(microseconds * 20_000)
     )
 
 
@@ -228,7 +229,8 @@
     cap_ref, gains_ref, cos_ref, sin_ref = refs[LINE + GROUP : LINE + GROUP + 4]
     outs = refs[LINE + GROUP + 4 :]
     comb_refs = outs[:LINE]
-    own_ref, other_ref, stat_ref, qs_ref, ks_ref, vs_ref = outs[LINE:]
+    own_ref, other_ref, stat_ref, qs_ref, ks_ref, pair_ref = outs[LINE : LINE + 6]
+    value_ref, cap_value_ref, sum_ref = outs[LINE + 6 :]
     b, s = ids[0], ids[1]
     width, rows = q_refs[0].shape
     heads = width // HD
@@ -240,6 +242,7 @@
 
     key_gains = [gain_of(h, 1) for h in range(heads)]
     query_gains = [gain_of(h, 0) for h in range(heads)]
+    is_one = lax.broadcasted_iota(jnp.int32, (rows, 2 * HD), 1) < HD
     for j, kv_ref in enumerate(kv_refs):
         for k in range(LINE):
             slot = slot_of(b, k, j)
@@ -248,8 +251,18 @@
             for h in range(heads):
                 at = slice(h * HD, h * HD + HD)
                 raw = kv_ref[k, at, :].astype(F32)
-                ks_ref[slot, at, :] = norm_rope(raw, key_gains[h], cosine, sine).astype(BF)
-            vs_ref[slot] = kv_ref[k, width:, :]
+                keys = norm_rope(raw, key_gains[h], cosine, sine)
+                values = kv_ref[k, width + h * HD : width + h * HD + HD, :].astype(F32)
+                ks_ref[slot, at, :] = keys.astype(BF)
+                pair = jnp.concatenate([keys, values], axis=0).T
+                pair_ref[slot, h] = pair.astype(BF)
+                value_ref[slot, h] = jnp.where(is_one, 1.0, pair).astype(BF)
+    cap_one = is_one[:CAP]
+    for c in range(CLIPS):
+        for h in range(heads):
+            values = cap_ref[c, width + h * HD : width + h * HD + HD, :].astype(F32)
+            both = jnp.concatenate([values, values], axis=0).T
+            cap_value_ref[c, h] = jnp.where(cap_one, 1.0, both).astype(BF)
 
     for i in range(LINE):
         slot = slot_of(b, i, 0)
@@ -259,33 +272,29 @@
         for h in range(heads):
             at = slice(h * HD, h * HD + HD)
             raw = q_refs[i][at, :].astype(F32)
-            turned = norm_rope(raw, query_gains[h], cosine, sine).astype(BF)
-            turned = (turned.astype(F32) * scale).astype(BF)
-            qs_ref[i, at, :] = turned
-            queries.append(turned)
-
-        def step(n, state):
-            totals, sums = state
-            new_totals, new_sums = [], []
+            turned = norm_rope(raw, query_gains[h], cosine, sine).astype(BF).astype(F32) * scale
+            qs_ref[i, at, :] = turned.astype(BF)
+            queries.append(turned.T.astype(BF))
+        sum_ref[...] = jnp.zeros_like(sum_ref)
+
+        def step(n, carry):
             for h in range(heads):
                 at = slice(h * HD, h * HD + HD)
-                weights = jnp.exp(mm(ks_ref[n, at, :], queries[h], TN))
-                new_totals.append(totals[h] + jnp.sum(weights, axis=0, keepdims=True))
-                new_sums.append(sums[h] + mm(vs_ref[n, at, :], weights.astype(BF), NN))
-            return tuple(new_totals), tuple(new_sums)
-
-        zero_total = tuple(jnp.zeros((1, rows), F32) for _ in range(heads))
-        zero_sum = tuple(jnp.zeros((HD, rows), F32) for _ in range(heads))
-        totals, sums = lax.fori_loop(first, last, step, (zero_total, zero_sum))
-        usable = lax.broadcasted_iota(jnp.int32, (CAP, rows), 0) < lengths[clip]
+                weights = jnp.exp(mm(queries[h], ks_ref[n, at, :], NN))
+                sum_ref[h] += mm(weights.astype(BF), value_ref[n, h], NN)
+            return carry
+
+        lax.fori_loop(first, last, step, 0)
+        usable = lax.broadcasted_iota(jnp.int32, (rows, CAP), 1) < lengths[clip]
         for h in range(heads):
             at = slice(h * HD, h * HD + HD)
-            inverse = 1.0 / totals[h]
-            own = sums[h] * inverse
-            weights = jnp.where(usable, jnp.exp(mm(cap_ref[clip, at, :], queries[h], TN)), 0.0)
-            cap_inverse = 1.0 / jnp.sum(weights, axis=0, keepdims=True)
-            at_value = slice(width + h * HD, width + h * HD + HD)
-            other = mm(cap_ref[clip, at_value, :], weights.astype(BF), NN) * cap_inverse
+            total = sum_ref[h].T
+            inverse = 1.0 / total[0:1]
+            own = total[HD:] * inverse
+            weights = jnp.where(usable, jnp.exp(mm(queries[h], cap_ref[clip, at, :], NN)), 0.0)
+            cap_total = mm(weights.astype(BF), cap_value_ref[clip, h], NN).T
+            cap_inverse = 1.0 / cap_total[0:1]
+            other = cap_total[HD:] * cap_inverse
             own_ref[i, at, :] = own
             other_ref[i, at, :] = other
             gate = gates[(s * LINE + b // GROUP) * heads + h]
@@ -297,6 +306,7 @@
 def attend(ids, slices, lengths, gates, queries, kv_pieces, cap_kv, gains, cosine, sine):
     width, rows = queries[0].shape
     slots = LINE * GROUP
+    heads = width // HD
     outs = pl.pallas_call(
         attend_kernel,
         in_specs=[SMEM] * 4 + [VMEM] * (LINE + GROUP + 4),
@@ -308,7 +318,12 @@
             shape((LINE, 8, rows), F32),
             shape((LINE, width, rows), BF),
             shape((slots, width, rows), BF),
-            shape((slots, width, rows), BF),
+            shape((slots, heads, rows, 2 * HD), BF),
+        ],
+        scratch_shapes=[
+            pltpu.VMEM((slots, heads, rows, 2 * HD), BF),
+            pltpu.VMEM((CLIPS, heads, CAP, 2 * HD), BF),
+            pltpu.VMEM((heads, rows, 2 * HD), F32),
         ],
         name="attend",
         cost_estimate=cost(33),
@@ -386,13 +401,11 @@
     came_ref,
     down_ref,
     inner_ref,
-    gkept_ref,
-    gcame_ref,
+    grads_ref,
     in16_ref,
     mid_ref,
     near_ref,
     far_ref,
-    mean_ref,
     near_out_ref,
     far_out_ref,
     acc_in,
@@ -434,8 +447,8 @@
     grad_kept = jnp.where(s == 0, grad_gate, grad_up).astype(BF)
     grad_came = jnp.where(s == 0, grad_up, grad_gate).astype(BF)
     inner_ref[...] = inner
-    gkept_ref[...] = grad_kept
-    gcame_ref[...] = grad_came
+    grads_ref[0] = grad_kept
+    grads_ref[1] = grad_came
     acc_in[...] += mm(grad_kept, w_kept, NN) + mm(grad_came, w_came, NN)
     acc_out[...] += mm(inner, w_down, NN)
 
@@ -445,9 +458,15 @@
         part = jnp.sum(
             acc_in[...] * mlp_gain * (middle * row_inverse(middle)), axis=-1, keepdims=True
         )
-        mean_ref[...] = jnp.broadcast_to(part, (part.shape[0], 128)).T[:8]
-        near_ref[...] = acc_in[:, pl.ds(pl.multiple_of(s * half, half), half)]
-        far_ref[...] = acc_in[:, pl.ds(pl.multiple_of((1 - s) * half, half), half)].astype(BF)
+        near_ref[:, :half] = acc_in[:, pl.ds(pl.multiple_of(s * half, half), half)]
+        near_ref[:, half:] = jnp.broadcast_to(part, (part.shape[0], 128))
+        far_ref[:, :half] = acc_in[:, pl.ds(pl.multiple_of((1 - s) * half, half), half)].astype(BF)
+        high = part.astype(BF).astype(F32)
+        middle_part = (part - high).astype(BF).astype(F32)
+        low_part = part - high - middle_part
+        lane = lax.broadcasted_iota(jnp.int32, (part.shape[0], 128), 1)
+        spread = jnp.where(lane == 0, high, jnp.where(lane == 1, middle_part, jnp.where(lane == 2, low_part, 0.0)))
+        far_ref[:, half:] = spread.astype(BF)
         near_out_ref[...] = acc_out[pl.ds(pl.multiple_of(s * count, count), count), :]
         far_out_ref[...] = acc_out[pl.ds(pl.multiple_of((1 - s) * count, count), count), :].astype(BF)
 
@@ -476,25 +495,26 @@
                 pl.BlockSpec((tile, D), lambda i, ids: ((1 - ids[1]) * steps + i, 0)),
                 pl.BlockSpec((tile, D), lambda i, ids: (i, 0)),
             ],
-            out_specs=[pl.BlockSpec((rows, tile), lambda i, ids: (0, i))] * 3
+            out_specs=[
+                pl.BlockSpec((rows, tile), lambda i, ids: (0, i)),
+                pl.BlockSpec((2, rows, tile), lambda i, ids: (0, 0, i)),
+            ]
             + [
                 fixed(rows, D),
                 fixed(rows, D),
-                fixed(rows, half),
-                fixed(rows, half),
-                fixed(8, rows),
+                fixed(rows, half + 128),
+                fixed(rows, half + 128),
                 fixed(count, D),
                 fixed(count, D),
             ],
             scratch_shapes=[pltpu.VMEM((rows, D), F32), pltpu.VMEM((rows, D), F32)],
         ),
-        out_shape=[shape((rows, units), BF)] * 3
+        out_shape=[shape((rows, units), BF), shape((2, rows, units), BF)]
         + [
             shape((rows, D), BF),
             shape((rows, D), F32),
-            shape((rows, half), F32),
-            shape((rows, half), BF),
-            shape((8, rows), F32),
+            shape((rows, half + 128), F32),
+            shape((rows, half + 128), BF),
             shape((count, D), F32),
             shape((count, D), BF),
         ],
@@ -507,8 +527,6 @@
     ids,
     near_ref,
     recv_ref,
-    mean_a,
-    mean_b,
     mid_ref,
     cot_a,
     cot_b,
@@ -522,9 +540,9 @@
     far_mid_ref,
     *refs,
 ):
-    near_refs, far_refs, scratch = refs[:LINE], refs[LINE : 2 * LINE], refs[2 * LINE]
+    near_refs, far_refs, scratch = refs[:2], refs[2:4], refs[4]
     b, s = ids[0], ids[1]
-    half = near_ref.shape[1]
+    half = D // 2
     count = cot_a.shape[0]
     cols = pl.ds(pl.multiple_of(s * half, half), half)
     gate, scale2 = mod_ref[2:3, cols], mod_ref[4:5, cols]
@@ -532,9 +550,9 @@
     middle = mid_ref[...]
     inverse = row_inverse(middle)
     unit = mid_ref[:, cols] * inverse
-    means = (mean_a[...] + mean_b[...]) * (1.0 / D)
-    mean = jnp.concatenate([means] * 16, axis=0).T[:, 0:1]
-    grad_in = near_ref[...] + recv_ref[...].astype(F32)
+    parts = jnp.sum(recv_ref[:, half:].astype(F32), axis=-1, keepdims=True)
+    mean = (near_ref[:, half : half + 1] + parts) * (1.0 / D)
+    grad_in = near_ref[:, :half] + recv_ref[:, :half].astype(F32)
     cot_own, cot_far = cot_a[:, cols].astype(F32), cot_b[:, cols].astype(F32)
     cot = jnp.concatenate(
         [jnp.where(s == 0, cot_own, cot_far), jnp.where(s == 0, cot_far, cot_own)], axis=0
@@ -552,34 +570,56 @@
     near_mid_ref[...] = jnp.where(s == 0, top, low)
     far_mid_ref[...] = jnp.where(s == 0, low, top).astype(BF)
     scratch[...] = mm(grad_branch, w_ref[...], NN).T
-    width = near_refs[0].shape[0]
-    for k in range(LINE):
+    width = near_refs[0].shape[0] // 2
+    for n, k in enumerate(SENDS):
         at = chunk_at(b, k, width)
-        near_refs[k][...] = scratch[pl.ds(pl.multiple_of(s * half + at, HD), width), :]
-        far_refs[k][...] = scratch[pl.ds(pl.multiple_of((1 - s) * half + at, HD), width), :].astype(BF)
-
-
-def mid_back(ids, near, received, mean_a, mean_b, middle, cots, branch, mod, gain, w_out):
-    rows, half = near.shape
+        to = slice(n % 2 * width, n % 2 * width + width)
+        near_refs[n // 2][to, :] = scratch[pl.ds(pl.multiple_of(s * half + at, HD), width), :]
+        far_refs[n // 2][to, :] = scratch[
+            pl.ds(pl.multiple_of((1 - s) * half + at, HD), width), :
+        ].astype(BF)
+
+
+def mid_back(ids, near, received, middle, cots, branch, mod, gain, w_out):
+    rows, half = branch.shape
     width = half // LINE
     count = cots[0].shape[0]
     outs = pl.pallas_call(
         mid_kernel,
-        in_specs=[SMEM] + [VMEM] * 11,
-        out_specs=[VMEM] * (4 + 2 * LINE),
+        in_specs=[SMEM] + [VMEM] * 9,
+        out_specs=[VMEM] * 8,
         out_shape=[
             shape((8, half), F32),
             shape((rows, half), BF),
             shape((count, half), F32),
             shape((count, half), BF),
         ]
-        + [shape((width, rows), F32)] * LINE
-        + [shape((width, rows), BF)] * LINE,
+        + [shape((2 * width, rows), F32)] * 2
+        + [shape((2 * width, rows), BF)] * 2,
         scratch_shapes=[pltpu.VMEM((D, rows), F32)],
         name="mid_back",
         cost_estimate=cost(5.5),
-    )(ids, near, received, mean_a, mean_b, middle, *cots, branch, mod, gain, w_out)
-    return outs[:4], outs[4 : 4 + LINE], outs[4 + LINE :]
+    )(ids, near, received, middle, *cots, branch, mod, gain, w_out)
+    return outs[:4], outs[4:6], outs[6:]
+
+
+def add_pair_kernel(near_ref, recv_ref, a_ref, b_ref):
+    width = a_ref.shape[0]
+    total = (near_ref[...] + recv_ref[...].astype(F32)).astype(BF)
+    a_ref[...] = total[:width]
+    b_ref[...] = total[width:]
+
+
+def add_pair(near, received):
+    both, rows = near.shape
+    return pl.pallas_call(
+        add_pair_kernel,
+        in_specs=[VMEM, VMEM],
+        out_specs=[VMEM, VMEM],
+        out_shape=[shape((both // 2, rows), BF)] * 2,
+        name="add_pair",
+        cost_estimate=cost(1),
+    )(near, received)
 
 
 def place_row(b, column):
@@ -619,14 +659,14 @@
 
 def attend_back_kernel(ids, slices, lengths, gates, *refs):
     q_refs, g_refs = refs[:LINE], refs[LINE : 2 * LINE]
-    (own_ref, other_ref, stat_ref, qs_ref, ks_ref, vs_ref, cap_ref, gains_ref, cos_ref, sin_ref) = refs[
+    (own_ref, other_ref, stat_ref, qs_ref, ks_ref, pair_ref, cap_ref, gains_ref, cos_ref, sin_ref) = refs[
         2 * LINE : 2 * LINE + 10
     ]
     outs = refs[2 * LINE + 10 :]
     gq_refs = outs[:LINE]
     qgain_ref, keep_ref, send_ref, dgate_ref = outs[LINE : LINE + 4]
     dkv_refs = outs[LINE + 4 : LINE + 4 + GROUP]
-    acc_ref, dcap_ref = outs[LINE + 4 + GROUP :]
+    acc_ref, dcap_ref, dq_ref = outs[LINE + 4 + GROUP :]
     b, s = ids[0], ids[1]
     width, rows = q_refs[0].shape
     heads = width // HD
@@ -641,6 +681,7 @@
         slot = slot_of(b, i, 0)
         clip, first, last = clip_at(slices, slot)
         queries, grads, deltas, inverses = [], [], [], []
+        tall_q, tall_g, wide = [], [], []
         for h in range(heads):
             at = slice(h * HD, h * HD + HD)
             grad = g_refs[i][at, :]
@@ -648,24 +689,26 @@
             grads.append(grad)
             deltas.append(jnp.sum(grad.astype(F32) * own_ref[i, at, :], axis=0, keepdims=True))
             inverses.append(stat_ref[i, h : h + 1, :])
-
-        def step(n, state):
-            out = []
+            blank = jnp.zeros((HD, rows), F32)
+            query_pad = jnp.concatenate([queries[h].astype(F32), blank], axis=0)
+            grad_pad = jnp.concatenate([blank, grad.astype(F32)], axis=0)
+            tall_q.append(query_pad.astype(BF))
+            tall_g.append(grad_pad.astype(BF))
+            wide.append(jnp.concatenate([query_pad.T, grad_pad.T], axis=0).astype(BF))
+        dq_ref[...] = jnp.zeros_like(dq_ref)
+
+        def step(n, carry):
             for h in range(heads):
                 at = slice(h * HD, h * HD + HD)
-                at_value = slice(width + h * HD, width + h * HD + HD)
-                keys, values = ks_ref[n, at, :], vs_ref[n, at, :]
-                prob = jnp.exp(mm(keys, queries[h], TN)) * inverses[h]
-                grad_prob = mm(values, grads[h], TN)
-                grad_score = (prob * (grad_prob - deltas[h])).astype(BF)
-                acc_ref[n, at_value, :] += mm(grads[h], prob.astype(BF), NT)
-                acc_ref[n, at, :] += mm(queries[h], grad_score, NT)
-                out.append(state[h] + mm(keys, grad_score, NN))
-            return tuple(out)
-
-        query_grads = lax.fori_loop(
-            first, last, step, tuple(jnp.zeros((HD, rows), F32) for _ in range(heads))
-        )
+                pair = pair_ref[n, h]
+                prob = jnp.exp(mm(pair, tall_q[h], NN)) * inverses[h]
+                grad_score = (prob * (mm(pair, tall_g[h], NN) - deltas[h])).astype(BF)
+                both = jnp.concatenate([grad_score, prob.astype(BF)], axis=1)
+                acc_ref[n, h] += mm(both, wide[h], NN)
+                dq_ref[at, :] += mm(ks_ref[n, at, :], grad_score, NN)
+            return carry
+
+        lax.fori_loop(first, last, step, 0)
         usable = lax.broadcasted_iota(jnp.int32, (CAP, rows), 0) < lengths[clip]
         cosine, sine = cos_ref[slot - first], sin_ref[slot - first]
         for h in range(heads):
@@ -682,7 +725,7 @@
             grad_prob = mm(cap_values, grad_other, TN)
             inner = jnp.sum(prob * grad_prob, axis=0, keepdims=True)
             grad_score = (prob * (grad_prob - inner)).astype(BF)
-            query_grad = (query_grads[h] + mm(cap_keys, grad_score, NN)) * scale
+            query_grad = (dq_ref[at, :] + mm(cap_keys, grad_score, NN)) * scale
             dcap_ref[clip, at, :] += mm(queries[h], grad_score, NT)
             dcap_ref[clip, at_value, :] += mm(grad_other, prob.astype(BF), NT)
             part = jnp.sum(grad * other_ref[i, at, :], axis=0, keepdims=True)
@@ -696,7 +739,11 @@
 
     for j, dkv_ref in enumerate(dkv_refs):
         for k in range(LINE):
-            dkv_ref[k] = acc_ref[slot_of(b, k, j)].astype(BF)
+            slot = slot_of(b, k, j)
+            for h in range(heads):
+                both = acc_ref[slot, h].T.astype(BF)
+                dkv_ref[k, h * HD : h * HD + HD, :] = both[:HD]
+                dkv_ref[k, width + h * HD : width + h * HD + HD, :] = both[HD:]
     core = lax.rem(b, 2)
     for i in range(2):
         keep_ref[i] = dcap_ref[2 * i + core]
@@ -718,8 +765,9 @@
         ]
         + [shape((LINE, 2 * width, rows), BF)] * GROUP,
         scratch_shapes=[
-            pltpu.VMEM((LINE * GROUP, 2 * width, rows), F32),
+            pltpu.VMEM((LINE * GROUP, width // HD, rows, 2 * HD), F32),
             pltpu.VMEM((CLIPS, 2 * width, CAP), F32),
+            pltpu.VMEM((width, rows), F32),
         ],
         name="attend_back",
         cost_estimate=cost(40),
@@ -1024,22 +1072,27 @@
     left, right, out_ref = refs[:count], refs[count : 2 * count], refs[-1]
     total = None
     for a_ref, g_ref in zip(left, right):
-        part = mm(a_ref[0, 0].reshape(-1, a_ref.shape[-1]), g_ref[...], dims)
+        block = g_ref[...].reshape(g_ref.shape[-2:])
+        part = mm(a_ref[0, 0].reshape(-1, a_ref.shape[-1]), block, dims)
         total = part if total is None else total + part
     out_ref[...] = total.reshape(out_ref.shape).astype(BF)
 
 
 def weight_grads(left, right, by_rows, tile, kind, total, place, into=None):
     _, _, chunks, columns, tokens = left[0][0].shape
-    rows = right[0].shape[0 if by_rows else 1]
+    rows = right[0].shape[-2 if by_rows else -1]
+    stack = right[0].shape[0] if right[0].ndim == 3 else 1
+    per = rows // tile
     left_specs = [
         pl.BlockSpec((1, 1, chunks, columns, tokens), lambda i, n=n: (n, kind, 0, 0, 0))
         for _, n in left
     ]
     if by_rows:
         right_spec = pl.BlockSpec((tile, tokens), lambda i: (i, 0))
+    elif stack == 1:
+        right_spec = pl.BlockSpec((tokens, tile), lambda i: (0, i))
     else:
-        right_spec = pl.BlockSpec((tokens, tile), lambda i: (0, i))
+        right_spec = pl.BlockSpec((1, tokens, tile), lambda i: (i // per, 0, i % per))
     args = [a for a, _ in left] + list(right)
     specs = left_specs + [right_spec] * len(right)
     aliases = {}
@@ -1049,7 +1102,7 @@
         specs.append(pl.BlockSpec(memory_space=pl.ANY))
     return pl.pallas_call(
         functools.partial(weight_kernel, len(left), NT if by_rows else NN),
-        grid=(rows // tile,),
+        grid=(stack * per,),
         in_specs=specs,
         out_specs=pl.BlockSpec((chunks, columns, tile), lambda i: (0, 0, place(i))),
         out_shape=shape((chunks, columns, total), BF),
@@ -1106,6 +1159,9 @@
     def after(v, *others):
         return lax.optimization_barrier((v, *others))[0]
 
+    def fence(*values):
+        return lax.optimization_barrier(values)
+
     def pick(v, index):
         return lax.dynamic_index_in_dim(v, index, 0, False)
 
@@ -1137,19 +1193,23 @@
     )
     local = lax.slice_in_dim(projected, local_width, 2 * local_width, axis=0)
     swapped = xswap(local)
+    def scatter(parts):
+        return lax.psum_scatter(parts, "z", scatter_dimension=0, tiled=False)
+
     hid_own, hid_c, hid_y = cut(ids, [hidden], [False])
+    swapped, hid_own, hid_c, hid_y, gains = fence(swapped, hid_own, hid_c, hid_y, gains)
+    kv_parts, q_parts = route(ids, projected, swapped)
     came = lax.all_gather(after(sent, swapped), ("seq", "c"), axis=0, tiled=True)
-    swapped = after(swapped, hid_own)
-    kv_parts, q_parts = route(ids, projected, swapped)
     kv_here = spread(kv_parts)
     q_here = spread(q_parts)
     caption_rows = caption.reshape(CLIPS * CAP, YD)
     cap_raw, cap_kv = caption_keys(ids, w_caption, after(caption_rows, kv_parts[0]), gains)
-    kv_here[1] = after(kv_here[1], cap_kv, cosine, sine)
-    cot_far = xswap(after(cotangent, cap_kv))
+    cap_raw, cap_kv, cosine, sine, *kv_here = fence(cap_raw, cap_kv, cosine, sine, *kv_here)
     kv_own = jnp.stack(kv_here)
     kv_y = yswap(kv_own)
     kv_c = cswap(kv_own)
+    cot_far = xswap(after(cotangent, kv_own))
+    kv_y = after(kv_y, kv_c, *q_here[1:], cot_far)
     kv_cy = cswap(kv_y)
     kv_pieces = [kv_own, kv_c, kv_y, kv_cy]
     grad_mlp = (
@@ -1160,112 +1220,151 @@
         ).astype(F32)
         * mod[5:6]
     ).astype(BF)
-    q_here[0] = after(q_here[0], grad_mlp)
+    q_here[0], hid_y, hid_c = fence(q_here[0], hid_y, hid_c, grad_mlp)[:3]
+    hid_came_y, hid_came_c = yswap(hid_y), cswap(hid_c)
     combined, saved = attend(
         ids, clip_slices, caption_lengths, gates, q_here, kv_pieces, cap_kv, gains, cosine, sine
     )
+    combined, saved, hid_came_y, hid_came_c = fence(combined, saved, hid_came_y, hid_came_c)
     heads_own = unspread(combined)
     heads_far = [xswap(v) for v in heads_own]
     attention, branch = out_proj(ids, heads_own, heads_far, w_out)
     branch_far = xswap(branch)
     att_own, att_c, att_y = cut(ids, [attention, grad_mlp], [True, False])
-    branch_far = after(branch_far, att_own)
-    (
-        inner,
-        grad_kept,
-        grad_came,
-        mlp_in,
-        middle,
-        near,
-        far,
-        mean_near,
-        near_out,
-        far_out,
-    ) = ffn(ids, [tokens, tok_far], [branch, branch_far], grad_mlp, mod, ffn_row, w_gate_up, came, w_down)
+    branch_far, att_own, att_c, att_y = fence(branch_far, att_own, att_c, att_y)
+    att_came_y = yswap(att_y)
+    att_came_c = cswap(att_c)
+    hid_came_yc = cswap(after(hid_came_y, branch_far))
+    hid_left = [(hid_own, 0), (hid_came_c, 0), (hid_came_y, 0), (hid_came_yc, 1)]
+    inner, grads_in, mlp_in, middle, near, far, near_out, far_out = ffn(
+        ids, [tokens, tok_far], [branch, branch_far], grad_mlp, mod, ffn_row, w_gate_up, came, w_down
+    )
+    inner, grads_in, mlp_in, near, far, att_came_y, att_came_c, hid_came_yc = fence(
+        inner, grads_in, mlp_in, near, far, att_came_y, att_came_c, hid_came_yc
+    )
+    hid_left[3] = (hid_came_yc, 1)
+
     received = xswap(far)
-    mean_far = xswap(mean_near)
+    inner_y = yswap(inner)
+    inner_c = cswap(inner)
+    grads_c = cswap(grads_in)
+    att_came_yc = cswap(att_came_y)
+    att_left = [(att_own, 0), (att_came_c, 0), (att_came_y, 0), (att_came_yc, 1)]
     ffn_own, ffn_c, ffn_y = cut(ids, [mlp_in], [False])
-    received = after(received, ffn_own)
-
-    def left_of(own, c_part, y_part):
-        came_y = yswap(y_part)
-        return [(own, 0), (cswap(c_part), 0), (came_y, 0), (cswap(came_y), 1)]
-
-    def right_of(v):
-        far_v = yswap(v)
-        return [v, cswap(v), far_v, cswap(far_v)]
-
-    def line_sum(parts):
-        right_in = left_in = None
-        for t in range(1, LINE):
-            to_right = pick(parts, jnp.clip(LINE - t + z, 0, LINE - 1))
-            to_left = pick(parts, jnp.clip(t - LINE + z, 0, LINE - 1))
-            if t > 1:
-                to_right = (to_right.astype(F32) + right_in.astype(F32)).astype(BF)
-                to_left = (to_left.astype(F32) + left_in.astype(F32)).astype(BF)
-            ends = range(GROUP * t)
-            right_in = lax.ppermute(to_right, BUCKET, [(i, i + GROUP) for i in ends])
-            last = bucket_count - 1
-            left_in = lax.ppermute(to_left, BUCKET, [(last - i, last - i - GROUP) for i in ends])
-        return pick(parts, z).astype(F32) + right_in.astype(F32) + left_in.astype(F32)
-
-    def scatter(parts):
-        return lax.psum_scatter(parts, "z", scatter_dimension=0, tiled=False)
-
-    att_left = left_of(att_own, att_c, att_y)
-    inner_all = right_of(inner)
+    received, ffn_own, inner_c, grads_c, att_came_yc = fence(
+        received, ffn_own, inner_c, grads_c, att_came_yc
+    )
+    att_left[3] = (att_came_yc, 1)
+    (sums, grad_branch, mid_near, mid_far), near_heads, far_heads = mid_back(
+        ids, near, received, middle, [cotangent, cot_far], branch, mod, ffn_row, w_out
+    )
+    recv_a = xswap(far_heads[0])
+    recv_b = xswap(far_heads[1])
+    ffn_came_c = cswap(after(ffn_c, far_heads[0]))
+    branch_c = cswap(after(grad_branch, far_heads[0]))
+    recv_a, ffn_came_c, branch_c = fence(recv_a, ffn_came_c, branch_c)
+    grad_1, grad_2 = add_pair(near_heads[0], recv_a)
+    grad_3, grad_0 = add_pair(near_heads[1], after(recv_b, grad_1))
+    inner_y = after(inner_y, grad_0)
+    inner_yc = cswap(inner_y)
+    branch_y = yswap(after(grad_branch, inner_y))
+    ffn_came_y = yswap(after(ffn_y, inner_y))
+    inner_all = [inner, inner_c, inner_y, inner_yc]
     tile = 512
     per = units // tile
-    (sums, grad_branch, mid_near, mid_far), near_heads, far_heads = mid_back(
-        ids, near, received, mean_near, mean_far, middle, [cotangent, cot_far], branch, mod, ffn_row, w_out
-    )
-    grad_heads = [
-        (near_heads[k] + xswap(far_heads[k]).astype(F32)).astype(BF) for k in range(LINE)
-    ]
-    grad_here = spread(grad_heads)
-    parts_inner = weight_grads(att_left, inner_all, False, tile, 1, units, lambda i: i)
+    grad_here = spread([grad_0, grad_1, grad_2, grad_3])
+    total = units + local_width
+    parts_inner = weight_grads(att_left, inner_all, False, tile, 1, total, lambda i: i)
+    parts_inner, branch_y, ffn_came_y, *grad_here = fence(
+        parts_inner, branch_y, ffn_came_y, *grad_here
+    )
+    ffn_came_yc = cswap(ffn_came_y)
+    branch_all = [grad_branch, branch_c, branch_y, cswap(branch_y)]
+    step = 256
+    parts_inner = weight_grads(
+        att_left, branch_all, False, step, 0, total, lambda i: i + units // step, parts_inner
+    )
     sum_inner = scatter(parts_inner)
-    ffn_left = left_of(*[after(v, inner_all[2]) for v in (ffn_own, ffn_c, ffn_y)])
-    kept_all = right_of(after(grad_kept, inner_all[2]))
-    out_recv = xswap(after(far_out, grad_heads[0]))
-    output, early = output_sums(ids, clip_slices, near_out, out_recv, middle, cotangent, mod, sums)
-    grad_here[0] = after(grad_here[0], parts_inner)
+    ffn_left = [(ffn_own, 0), (ffn_came_c, 0), (ffn_came_y, 0), (ffn_came_yc, 1)]
+    grads_op, out_op, mid_op, grad_here[0], ffn_came_yc, _ = fence(
+        grads_in, far_out, mid_far, grad_here[0], ffn_came_yc, parts_inner
+    )
+    grads_y = yswap(grads_op)
+    out_recv = xswap(out_op)
+    mid_came = xswap(mid_op)
     grads_q, (q_gain_part, cap_keep, cap_send, gate_part), grads_kv = attend_back(
         ids, clip_slices, caption_lengths, gates, q_here, grad_here, saved, cap_kv, gains, cosine, sine
     )
-    came_all = right_of(after(grad_came, kept_all[2]))
-    here = (grads_kv[0].astype(F32) + cswap(grads_kv[1]).astype(F32)).astype(BF)
-    away = (grads_kv[2].astype(F32) + cswap(grads_kv[3]).astype(F32)).astype(BF)
+    grads_q, grads_kv, cap_send, grads_y, out_recv, mid_came = fence(
+        grads_q, grads_kv, cap_send, grads_y, out_recv, mid_came
+    )
+
+    kv_c3, grads_yc = cswap(grads_kv[3]), cswap(grads_y)
+    kv_c1, cap_c = cswap(grads_kv[1]), cswap(cap_send)
+    away = (grads_kv[2].astype(F32) + kv_c3.astype(F32)).astype(BF)
+    away, grads_yc, kv_c1, cap_c, *grads_q = fence(away, grads_yc, kv_c1, cap_c, *grads_q)
     away_here = yswap(away)
     back_q = unspread(grads_q)
-    pair = cap_keep + cswap(cap_send)
-    mid_came = xswap(after(mid_far, away))
-
-    kept_all[0] = after(kept_all[0], away)
-    parts_a = weight_grads(ffn_left, kept_all, False, tile, 0, 2 * units, lambda i: i)
-    parts_a = weight_grads(ffn_left, came_all, False, tile, 0, 2 * units, lambda i: i + per, parts_a)
-    sum_a = scatter(parts_a)
-    away_here = after(away_here, parts_a)
+    here = (grads_kv[0].astype(F32) + kv_c1.astype(F32)).astype(BF)
+    pair = cap_keep + cap_c
+    grads_all = [grads_in, grads_c, grads_y, grads_yc]
+    parts_a = weight_grads(ffn_left, grads_all, False, tile, 0, 2 * units, lambda i: i)
+    output, early = output_sums(ids, clip_slices, near_out, out_recv, middle, cotangent, mod, sums)
+    away_here, output, parts_a, here, pair, sum_inner, *back_q = fence(
+        away_here, output, parts_a, here, pair, sum_inner, *back_q
+    )
     back_kv, k_gain_part = keys_back(ids, clip_slices, here, away_here, kv_own, gains, cosine, sine)
-    back_kv = unspread(back_kv)
-    branch_all = right_of(after(grad_branch, away_here))
-    hid_left = left_of(hid_own, hid_c, hid_y)
-
-    cap_total = pick(pair, y) + yswap(after(pick(pair, 1 - y), away_here))
+    back_kv, k_gain_part = fence(back_kv, k_gain_part)
+    back_kv = fence(*unspread(back_kv))
+    sum_a = scatter(after(parts_a, *back_kv))
+
+    packed, send = pack(ids, back_q, back_kv)
+    packed, send = fence(packed, send)
+    packed_recv = xswap(send)
+    packed_y = yswap(packed)
+    packed_c = cswap(packed)
+    cap_y = yswap(after(pick(pair, 1 - y), packed))
+    cap_total = pick(pair, y) + cap_y
     raw_cap, cap_gain_part = caption_back(ids, cap_total, cap_raw, gains)
-    raw_y = yswap(raw_cap)
-    cap_parts = caption_weights(ids, [raw_cap, cswap(raw_cap), raw_y, cswap(raw_y)], caption_rows)
-    parts_out = weight_grads(att_left, branch_all, False, 384, 0, local_width, lambda i: i)
-    sum_out = scatter(parts_out)
-    back_kv[1] = after(back_kv[1], parts_out, cap_parts[0])
-
-    packed, send = pack(ids, back_q, back_kv)
-    packed_recv = xswap(send)
-    packed_all = right_of(packed)
-    recv_all = right_of(packed_recv)
-    cap_parts = unspread([after(v, packed) for v in cap_parts])
+    packed_recv, packed_c, raw_cap, cap_gain_part = fence(packed_recv, packed_c, raw_cap, cap_gain_part)
+    recv_y = yswap(packed_recv)
+    recv_c = cswap(packed_recv)
     tok_near, tok_send = qkv_back(ids, packed, packed_recv, w_qkv)
+    packed_y, recv_c, tok_near, tok_send, raw_cap = fence(
+        packed_y, recv_c, tok_near, tok_send, raw_cap
+    )
     tok_recv = xswap(tok_send)
+    raw_y, raw_c = yswap(raw_cap), cswap(raw_cap)
+    packed_all = [packed, packed_c, packed_y, cswap(packed_y)]
+    tile = 384
+    parts_c = weight_grads(
+        hid_left, packed_all, True, tile, 0, 3 * local_width, lambda i: jnp.where(i < 2, i, i + 2)
+    )
+    recv_y = after(recv_y, parts_c)
+    recv_all = [packed_recv, recv_c, recv_y, cswap(recv_y)]
+    parts_c = weight_grads(
+        hid_left, recv_all, True, tile, 0, 3 * local_width, lambda i: i + 2, parts_c
+    )
+    tok_recv, parts_c, raw_y, raw_c = fence(tok_recv, parts_c, raw_y, raw_c)
+
+    def line_first(parts):
+        to_right, to_left = pick(parts, LINE - 1), pick(parts, 0)
+        ends, last = range(GROUP), bucket_count - 1
+        right_in = lax.ppermute(to_right, BUCKET, [(i, i + GROUP) for i in ends])
+        left_in = lax.ppermute(to_left, BUCKET, [(last - i, last - i - GROUP) for i in ends])
+        return right_in, left_in
+
+    def line_next(parts, t, right_in, left_in):
+        to_right = pick(parts, jnp.clip(LINE - t + z, 0, LINE - 1))
+        to_left = pick(parts, jnp.clip(t - LINE + z, 0, LINE - 1))
+        to_right = (to_right.astype(F32) + right_in.astype(F32)).astype(BF)
+        to_left = (to_left.astype(F32) + left_in.astype(F32)).astype(BF)
+        ends, last = range(GROUP * t), bucket_count - 1
+        right_in = lax.ppermute(to_right, BUCKET, [(i, i + GROUP) for i in ends])
+        left_in = lax.ppermute(to_left, BUCKET, [(last - i, last - i - GROUP) for i in ends])
+        return right_in, left_in
+
+    line = line_first(parts_c)
     token_grad, late = tokens_back(
         ids,
         clip_slices,
@@ -1278,23 +1377,23 @@
         norm_row,
         [q_gain_part, k_gain_part, cap_gain_part, gate_part, early],
     )
-    tile = 384
-    parts_c = weight_grads(
-        hid_left, packed_all, True, tile, 0, 3 * local_width, lambda i: jnp.where(i < 2, i, i + 2)
-    )
-    parts_c = weight_grads(
-        hid_left, recv_all, True, tile, 0, 3 * local_width, lambda i: i + 2, parts_c
-    )
-    sum_c = line_sum(parts_c)
+    token_grad, late, *line = fence(token_grad, late, *line)
+    line = line_next(parts_c, 2, *line)
+    late = late + cswap(late)
+    late = late + yswap(late)
+    late = late + hop(late, lambda i: i ^ GROUP)
+    raw_yc = cswap(after(raw_y, late))
+    late, raw_yc, *line = fence(late, raw_yc, *line)
+    line = line_next(parts_c, 3, *line)
+    late = late + hop(late, lambda i: i ^ (2 * GROUP))
+    late_far = xswap(late)
+    late_far, sum_a, *line = fence(late_far, sum_a, *line)
+    sum_c = pick(parts_c, z).astype(F32) + line[0].astype(F32) + line[1].astype(F32)
+    cap_parts = caption_weights(ids, [after(raw_cap, late), raw_c, raw_y, raw_yc], caption_rows)
+    cap_parts = unspread(cap_parts)
     caption_w_grad = caption_join(ids, cap_parts)
-    def bucket_sum(v):
-        v = v + cswap(v)
-        v = v + yswap(v)
-        v = v + hop(v, lambda i: i ^ GROUP)
-        return v + hop(v, lambda i: i ^ (2 * GROUP))
-
-    late_sum = bucket_sum(late)
-    late_far = xswap(late_sum)
+    late_sum = late
+
     mod_grad, gain_rows = finish(ids, late_sum, late_far)
     mod_mine = mod_grad.astype(BF)
     cols_local = CD // bucket_count
@@ -1310,7 +1409,7 @@
         [gain_rows[5, :heads_each], gain_rows[5, local_width : local_width + heads_each]]
     )
 
-    down_out = sum_inner.astype(F32).T
+    down_out = sum_inner[:, :units].astype(F32).T
     kept_out = sum_a[:, :units].astype(F32)
     came_out = xswap(sum_a[:, units:]).astype(F32)
     gate_up_out = jnp.where(
@@ -1330,7 +1429,7 @@
         caption_w_grad,
         gain_rows[3],
         cross_out,
-        sum_out.astype(F32).T,
+        sum_inner[:, units:].astype(F32).T,
         gain_rows[4],
         gate_up_out,
         down_out,

time: 594 us -> 507 us (0.85)
  waiting for transfers between devices: 228 us -> 147 us
  Pallas kernels: 189 us -> 178 us
  starting transfers between devices: 92.8 us -> 99.6 us
    ppermute x63 -> x60, waiting for transfers between devices: 162 us -> 83.7 us  [hop(): return lax.ppermute(v, BUCKET, [(i, to(i)) for i in range(bucket_count)])]
    ppermute x6, waiting for transfers between devices: 23.5 us -> 7.1 us  [the longest x1 7.08 us: line_first(): right_in = lax.ppermute(to_right, BUCKET, [(i, i + GROUP) for i in ends])]
    ppermute x63 -> x60, starting transfers between devices: 49.5 us -> 64.2 us  [hop(): return lax.ppermute(v, BUCKET, [(i, to(i)) for i in range(bucket_count)])]
    ppermute x22 -> x19, waiting for transfers between devices: 42.8 us -> 55.7 us  [xswap(): return lax.ppermute(v, 'seq', [(0, 1), (1, 0)])]
    pallas_call x1, Pallas kernels: 34 us -> 23.8 us  [attend(): pl.pallas_call(attend_kernel, in_specs=[SMEM] * 4 + [VMEM] * (LINE + GROU...]
    ppermute x22 -> x19, starting transfers between devices: 28.6 us -> 25.2 us  [xswap(): return lax.ppermute(v, 'seq', [(0, 1), (1, 0)])]
    unnamed x172 -> x170, local copies, waits for them, and re-layouts: 11.9 us -> 14.7 us
    pallas_call x6 -> x5, Pallas kernels: 29.1 us -> 28.1 us  [weight_grads(): pl.pallas_call(functools.partial(weight_kernel, len(left), NT if by_rows...]
  transfers between devices with their start and end apart: 95 -> 88, of which waited for: 36 -> 37; matrix products, arithmetic and copies ran while one was open for 8% -> 7% of each run, Pallas kernels for 28% -> 33%
where the time goes in v3:
time: 507 us; the launch traced here: 498 us
  Pallas kernels  178 us (35%)
  waiting for transfers between devices  147 us (29%)
  starting transfers between devices  99.6 us (20%)
  local copies, waits for them, and re-layouts  25.1 us (5%)
  other arithmetic  19.8 us (4%)
  between operations  15.2 us (3%)
  matrix products  12.7 us (3%)
    ppermute x60, waiting for transfers between devices, hop(): return lax.ppermute(v, BUCKET, [(i, to(i)) for i in range(bucket_count)])  83.7 us
    ppermute x60, starting transfers between devices, hop(): return lax.ppermute(v, BUCKET, [(i, to(i)) for i in range(bucket_count)])  64.2 us
    ppermute x19, waiting for transfers between devices, xswap(): return lax.ppermute(v, 'seq', [(0, 1), (1, 0)])  55.7 us
    pallas_call x1, Pallas kernels, attend_back(): pl.pallas_call(attend_back_kernel, in_specs=[SMEM] * 4 + [VMEM] * (2 * LI...  36.7 us
    pallas_call x5, Pallas kernels, weight_grads(): pl.pallas_call(functools.partial(weight_kernel, len(left), NT if by_rows...  28.1 us
    ppermute x19, starting transfers between devices, xswap(): return lax.ppermute(v, 'seq', [(0, 1), (1, 0)])  25.2 us
    pallas_call x1, Pallas kernels, attend(): pl.pallas_call(attend_kernel, in_specs=[SMEM] * 4 + [VMEM] * (LINE + GROU...  23.8 us
    pallas_call x1, Pallas kernels, ffn(): pl.pallas_call(ffn_kernel, grid_spec=pltpu.PrefetchScalarGridSpec(num_sca...  19.9 us
  transfers between devices with their start and end apart: 88, of which 37 were waited for; matrix products, arithmetic and copies ran while one was open for 7% of the time, Pallas kernels for 33%

profile of v3, /device:TPU:0, one launch (start us, length us, event | category | flops | bytes accessed | tf_op | source)
XLA Modules:
  0.0 497.5 jit_solution(17842202231221993228)
XLA Ops:
  11.0 6.2 %fusion.11.mod_a = f32[4,4608]{1,0:T(4,128)S(1)} fusion(bf16[4,1024]{1,0:T(4,128)(2,1)S(1)} %multiply_convert_fusion.1, bf16[4608,1024]{1,0:T(8,128)(2,1)} %param.24), kind=kOutput, calls=%fused_computation.49 | convolution fusion | flops 37748736 | bytes 9519104 | tf_op jit(solution)/shard_map/dot_general | solution.py:43
  23.6 6.6 %pre.1 = (bf16[2304,256]{1,0:T(8,128)(2,1)}, bf16[256,1536]{1,0:T(8,128)(2,1)}, f32[8,1536]{1,0:T(8,128)}) custom-call(s32[2]{0:T(128)} %pad_add_fusion.ids, s32[4]{0:T(128)} %slices.11, bf16[128,1536]{1,0:T(8,128)(2,1)} %tok_ref.1, bf16[128,1536]{1,0:T(8,128)(2,1)} %copy-done.7, f32[4,4608]{1,0:T(4,128)} %copy-done.45, f32[4,4608]{1,0:T(4,128)} %copy-done.74, ...), custom_call_target="tpu_custom_call" | custom-call | bytes 120000 | tf_op jit(solution)/shard_map/pre/pallas_call | solution.py:123
  35.7 6.1 %collective-permute-done.2.r_ref = bf16[768,256]{1,0:T(8,128)(2,1)S(1)} collective-permute-done((bf16[768,256]{1,0:T(8,128)(2,1)S(1)}, bf16[768,256]{1,0:T(8,128)(2,1)S(1)}, u32[]{:S(2)}, u32[]{:S(2)}) %collective-permute-start.2) | collective-permute-done | bytes 393248 | tf_op jit(solution)/shard_map/ppermute | solution.py:1145
  54.8 8.8 %caption_keys.1 = (f32[384,512]{1,0:T(8,128)}, bf16[4,384,128]{2,1,0:T(8,128)(2,1)}) custom-call(s32[2]{0:T(128)} %pad_add_fusion.ids, bf16[2,768,4096]{2,1,0:T(8,128)(2,1)} %w_ref.5, bf16[512,4096]{1,0:T(8,128)(2,1)} %bitcast.47, f32[1536,3]{1,0:T(8,128)} %copy.38.gains_ref.refs_9_.refs_15_), custom_call_target="tpu_custom_call" | custom-call | bytes 160000 | tf_op jit(solution)/shard_map/caption_keys/pallas_call | solution.py:205
  79.6 6.0 %collective-permute-done.6.cot_b = bf16[128,1536]{1,0:T(8,128)(2,1)S(1)} collective-permute-done((bf16[128,1536]{1,0:T(8,128)(2,1)S(1)}, bf16[128,1536]{1,0:T(8,128)(2,1)S(1)}, u32[]{:S(2)}, u32[]{:S(2)}) %collective-permute-start.6) | collective-permute-done | bytes 393248 | tf_op jit(solution)/shard_map/ppermute | solution.py:1145
  88.2 23.8 %attend.1 = (bf16[192,256]{1,0:T(8,128)(2,1)}, bf16[192,256]{1,0:T(8,128)(2,1)}, bf16[192,256]{1,0:T(8,128)(2,1)}, bf16[192,256]{1,0:T(8,128)(2,1)}, f32[4,192,2...) custom-call(s32[2]{0:T(128)} %pad_add_fusion.ids, ...), custom_call_target="tpu_custom_call" | custom-call | bytes 660000 | tf_op jit(solution)/shard_map/attend/pallas_call | solution.py:310
  127.8 5.6 %collective-permute-done.20.refs_6_ = bf16[192,256]{1,0:T(8,128)(2,1)S(1)} collective-permute-done((bf16[192,256]{1,0:T(8,128)(2,1)S(1)}, bf16[192,256]{1,0:T(8,128)(2,1)S(1)}, u32[]{:S(2)}, u32[]{:S(2)}) %collective-permute-start.20) | collective-permute-done | bytes 98336 | tf_op jit(solution)/shard_map/ppermute | solution.py:1145
  146.0 6.1 %collective-permute-done.22.br_b = bf16[256,768]{1,0:T(8,128)(2,1)S(1)} collective-permute-done((bf16[256,768]{1,0:T(8,128)(2,1)}, bf16[256,768]{1,0:T(8,128)(2,1)S(1)}, u32[]{:S(2)}, u32[]{:S(2)}) %collective-permute-start.22) | collective-permute-done | bytes 393248 | tf_op jit(solution)/shard_map/ppermute | solution.py:1145
  153.3 19.9 %ffn.1 = (bf16[256,2048]{1,0:T(8,128)(2,1)}, bf16[2,256,2048]{2,1,0:T(8,128)(2,1)}, bf16[256,1536]{1,0:T(8,128)(2,1)}, f32[256,1536]{1,0:T(8,128)}, f32[256,896]...) custom-call(s32[2]{0:T(128)} %pad_add_fusion.ids, ...), custom_call_target="tpu_custom_call" | custom-call | bytes 360000 | tf_op jit(solution)/shard_map/ffn/pallas_call | solution.py:487
  180.0 8.8 %collective-permute-done.26.recv_ref = bf16[256,896]{1,0:T(8,128)(2,1)S(1)} collective-permute-done((bf16[256,896]{1,0:T(8,128)(2,1)}, bf16[256,896]{1,0:T(8,128)(2,1)S(1)}, u32[]{:S(2)}, u32[]{:S(2)}) %collective-permute-start.26) | collective-permute-done | bytes 458784 | tf_op jit(solution)/shard_map/ppermute | solution.py:1145
  189.6 5.6 %mid_back.1 = (f32[8,768]{1,0:T(8,128)}, bf16[256,768]{1,0:T(8,128)(2,1)}, f32[128,768]{1,0:T(8,128)}, bf16[128,768]{1,0:T(8,128)(2,1)}, f32[384,256]{1,0:T(8,12...) custom-call(s32[2]{0:T(128)} %pad_add_fusion.ids, ...), custom_call_target="tpu_custom_call" | custom-call | bytes 110000 | tf_op jit(solution)/shard_map/mid_back/pallas_call | solution.py:587
  197.6 5.7 %collective-permute-done.32.recv_ref = bf16[384,256]{1,0:T(8,128)(2,1)S(1)} collective-permute-done((bf16[384,256]{1,0:T(8,128)(2,1)}, bf16[384,256]{1,0:T(8,128)(2,1)S(1)}, u32[]{:S(2)}, u32[]{:S(2)}) %collective-permute-start.32) | collective-permute-done | bytes 196640 | tf_op jit(solution)/shard_map/ppermute | solution.py:1145
  216.0 5.5 %weight_grads.5.refs_8_ = bf16[4,96,2816]{2,1,0:T(8,128)(2,1)} custom-call(bf16[1,2,4,96,256]{4,3,2,1,0:T(8,128)(2,1)} %get-tuple-element.314.refs_0_, bf16[1,2,4,96,256]{4,3,2,1,0:T(8,128)(2,1)} %copy-done.8, bf16[2,2,4,96,256]{4,3,2,1,0:T(8,128)(2,1)} %copy-done.3, bf16[2,2,4,96,256]{4,3,2,1,0:T(8,128)(2,1)} %copy-done.4, ...), custom_call_target="tpu_custom_call" | custom-call | bytes 100000 | tf_op jit(solution)/shard_map/weight_grads/pallas_call | solution.py:1103
  222.5 7.2 %collective-permute-done.37.refs_2_ = bf16[2,1,4,96,256]{4,3,2,1,0:T(8,128)(2,1)S(1)} collective-permute-done((bf16[2,1,4,96,256]{4,3,2,1,0:T(8,128)(2,1)}, bf16[2,1,4,96,256]{4,3,2,1,0:T(8,128)(2,1)S(1)}, u32[]{:S(2)}, u32[]{:S(2)}) %collective-permute-start.37) | collective-permute-done | bytes 393248 | tf_op jit(solution)/shard_map/ppermute | solution.py:1148
  239.7 36.7 %attend_back.1 = (bf16[192,256]{1,0:T(8,128)(2,1)}, bf16[192,256]{1,0:T(8,128)(2,1)}, bf16[192,256]{1,0:T(8,128)(2,1)}, bf16[192,256]{1,0:T(8,128)(2,1)}, f32[19...) custom-call(s32[2]{0:T(128)} %pad_add_fusion.ids, ...), custom_call_target="tpu_custom_call" | custom-call | bytes 800000 | tf_op jit(solution)/shard_map/attend_back/pallas_call | solution.py:755
  276.4 8.0 %collective-permute-done.43.refs_6_ = bf16[2,256,2048]{2,1,0:T(8,128)(2,1)} collective-permute-done((bf16[2,256,2048]{2,1,0:T(8,128)(2,1)S(1)}, bf16[2,256,2048]{2,1,0:T(8,128)(2,1)}, u32[]{:S(2)}, u32[]{:S(2)}) %collective-permute-start.43) | collective-permute-done | bytes 2097184 | tf_op jit(solution)/shard_map/ppermute | solution.py:1148
  302.4 9.5 %weight_grads.7 = bf16[4,96,4096]{2,1,0:T(8,128)(2,1)} custom-call(bf16[1,1,4,96,256]{4,3,2,1,0:T(8,128)(2,1)} %get-tuple-element.377.refs_0_, bf16[1,1,4,96,256]{4,3,2,1,0:T(8,128)(2,1)} %copy-done.56, bf16[2,1,4,96,256]{4,3,2,1,0:T(8,128)(2,1)} %copy-done.30, bf16[2,1,4,96,256]{4,3,2,1,0:T(8,128)(2,1)} %copy-done.31, ...), custom_call_target="tpu_custom_call" | custom-call | bytes 100000 | tf_op jit(solution)/shard_map/weight_grads/pallas_call | solution.py:1103
  325.7 11.9 %collective-permute-done.55.refs_6_ = bf16[384,256]{1,0:T(8,128)(2,1)S(1)} collective-permute-done((bf16[384,256]{1,0:T(8,128)(2,1)}, bf16[384,256]{1,0:T(8,128)(2,1)S(1)}, u32[]{:S(2)}, u32[]{:S(2)}) %collective-permute-start.55) | collective-permute-done | bytes 196640 | tf_op jit(solution)/shard_map/ppermute | solution.py:1148
  354.4 7.3 %qkv_back.1 = (f32[128,1536]{1,0:T(8,128)}, bf16[128,1536]{1,0:T(8,128)(2,1)}) custom-call(s32[2]{0:T(128)} %pad_add_fusion.ids, bf16[1536,256]{1,0:T(8,128)(2,1)} %get-tuple-element.404.own_ref.refs_4_, bf16[768,256]{1,0:T(8,128)(2,1)} %copy-done.9, bf16[2304,1536]{1,0:T(8,128)(2,1)} %w_ref.7), custom_call_target="tpu_custom_call" | custom-call | bytes 120000 | tf_op jit(solution)/shard_map/qkv_back/pallas_call | solution.py:876
  368.6 5.5 %weight_grads.8.refs_8_ = bf16[4,96,2304]{2,1,0:T(8,128)(2,1)} custom-call(bf16[1,1,4,96,256]{4,3,2,1,0:T(8,128)(2,1)} %get-tuple-element.417.refs_0_, bf16[1,1,4,96,256]{4,3,2,1,0:T(8,128)(2,1)} %copy-done.14, bf16[2,1,4,96,256]{4,3,2,1,0:T(8,128)(2,1)} %copy-done.10, bf16[2,1,4,96,256]{4,3,2,1,0:T(8,128)(2,1)} %copy-done.11, ...), custom_call_target="tpu_custom_call" | custom-call | bytes 100000 | tf_op jit(solution)/shard_map/weight_grads/pallas_call | solution.py:1103
  395.9 7.1 %collective-permute-done.68 = bf16[96,2304]{1,0:T(8,128)(2,1)S(1)} collective-permute-done((bf16[96,2304]{1,0:T(8,128)(2,1)S(1)}, bf16[96,2304]{1,0:T(8,128)(2,1)S(1)}, u32[]{:S(2)}, u32[]{:S(2)}) %collective-permute-start.68) | collective-permute-done | bytes 442400 | tf_op jit(solution)/shard_map/ppermute | solution.py:1353
  425.5 5.6 %collective-permute-start.76 = (f32[48,768]{1,0:T(8,128)S(1)}, f32[48,768]{1,0:T(8,128)S(1)}, u32[]{:S(2)}, u32[]{:S(2)}) collective-permute-start(f32[48,768]{1,0:T(8,128)S(1)} %add.130), channel_id=1, source_target_pairs={{0,16},{2,18},{4,20},{6,22},{8,24},{10,26},{12,28},{14,30},{16,0},... | collective-permute-start | bytes 442376 | tf_op jit(solution)/shard_map/ppermute | solution.py:1148
  451.9 10.5 %collective-permute-start.83 = (bf16[384,256]{1,0:T(8,128)(2,1)}, bf16[384,256]{1,0:T(8,128)(2,1)S(1)}, u32[]{:S(2)}, u32[]{:S(2)}) collective-permute-start(bf16[384,256]{1,0:T(8,128)(2,1)} %get-tuple-element.458), channel_id=1, source_target_pairs={{0,8},{2,10},{4,12},{6,14},{8,16},{10,18},{12,20},{14,22},{16,24},... | collective-permute-start | bytes 589832 | tf_op jit(solution)/shard_map/ppermute | solution.py:1148
  483.2 5.9 %collective-permute-done.84 = bf16[96,2048]{1,0:T(8,128)(2,1)S(1)} collective-permute-done((bf16[96,2048]{1,0:T(8,128)(2,1)S(1)}, bf16[96,2048]{1,0:T(8,128)(2,1)S(1)}, u32[]{:S(2)}, u32[]{:S(2)}) %collective-permute-start.84) | collective-permute-done | bytes 393248 | tf_op jit(solution)/shard_map/ppermute | solution.py:1145
  (395 shorter events, 252.1 us)
Async XLA Ops:
  7.2 146.1 %all-gather.2.cloned.1.call-start = ((), (), s32[]{:S(2)}) async-start(), calls=%async_computation.2 | async-start | bytes 15728640 | tf_op jit(solution)/shard_map/all_gather | solution.py:1202
  41.9 270.1 %reduce-scatter.3.cloned.1.call-start = ((), (), s32[]{:S(2)}) async-start(), calls=%async_computation.3 | async-start | bytes 2703360 | tf_op jit(solution)/shard_map/reduce_scatter | solution.py:1197
  45.1 18.5 %collective-permute-start.3 = (bf16[384,256]{1,0:T(8,128)(2,1)}, bf16[384,256]{1,0:T(8,128)(2,1)S(1)}, u32[]{:S(2)}, u32[]{:S(2)}) collective-permute-start(bf16[384,256]{1,0:T(8,128)(2,1)} %get-tuple-element.253), channel_id=1, source_target_pairs={{0,8},{2,10},{4,12},{6,14},{8,16},{10,18},{12,20},{14,22},{16,24},... | collective-permute-start | bytes 589832 | tf_op jit(solution)/shard_map/ppermute | solution.py:1148
  63.8 21.9 %collective-permute-start.10 = (bf16[4,384,256]{2,1,0:T(8,128)(2,1)S(1)}, bf16[4,384,256]{2,1,0:T(8,128)(2,1)S(1)}, u32[]{:S(2)}, u32[]{:S(2)}) collective-permute-start(bf16[4,384,256]{2,1,0:T(8,128)(2,1)S(1)} %pad_maximum_fusion.refs_4_.kv_ref), channel_id=1, source_target_pairs={{0,2},{2,0},{4,6},{6,4},{8,10},{10,8},{12,14},{14,12},{16,18},{18,... | collective-permute-start | bytes 2359304 | tf_op jit(solution)/shard_map/ppermute | solution.py:1148
  63.8 21.8 %collective-permute-start.11 = (bf16[4,384,256]{2,1,0:T(8,128)(2,1)S(1)}, bf16[4,384,256]{2,1,0:T(8,128)(2,1)S(1)}, u32[]{:S(2)}, u32[]{:S(2)}) collective-permute-start(bf16[4,384,256]{2,1,0:T(8,128)(2,1)S(1)} %pad_maximum_fusion.refs_4_.kv_ref), channel_id=1, source_target_pairs={{0,4},{2,6},{4,0},{6,2},{8,12},{10,14},{12,8},{14,10},{16,20},{18,... | collective-permute-start | bytes 2359304 | tf_op jit(solution)/shard_map/ppermute | solution.py:1148
  65.5 20.1 %collective-permute-start.6 = (bf16[128,1536]{1,0:T(8,128)(2,1)S(1)}, bf16[128,1536]{1,0:T(8,128)(2,1)S(1)}, u32[]{:S(2)}, u32[]{:S(2)}) collective-permute-start(bf16[128,1536]{1,0:T(8,128)(2,1)S(1)} %copy-done.2), channel_id=1, source_target_pairs={{0,1},{1,0},{2,3},{3,2},{4,5},{5,4},{6,7},{7,6},{8,9},{9,8},{10,11... | collective-permute-start | bytes 1179656 | tf_op jit(solution)/shard_map/ppermute | solution.py:1145
  87.3 24.8 %collective-permute-start.13 = (bf16[2,1,4,96,256]{4,3,2,1,0:T(8,128)(2,1)}, bf16[2,1,4,96,256]{4,3,2,1,0:T(8,128)(2,1)S(1)}, u32[]{:S(2)}, u32[]{:S(2)}) collective-permute-start(bf16[2,1,4,96,256]{4,3,2,1,0:T(8,128)(2,1)} %get-tuple-element.280), channel_id=1, source_target_pairs={{0,4},{2,6},{4,0},{6,2},{8,12},{10,14},{12,8},{14,10},{16,20},{18,... | collective-permute-start | bytes 1179656 | tf_op jit(solution)/shard_map/ppermute | solution.py:1148
  87.6 24.4 %collective-permute-start.14 = (bf16[1,1,4,96,256]{4,3,2,1,0:T(8,128)(2,1)}, bf16[1,1,4,96,256]{4,3,2,1,0:T(8,128)(2,1)S(1)}, u32[]{:S(2)}, u32[]{:S(2)}) collective-permute-start(bf16[1,1,4,96,256]{4,3,2,1,0:T(8,128)(2,1)} %get-tuple-element.281), channel_id=1, source_target_pairs={{0,2},{2,0},{4,6},{6,4},{8,10},{10,8},{12,14},{14,12},{16,18},{18,... | collective-permute-start | bytes 589832 | tf_op jit(solution)/shard_map/ppermute | solution.py:1148
  152.2 21.1 %collective-permute-start.23 = (bf16[2,2,4,96,256]{4,3,2,1,0:T(8,128)(2,1)}, bf16[2,2,4,96,256]{4,3,2,1,0:T(8,128)(2,1)S(1)}, u32[]{:S(2)}, u32[]{:S(2)}) collective-permute-start(bf16[2,2,4,96,256]{4,3,2,1,0:T(8,128)(2,1)} %get-tuple-element.299), channel_id=1, source_target_pairs={{0,4},{2,6},{4,0},{6,2},{8,12},{10,14},{12,8},{14,10},{16,20},{18,... | collective-permute-start | bytes 2359304 | tf_op jit(solution)/shard_map/ppermute | solution.py:1148
  152.2 21.1 %collective-permute-start.24 = (bf16[1,2,4,96,256]{4,3,2,1,0:T(8,128)(2,1)}, bf16[1,2,4,96,256]{4,3,2,1,0:T(8,128)(2,1)S(1)}, u32[]{:S(2)}, u32[]{:S(2)}) collective-permute-start(bf16[1,2,4,96,256]{4,3,2,1,0:T(8,128)(2,1)} %get-tuple-element.300), channel_id=1, source_target_pairs={{0,2},{2,0},{4,6},{6,4},{8,10},{10,8},{12,14},{14,12},{16,18},{18,... | collective-permute-start | bytes 1179656 | tf_op jit(solution)/shard_map/ppermute | solution.py:1148
  152.2 21.1 %collective-permute-start.25 = (bf16[2,1,4,96,256]{4,3,2,1,0:T(8,128)(2,1)S(1)}, bf16[2,1,4,96,256]{4,3,2,1,0:T(8,128)(2,1)S(1)}, u32[]{:S(2)}, u32[]{:S(2)}) collective-permute-start(bf16[2,1,4,96,256]{4,3,2,1,0:T(8,128)(2,1)S(1)} %collective-permute-done.13.refs_2_), channel_id=1, source_target_pairs={{0,2},{2,0},{4,6},{6,4},{8,10},{10,8},{12,14},{14,12},{16,18},{18,... | collective-permute-start | bytes 1179656 | tf_op jit(solution)/shard_map/ppermute | solution.py:1148
  174.0 35.6 %collective-permute-start.30 = (bf16[256,2048]{1,0:T(8,128)(2,1)}, bf16[256,2048]{1,0:T(8,128)(2,1)}, u32[]{:S(2)}, u32[]{:S(2)}) collective-permute-start(bf16[256,2048]{1,0:T(8,128)(2,1)} %get-tuple-element.309.refs_4_), channel_id=1, source_target_pairs={{0,4},{2,6},{4,0},{6,2},{8,12},{10,14},{12,8},{14,10},{16,20},{18,... | collective-permute-start | bytes 3145736 | tf_op jit(solution)/shard_map/ppermute | solution.py:1148
  209.9 19.8 %collective-permute-start.37 = (bf16[2,1,4,96,256]{4,3,2,1,0:T(8,128)(2,1)}, bf16[2,1,4,96,256]{4,3,2,1,0:T(8,128)(2,1)S(1)}, u32[]{:S(2)}, u32[]{:S(2)}) collective-permute-start(bf16[2,1,4,96,256]{4,3,2,1,0:T(8,128)(2,1)} %get-tuple-element.333), channel_id=1, source_target_pairs={{0,4},{2,6},{4,0},{6,2},{8,12},{10,14},{12,8},{14,10},{16,20},{18,... | collective-permute-start | bytes 1179656 | tf_op jit(solution)/shard_map/ppermute | solution.py:1148
  236.6 47.8 %collective-permute-start.43 = (bf16[2,256,2048]{2,1,0:T(8,128)(2,1)S(1)}, bf16[2,256,2048]{2,1,0:T(8,128)(2,1)}, u32[]{:S(2)}, u32[]{:S(2)}) collective-permute-start(bf16[2,256,2048]{2,1,0:T(8,128)(2,1)S(1)} %copy-done.5), channel_id=1, source_target_pairs={{0,4},{2,6},{4,0},{6,2},{8,12},{10,14},{12,8},{14,10},{16,20},{18,... | collective-permute-start | bytes 6291464 | tf_op jit(solution)/shard_map/ppermute | solution.py:1148
  236.9 232.2 %reduce-scatter.5.cloned.1.call-start = ((), (), s32[]{:S(2)}) async-start(), calls=%async_computation.4 | async-start | bytes 3932160 | tf_op jit(solution)/shard_map/reduce_scatter | solution.py:1197
  237.7 38.7 %collective-permute-start.44 = (bf16[128,1536]{1,0:T(8,128)(2,1)S(1)}, bf16[128,1536]{1,0:T(8,128)(2,1)S(1)}, u32[]{:S(2)}, u32[]{:S(2)}) collective-permute-start(bf16[128,1536]{1,0:T(8,128)(2,1)S(1)} %copy-done.82), channel_id=1, source_target_pairs={{0,1},{1,0},{2,3},{3,2},{4,5},{5,4},{6,7},{7,6},{8,9},{9,8},{10,11... | collective-permute-start | bytes 1179656 | tf_op jit(solution)/shard_map/ppermute | solution.py:1145
  239.3 37.1 %collective-permute-start.45 = (bf16[128,768]{1,0:T(8,128)(2,1)}, bf16[128,768]{1,0:T(8,128)(2,1)S(1)}, u32[]{:S(2)}, u32[]{:S(2)}) collective-permute-start(bf16[128,768]{1,0:T(8,128)(2,1)} %get-tuple-element.362), channel_id=1, source_target_pairs={{0,1},{1,0},{2,3},{3,2},{4,5},{5,4},{6,7},{7,6},{8,9},{9,8},{10,11... | collective-permute-start | bytes 589832 | tf_op jit(solution)/shard_map/ppermute | solution.py:1145
  293.0 19.8 %collective-permute-start.50 = (bf16[4,384,256]{2,1,0:T(8,128)(2,1)}, bf16[4,384,256]{2,1,0:T(8,128)(2,1)S(1)}, u32[]{:S(2)}, u32[]{:S(2)}) collective-permute-start(bf16[4,384,256]{2,1,0:T(8,128)(2,1)} %add_convert_fusion.1), channel_id=1, source_target_pairs={{0,4},{2,6},{4,0},{6,2},{8,12},{10,14},{12,8},{14,10},{16,20},{18,... | collective-permute-start | bytes 2359304 | tf_op jit(solution)/shard_map/ppermute | solution.py:1148
  320.0 17.6 %collective-permute-start.55 = (bf16[384,256]{1,0:T(8,128)(2,1)}, bf16[384,256]{1,0:T(8,128)(2,1)S(1)}, u32[]{:S(2)}, u32[]{:S(2)}) collective-permute-start(bf16[384,256]{1,0:T(8,128)(2,1)} %get-tuple-element.398), channel_id=1, source_target_pairs={{0,16},{2,18},{4,20},{6,22},{8,24},{10,26},{12,28},{14,30},{16,0},... | collective-permute-start | bytes 589832 | tf_op jit(solution)/shard_map/ppermute | solution.py:1148
  343.6 21.8 %collective-permute-start.57 = (bf16[1536,256]{1,0:T(8,128)(2,1)}, bf16[1536,256]{1,0:T(8,128)(2,1)S(1)}, u32[]{:S(2)}, u32[]{:S(2)}) collective-permute-start(bf16[1536,256]{1,0:T(8,128)(2,1)} %get-tuple-element.404.own_ref.refs_4_), channel_id=1, source_target_pairs={{0,4},{2,6},{4,0},{6,2},{8,12},{10,14},{12,8},{14,10},{16,20},{18,... | collective-permute-start | bytes 2359304 | tf_op jit(solution)/shard_map/ppermute | solution.py:1148
  406.0 18.0 %collective-permute-start.74 = (bf16[96,2304]{1,0:T(8,128)(2,1)}, bf16[96,2304]{1,0:T(8,128)(2,1)S(1)}, u32[]{:S(2)}, u32[]{:S(2)}) collective-permute-start(bf16[96,2304]{1,0:T(8,128)(2,1)} %get-tuple-element.469), channel_id=1, source_target_pairs={{0,8},{2,10},{4,12},{6,14},{8,16},{10,18},{12,20},{14,22},{1,9},{3... | collective-permute-start | bytes 1327112 | tf_op jit(solution)/shard_map/ppermute | solution.py:1363
  432.2 36.9 %collective-permute-start.78 = (bf16[96,2304]{1,0:T(8,128)(2,1)}, bf16[96,2304]{1,0:T(8,128)(2,1)S(1)}, u32[]{:S(2)}, u32[]{:S(2)}) collective-permute-start(bf16[96,2304]{1,0:T(8,128)(2,1)} %get-tuple-element.467), channel_id=1, source_target_pairs={{0,8},{2,10},{4,12},{6,14},{8,16},{10,18},{12,20},{14,22},{16,24},... | collective-permute-start | bytes 1327112 | tf_op jit(solution)/shard_map/ppermute | solution.py:1363
  433.6 35.5 %collective-permute-start.79 = (bf16[96,2304]{1,0:T(8,128)(2,1)}, bf16[96,2304]{1,0:T(8,128)(2,1)S(1)}, u32[]{:S(2)}, u32[]{:S(2)}) collective-permute-start(bf16[96,2304]{1,0:T(8,128)(2,1)} %get-tuple-element.466), channel_id=1, source_target_pairs={{30,22},{28,20},{26,18},{24,16},{22,14},{20,12},{18,10},{16,8},{14... | collective-permute-start | bytes 1327112 | tf_op jit(solution)/shard_map/ppermute | solution.py:1364
  445.9 23.2 %collective-permute-start.77 = (f32[48,768]{1,0:T(8,128)S(1)}, f32[48,768]{1,0:T(8,128)S(1)}, u32[]{:S(2)}, u32[]{:S(2)}) collective-permute-start(f32[48,768]{1,0:T(8,128)S(1)} %add.134.late_a), channel_id=1, source_target_pairs={{0,1},{1,0},{2,3},{3,2},{4,5},{5,4},{6,7},{7,6},{8,9},{9,8},{10,11... | collective-permute-start | bytes 442376 | tf_op jit(solution)/shard_map/ppermute | solution.py:1145
  (149 other events, 1421.5 us)
Sparse Core Ops, SparseCore 0:
  42.0 100.4 all-gather.1
  237.1 45.0 reduce-scatter.2
  337.8 59.0 reduce-scatter.4

commit v4 on v3

--- a/solution.py
+++ b/solution.py
@@ -400,8 +400,10 @@
     kept_ref,
     came_ref,
     down_ref,
-    inner_ref,
-    grads_ref,
+    inner_a_ref,
+    inner_b_ref,
+    gkept_ref,
+    gcame_ref,
     in16_ref,
     mid_ref,
     near_ref,
@@ -446,9 +448,16 @@
     grad_up = grad_inner * silu
     grad_kept = jnp.where(s == 0, grad_gate, grad_up).astype(BF)
     grad_came = jnp.where(s == 0, grad_up, grad_gate).astype(BF)
-    inner_ref[...] = inner
-    grads_ref[0] = grad_kept
-    grads_ref[1] = grad_came
+    @pl.when(step < steps // 2)
+    def _():
+        inner_a_ref[...] = inner
+
+    @pl.when(step >= steps // 2)
+    def _():
+        inner_b_ref[...] = inner
+
+    gkept_ref[...] = grad_kept
+    gcame_ref[...] = grad_came
     acc_in[...] += mm(grad_kept, w_kept, NN) + mm(grad_came, w_came, NN)
     acc_out[...] += mm(inner, w_down, NN)
 
@@ -496,9 +505,10 @@
                 pl.BlockSpec((tile, D), lambda i, ids: (i, 0)),
             ],
             out_specs=[
-                pl.BlockSpec((rows, tile), lambda i, ids: (0, i)),
-                pl.BlockSpec((2, rows, tile), lambda i, ids: (0, 0, i)),
+                pl.BlockSpec((rows, tile), lambda i, ids: (0, jnp.minimum(i, steps // 2 - 1))),
+                pl.BlockSpec((rows, tile), lambda i, ids: (0, jnp.maximum(i - steps // 2, 0))),
             ]
+            + [pl.BlockSpec((rows, tile), lambda i, ids: (0, i))] * 2
             + [
                 fixed(rows, D),
                 fixed(rows, D),
@@ -509,7 +519,8 @@
             ],
             scratch_shapes=[pltpu.VMEM((rows, D), F32), pltpu.VMEM((rows, D), F32)],
         ),
-        out_shape=[shape((rows, units), BF), shape((2, rows, units), BF)]
+        out_shape=[shape((rows, units // 2), BF)] * 2
+        + [shape((rows, units), BF)] * 2
         + [
             shape((rows, D), BF),
             shape((rows, D), F32),
@@ -812,23 +823,22 @@
 
 def pack_kernel(ids, *refs):
     q_refs, kv_refs = refs[:LINE], refs[LINE : 2 * LINE]
-    own_ref, send_ref = refs[2 * LINE :]
+    first_ref, second_ref, send_ref = refs[2 * LINE :]
     b, s = ids[0], ids[1]
     width = q_refs[0].shape[0]
-    local = LINE * width
     for k in range(LINE):
         at = chunk_at(b, k, width)
 
         @pl.when(s == 0)
         def _():
-            own_ref[pl.ds(at, width), :] = q_refs[k][...]
-            own_ref[pl.ds(local + at, width), :] = kv_refs[k][:width, :]
+            first_ref[pl.ds(at, width), :] = q_refs[k][...]
+            second_ref[pl.ds(at, width), :] = kv_refs[k][:width, :]
             send_ref[pl.ds(at, width), :] = kv_refs[k][width:, :]
 
         @pl.when(s == 1)
         def _():
-            own_ref[pl.ds(at, width), :] = kv_refs[k][:width, :]
-            own_ref[pl.ds(local + at, width), :] = kv_refs[k][width:, :]
+            first_ref[pl.ds(at, width), :] = kv_refs[k][:width, :]
+            second_ref[pl.ds(at, width), :] = kv_refs[k][width:, :]
             send_ref[pl.ds(at, width), :] = q_refs[k][...]
 
 
@@ -837,26 +847,24 @@
     return pl.pallas_call(
         pack_kernel,
         in_specs=[SMEM] + [VMEM] * (2 * LINE),
-        out_specs=[VMEM, VMEM],
-        out_shape=[shape((2 * LINE * width, rows), BF), shape((LINE * width, rows), BF)],
+        out_specs=[VMEM] * 3,
+        out_shape=[shape((LINE * width, rows), BF)] * 3,
         name="pack",
         cost_estimate=cost(2.5),
     )(ids, *grads_q, *grads_kv)
 
 
-def qkv_back_kernel(ids, own_ref, recv_ref, w_ref, near_ref, far_ref, acc_ref):
+def qkv_back_kernel(ids, first_ref, recv_ref, second_ref, w_ref, near_ref, far_ref, acc_ref):
     step = pl.program_id(0)
-    third = pl.num_programs(0) // 3
     count = near_ref.shape[0]
     s = ids[1]
 
-    @pl.when(step == 0)
-    def _():
-        acc_ref[...] = jnp.zeros_like(acc_ref)
-
-    middle = jnp.logical_and(step >= third, step < 2 * third)
-    grads = jnp.where(middle, recv_ref[...], own_ref[...])
-    acc_ref[...] += mm(grads, w_ref[...], TN)
+    for n, ref in enumerate((first_ref, recv_ref, second_ref)):
+
+        @pl.when(step == n)
+        def _():
+            part = mm(ref[...], w_ref[...], TN)
+            acc_ref[...] = part if n == 0 else acc_ref[...] + part
 
     @pl.when(step == pl.num_programs(0) - 1)
     def _():
@@ -864,32 +872,23 @@
         far_ref[...] = acc_ref[pl.ds(pl.multiple_of((1 - s) * count, count), count), :].astype(BF)
 
 
-def qkv_back(ids, own, received, w_qkv):
+def qkv_back(ids, first, received, second, w_qkv):
     local, rows = received.shape
     count = rows // 2
-    tile = local
-    third = local // tile
-
-    def own_at(i, ids):
-        return (jnp.where(i < third, i, jnp.clip(i - third, third - 1, 2 * third - 1)), 0)
-
+    whole = pl.BlockSpec((local, rows), lambda i, ids: (0, 0))
     return pl.pallas_call(
         qkv_back_kernel,
         grid_spec=pltpu.PrefetchScalarGridSpec(
             num_scalar_prefetch=1,
-            grid=(3 * third,),
-            in_specs=[
-                pl.BlockSpec((tile, rows), own_at),
-                pl.BlockSpec((tile, rows), lambda i, ids: (jnp.clip(i - third, 0, third - 1), 0)),
-                pl.BlockSpec((tile, D), lambda i, ids: (i, 0)),
-            ],
+            grid=(3,),
+            in_specs=[whole] * 3 + [pl.BlockSpec((local, D), lambda i, ids: (i, 0))],
             out_specs=[pl.BlockSpec((count, D), lambda i, ids: (0, 0))] * 2,
             scratch_shapes=[pltpu.VMEM((rows, D), F32)],
         ),
         out_shape=[shape((count, D), F32), shape((count, D), BF)],
         name="qkv_back",
         cost_estimate=cost(6),
-    )(ids, own, received, w_qkv)
+    )(ids, first, received, second, w_qkv)
 
 
 def tokens_kernel(
@@ -1236,135 +1235,145 @@
     att_came_c = cswap(att_c)
     hid_came_yc = cswap(after(hid_came_y, branch_far))
     hid_left = [(hid_own, 0), (hid_came_c, 0), (hid_came_y, 0), (hid_came_yc, 1)]
-    inner, grads_in, mlp_in, middle, near, far, near_out, far_out = ffn(
+    inner, inner_2, grad_kept, grad_came, mlp_in, middle, near, far, near_out, far_out = ffn(
         ids, [tokens, tok_far], [branch, branch_far], grad_mlp, mod, ffn_row, w_gate_up, came, w_down
     )
-    inner, grads_in, mlp_in, near, far, att_came_y, att_came_c, hid_came_yc = fence(
-        inner, grads_in, mlp_in, near, far, att_came_y, att_came_c, hid_came_yc
-    )
+    inner, inner_2, grad_kept, grad_came, mlp_in, near, far = fence(
+        inner, inner_2, grad_kept, grad_came, mlp_in, near, far
+    )
+    att_came_y, att_came_c, hid_came_yc, far = fence(att_came_y, att_came_c, hid_came_yc, far)
     hid_left[3] = (hid_came_yc, 1)
 
     received = xswap(far)
     inner_y = yswap(inner)
     inner_c = cswap(inner)
-    grads_c = cswap(grads_in)
+    kept_c = cswap(grad_kept)
     att_came_yc = cswap(att_came_y)
     att_left = [(att_own, 0), (att_came_c, 0), (att_came_y, 0), (att_came_yc, 1)]
     ffn_own, ffn_c, ffn_y = cut(ids, [mlp_in], [False])
-    received, ffn_own, inner_c, grads_c, att_came_yc = fence(
-        received, ffn_own, inner_c, grads_c, att_came_yc
+    received, ffn_own, ffn_c, ffn_y, inner_c, inner_y, kept_c, att_came_yc, came_op, inner_op = fence(
+        received, ffn_own, ffn_c, ffn_y, inner_c, inner_y, kept_c, att_came_yc, grad_came, inner_2
     )
     att_left[3] = (att_came_yc, 1)
+    inner_2y = yswap(inner_op)
+    inner_2c = cswap(inner_op)
+    inner_yc = cswap(inner_y)
+    ffn_came_c = cswap(ffn_c)
     (sums, grad_branch, mid_near, mid_far), near_heads, far_heads = mid_back(
         ids, near, received, middle, [cotangent, cot_far], branch, mod, ffn_row, w_out
     )
+    grad_branch, ffn_came_c, inner_yc, inner_2c, *far_heads = fence(
+        grad_branch, ffn_came_c, inner_yc, inner_2c, *far_heads
+    )
     recv_a = xswap(far_heads[0])
     recv_b = xswap(far_heads[1])
-    ffn_came_c = cswap(after(ffn_c, far_heads[0]))
-    branch_c = cswap(after(grad_branch, far_heads[0]))
-    recv_a, ffn_came_c, branch_c = fence(recv_a, ffn_came_c, branch_c)
+    branch_c = cswap(grad_branch)
+    recv_a, branch_c, inner_2y, ffn_y, branch_op, came_op = fence(
+        recv_a, branch_c, inner_2y, ffn_y, grad_branch, came_op
+    )
+    ffn_came_y = yswap(ffn_y)
+    inner_2yc = cswap(inner_2y)
     grad_1, grad_2 = add_pair(near_heads[0], recv_a)
     grad_3, grad_0 = add_pair(near_heads[1], after(recv_b, grad_1))
-    inner_y = after(inner_y, grad_0)
-    inner_yc = cswap(inner_y)
-    branch_y = yswap(after(grad_branch, inner_y))
-    ffn_came_y = yswap(after(ffn_y, inner_y))
-    inner_all = [inner, inner_c, inner_y, inner_yc]
+    grad_here = spread([grad_0, grad_1, grad_2, grad_3])
     tile = 512
     per = units // tile
-    grad_here = spread([grad_0, grad_1, grad_2, grad_3])
-    total = units + local_width
-    parts_inner = weight_grads(att_left, inner_all, False, tile, 1, total, lambda i: i)
-    parts_inner, branch_y, ffn_came_y, *grad_here = fence(
-        parts_inner, branch_y, ffn_came_y, *grad_here
-    )
-    ffn_came_yc = cswap(ffn_came_y)
-    branch_all = [grad_branch, branch_c, branch_y, cswap(branch_y)]
-    step = 256
     parts_inner = weight_grads(
-        att_left, branch_all, False, step, 0, total, lambda i: i + units // step, parts_inner
-    )
+        att_left, [after(inner, grad_0), inner_c, inner_y, inner_yc], False, tile, 1, units, lambda i: i
+    )
+    parts_inner = weight_grads(
+        att_left,
+        [inner_2, inner_2c, inner_2y, inner_2yc],
+        False,
+        tile,
+        1,
+        units,
+        lambda i: i + per // 2,
+        parts_inner,
+    )
+    parts_inner, ffn_came_y, *grad_here = fence(parts_inner, ffn_came_y, *grad_here)
     sum_inner = scatter(parts_inner)
-    ffn_left = [(ffn_own, 0), (ffn_came_c, 0), (ffn_came_y, 0), (ffn_came_yc, 1)]
-    grads_op, out_op, mid_op, grad_here[0], ffn_came_yc, _ = fence(
-        grads_in, far_out, mid_far, grad_here[0], ffn_came_yc, parts_inner
-    )
-    grads_y = yswap(grads_op)
+    grad_here[0], kept_op, came_op, out_op, mid_op = fence(
+        grad_here[0], grad_kept, grad_came, far_out, mid_far
+    )
+    kept_y = yswap(kept_op)
+    came_y = yswap(came_op)
+    came_c = cswap(came_op)
     out_recv = xswap(out_op)
     mid_came = xswap(mid_op)
     grads_q, (q_gain_part, cap_keep, cap_send, gate_part), grads_kv = attend_back(
         ids, clip_slices, caption_lengths, gates, q_here, grad_here, saved, cap_kv, gains, cosine, sine
     )
-    grads_q, grads_kv, cap_send, grads_y, out_recv, mid_came = fence(
-        grads_q, grads_kv, cap_send, grads_y, out_recv, mid_came
-    )
-
-    kv_c3, grads_yc = cswap(grads_kv[3]), cswap(grads_y)
+    grads_q, grads_kv, cap_send, kept_y, came_y, came_c, out_recv, mid_came = fence(
+        grads_q, grads_kv, cap_send, kept_y, came_y, came_c, out_recv, mid_came
+    )
+
+    kv_c3 = cswap(grads_kv[3])
     kv_c1, cap_c = cswap(grads_kv[1]), cswap(cap_send)
     away = (grads_kv[2].astype(F32) + kv_c3.astype(F32)).astype(BF)
-    away, grads_yc, kv_c1, cap_c, *grads_q = fence(away, grads_yc, kv_c1, cap_c, *grads_q)
+    away, kv_c1, cap_c, *grads_q = fence(away, kv_c1, cap_c, *grads_q)
     away_here = yswap(away)
+    ffn_came_yc, kept_yc, came_yc = fence(ffn_came_y, kept_y, came_y, away)[:3]
+    ffn_came_yc, kept_yc, came_yc = cswap(ffn_came_yc), cswap(kept_yc), cswap(came_yc)
+    ffn_came_yc, kept_yc, came_yc, *grads_q = fence(ffn_came_yc, kept_yc, came_yc, *grads_q)
+    ffn_left = [(ffn_own, 0), (ffn_came_c, 0), (ffn_came_y, 0), (ffn_came_yc, 1)]
+    kept_all = [grad_kept, kept_c, kept_y, kept_yc]
+    came_all = [grad_came, came_c, came_y, came_yc]
     back_q = unspread(grads_q)
     here = (grads_kv[0].astype(F32) + kv_c1.astype(F32)).astype(BF)
     pair = cap_keep + cap_c
-    grads_all = [grads_in, grads_c, grads_y, grads_yc]
-    parts_a = weight_grads(ffn_left, grads_all, False, tile, 0, 2 * units, lambda i: i)
+    parts_a = weight_grads(ffn_left, kept_all, False, tile, 0, 2 * units, lambda i: i)
+    parts_a = weight_grads(ffn_left, came_all, False, tile, 0, 2 * units, lambda i: i + per, parts_a)
     output, early = output_sums(ids, clip_slices, near_out, out_recv, middle, cotangent, mod, sums)
     away_here, output, parts_a, here, pair, sum_inner, *back_q = fence(
         away_here, output, parts_a, here, pair, sum_inner, *back_q
     )
     back_kv, k_gain_part = keys_back(ids, clip_slices, here, away_here, kv_own, gains, cosine, sine)
-    back_kv, k_gain_part = fence(back_kv, k_gain_part)
-    back_kv = fence(*unspread(back_kv))
-    sum_a = scatter(after(parts_a, *back_kv))
-
-    packed, send = pack(ids, back_q, back_kv)
-    packed, send = fence(packed, send)
+    back_kv, k_gain_part, branch_op = fence(back_kv, k_gain_part, branch_op)
+    branch_y = yswap(branch_op)
+    back_kv = unspread(back_kv)
+    *back_kv, parts_a, branch_y = fence(*back_kv, parts_a, branch_y)
+    sum_a = scatter(parts_a)
+
+    first, second, send = fence(*pack(ids, back_q, back_kv))
     packed_recv = xswap(send)
-    packed_y = yswap(packed)
-    packed_c = cswap(packed)
-    cap_y = yswap(after(pick(pair, 1 - y), packed))
+    first_y = yswap(first)
+    first_c = cswap(first)
+    branch_all = [grad_branch, branch_c, branch_y, cswap(after(branch_y, first))]
+    tile, total = 384, 4 * local_width
+    parts_c = weight_grads(att_left, branch_all, False, tile, 0, total, lambda i: i + 6)
+    cap_y = yswap(after(pick(pair, 1 - y), first))
     cap_total = pick(pair, y) + cap_y
     raw_cap, cap_gain_part = caption_back(ids, cap_total, cap_raw, gains)
-    packed_recv, packed_c, raw_cap, cap_gain_part = fence(packed_recv, packed_c, raw_cap, cap_gain_part)
-    recv_y = yswap(packed_recv)
+    packed_recv, first_y, first_c, raw_cap, cap_gain_part, second, parts_c = fence(
+        packed_recv, first_y, first_c, raw_cap, cap_gain_part, second, parts_c
+    )
+    second_y = yswap(second)
+    second_c = cswap(second)
     recv_c = cswap(packed_recv)
-    tok_near, tok_send = qkv_back(ids, packed, packed_recv, w_qkv)
-    packed_y, recv_c, tok_near, tok_send, raw_cap = fence(
-        packed_y, recv_c, tok_near, tok_send, raw_cap
+    first_yc = cswap(first_y)
+    tok_near, tok_send = qkv_back(ids, first, packed_recv, second, w_qkv)
+    tok_near, tok_send, second_y, second_c, recv_c, first_yc, recv_op, raw_cap = fence(
+        tok_near, tok_send, second_y, second_c, recv_c, first_yc, packed_recv, raw_cap
     )
     tok_recv = xswap(tok_send)
-    raw_y, raw_c = yswap(raw_cap), cswap(raw_cap)
-    packed_all = [packed, packed_c, packed_y, cswap(packed_y)]
-    tile = 384
+    recv_y = yswap(recv_op)
+    second_yc = cswap(second_y)
+    raw_c = cswap(raw_cap)
     parts_c = weight_grads(
-        hid_left, packed_all, True, tile, 0, 3 * local_width, lambda i: jnp.where(i < 2, i, i + 2)
-    )
-    recv_y = after(recv_y, parts_c)
-    recv_all = [packed_recv, recv_c, recv_y, cswap(recv_y)]
+        hid_left, [first, first_c, first_y, first_yc], True, tile, 0, total, lambda i: i, parts_c
+    )
     parts_c = weight_grads(
-        hid_left, recv_all, True, tile, 0, 3 * local_width, lambda i: i + 2, parts_c
-    )
-    tok_recv, parts_c, raw_y, raw_c = fence(tok_recv, parts_c, raw_y, raw_c)
-
-    def line_first(parts):
-        to_right, to_left = pick(parts, LINE - 1), pick(parts, 0)
-        ends, last = range(GROUP), bucket_count - 1
-        right_in = lax.ppermute(to_right, BUCKET, [(i, i + GROUP) for i in ends])
-        left_in = lax.ppermute(to_left, BUCKET, [(last - i, last - i - GROUP) for i in ends])
-        return right_in, left_in
-
-    def line_next(parts, t, right_in, left_in):
-        to_right = pick(parts, jnp.clip(LINE - t + z, 0, LINE - 1))
-        to_left = pick(parts, jnp.clip(t - LINE + z, 0, LINE - 1))
-        to_right = (to_right.astype(F32) + right_in.astype(F32)).astype(BF)
-        to_left = (to_left.astype(F32) + left_in.astype(F32)).astype(BF)
-        ends, last = range(GROUP * t), bucket_count - 1
-        right_in = lax.ppermute(to_right, BUCKET, [(i, i + GROUP) for i in ends])
-        left_in = lax.ppermute(to_left, BUCKET, [(last - i, last - i - GROUP) for i in ends])
-        return right_in, left_in
-
-    line = line_first(parts_c)
+        hid_left, [second, second_c, second_y, second_yc], True, tile, 0, total, lambda i: i + 4, parts_c
+    )
+    tok_recv, parts_c, recv_y, raw_c = fence(tok_recv, parts_c, recv_y, raw_c)
+    recv_yc = cswap(recv_y)
+    raw_y = yswap(raw_cap)
+    parts_c = weight_grads(
+        hid_left, [packed_recv, recv_c, recv_y, recv_yc], True, tile, 0, total, lambda i: i + 2, parts_c
+    )
+    parts_c, raw_y = fence(parts_c, raw_y)
+    sum_c = scatter(parts_c)
     token_grad, late = tokens_back(
         ids,
         clip_slices,
@@ -1377,25 +1386,25 @@
         norm_row,
         [q_gain_part, k_gain_part, cap_gain_part, gate_part, early],
     )
-    token_grad, late, *line = fence(token_grad, late, *line)
-    line = line_next(parts_c, 2, *line)
+    raw_yc = cswap(raw_y)
     late = late + cswap(late)
-    late = late + yswap(late)
-    late = late + hop(late, lambda i: i ^ GROUP)
-    raw_yc = cswap(after(raw_y, late))
-    late, raw_yc, *line = fence(late, raw_yc, *line)
-    line = line_next(parts_c, 3, *line)
+    cap_parts = caption_weights(ids, [raw_cap, raw_c, raw_y, raw_yc], caption_rows)
+    late_y = yswap(late)
+    late_y, cap_parts = fence(late_y, cap_parts)
+    late = late + late_y
+    late_z = hop(late, lambda i: i ^ GROUP)
+    late_z, sum_a = fence(late_z, sum_a)
+    late = late + late_z
     late = late + hop(late, lambda i: i ^ (2 * GROUP))
+    late, *cap_parts = fence(late, *cap_parts)
+    cap_parts = unspread(cap_parts)
     late_far = xswap(late)
-    late_far, sum_a, *line = fence(late_far, sum_a, *line)
-    sum_c = pick(parts_c, z).astype(F32) + line[0].astype(F32) + line[1].astype(F32)
-    cap_parts = caption_weights(ids, [after(raw_cap, late), raw_c, raw_y, raw_yc], caption_rows)
-    cap_parts = unspread(cap_parts)
-    caption_w_grad = caption_join(ids, cap_parts)
+    came_out = xswap(sum_a[:, units:])
     late_sum = late
 
     mod_grad, gain_rows = finish(ids, late_sum, late_far)
     mod_mine = mod_grad.astype(BF)
+    caption_w_grad = caption_join(ids, fence(*cap_parts, mod_mine)[:LINE])
     cols_local = CD // bucket_count
     act_cols = lax.dynamic_slice_in_dim(activation, b * cols_local, cols_local, 1)
     ada_grad = mm(mod_mine, act_cols, TN)
@@ -1409,27 +1418,28 @@
         [gain_rows[5, :heads_each], gain_rows[5, local_width : local_width + heads_each]]
     )
 
-    down_out = sum_inner[:, :units].astype(F32).T
+    down_out = sum_inner.astype(F32).T
     kept_out = sum_a[:, :units].astype(F32)
-    came_out = xswap(sum_a[:, units:]).astype(F32)
+    came_out = came_out.astype(F32)
     gate_up_out = jnp.where(
         s == 0,
         jnp.concatenate([kept_out, came_out], 1),
         jnp.concatenate([came_out, kept_out], 1),
     ).T
+    sum_c = after(sum_c, gate_up_out)
     return (
         output,
         token_grad,
         cond_grad,
         ada_grad,
         gain_rows[0],
-        sum_c.T,
+        sum_c[:, : 3 * local_width].astype(F32).T,
         gain_rows[1],
         gain_rows[2],
         caption_w_grad,
         gain_rows[3],
         cross_out,
-        sum_inner[:, units:].astype(F32).T,
+        sum_c[:, 3 * local_width :].astype(F32).T,
         gain_rows[4],
         gate_up_out,
         down_out,

time: 507 us -> 484 us (0.955)
  starting transfers between devices: 99.6 us -> 69.8 us
  waiting for transfers between devices: 147 us -> 155 us
  local copies, waits for them, and re-layouts: 25.1 us -> 20 us
    ppermute x60 -> x69, waiting for transfers between devices: 83.7 us -> 101 us  [hop(): return lax.ppermute(v, BUCKET, [(i, to(i)) for i in range(bucket_count)])]
    ppermute x60 -> x69, starting transfers between devices: 64.2 us -> 52.6 us  [hop(): return lax.ppermute(v, BUCKET, [(i, to(i)) for i in range(bucket_count)])]
    ppermute x6 -> x0, starting transfers between devices: 10.1 us -> none  [the longest x2 5.86 us: line_next(): right_in = lax.ppermute(to_right, BUCKET, [(i, i + GROUP) for i in ends])]
    ppermute x19, starting transfers between devices: 25.2 us -> 17.1 us  [xswap(): return lax.ppermute(v, 'seq', [(0, 1), (1, 0)])]
    ppermute x6 -> x0, waiting for transfers between devices: 7.1 us -> none  [the longest x1 7.08 us: line_first(): right_in = lax.ppermute(to_right, BUCKET, [(i, i + GROUP) for i in ends])]
    pallas_call x5 -> x8, Pallas kernels: 28.1 us -> 32.2 us  [weight_grads(): pl.pallas_call(functools.partial(weight_kernel, len(left), NT if by_rows...]
    unnamed x170 -> x180, local copies, waits for them, and re-layouts: 14.7 us -> 10.8 us
  transfers between devices with their start and end apart: 88 -> 92, of which waited for: 37 -> 34; matrix products, arithmetic and copies ran while one was open for 7% -> 6% of each run, Pallas kernels for 33% -> 36%
where the time goes in v4:
time: 484 us; the launch traced here: 475 us
  Pallas kernels  183 us (38%)
  waiting for transfers between devices  155 us (32%)
  starting transfers between devices  69.8 us (14%)
  other arithmetic  20.3 us (4%)
  local copies, waits for them, and re-layouts  20 us (4%)
  between operations  15.3 us (3%)
  matrix products  12.7 us (3%)
    ppermute x69, waiting for transfers between devices, hop(): return lax.ppermute(v, BUCKET, [(i, to(i)) for i in range(bucket_count)])  101 us
    ppermute x19, waiting for transfers between devices, xswap(): return lax.ppermute(v, 'seq', [(0, 1), (1, 0)])  53.6 us
    ppermute x69, starting transfers between devices, hop(): return lax.ppermute(v, BUCKET, [(i, to(i)) for i in range(bucket_count)])  52.6 us
    pallas_call x1, Pallas kernels, attend_back(): pl.pallas_call(attend_back_kernel, in_specs=[SMEM] * 4 + [VMEM] * (2 * LI...  36.7 us
    pallas_call x8, Pallas kernels, weight_grads(): pl.pallas_call(functools.partial(weight_kernel, len(left), NT if by_rows...  32.2 us
    pallas_call x1, Pallas kernels, attend(): pl.pallas_call(attend_kernel, in_specs=[SMEM] * 4 + [VMEM] * (LINE + GROU...  23.9 us
    pallas_call x1, Pallas kernels, ffn(): pl.pallas_call(ffn_kernel, grid_spec=pltpu.PrefetchScalarGridSpec(num_sca...  21.1 us
    ppermute x19, starting transfers between devices, xswap(): return lax.ppermute(v, 'seq', [(0, 1), (1, 0)])  17.1 us
  transfers between devices with their start and end apart: 92, of which 34 were waited for; matrix products, arithmetic and copies ran while one was open for 6% of the time, Pallas kernels for 36%

profile of v4, /device:TPU:0, one launch (start us, length us, event | category | flops | bytes accessed | tf_op | source)
XLA Modules:
  0.0 475.5 jit_solution(7216208254095106439)
XLA Ops:
  8.0 6.3 %fusion.4.mod_a = f32[4,4608]{1,0:T(4,128)S(1)} fusion(bf16[4,1024]{1,0:T(4,128)(2,1)S(1)} %multiply_convert_fusion.1, bf16[4608,1024]{1,0:T(8,128)(2,1)} %param.24), kind=kOutput, calls=%fused_computation.35 | convolution fusion | flops 37748736 | bytes 9519104 | tf_op jit(solution)/shard_map/dot_general | solution.py:43
  22.2 5.7 %collective-permute-done.tok_b = bf16[128,1536]{1,0:T(8,128)(2,1)S(1)} collective-permute-done((bf16[128,1536]{1,0:T(8,128)(2,1)S(1)}, bf16[128,1536]{1,0:T(8,128)(2,1)S(1)}, u32[]{:S(2)}, u32[]{:S(2)}) %collective-permute-start) | collective-permute-done | bytes 393248 | tf_op jit(solution)/shard_map/ppermute | solution.py:1144
  29.3 6.6 %pre.1 = (bf16[2304,256]{1,0:T(8,128)(2,1)}, bf16[256,1536]{1,0:T(8,128)(2,1)}, f32[8,1536]{1,0:T(8,128)}) custom-call(s32[2]{0:T(128)} %pad_add_fusion.ids, s32[4]{0:T(128)} %slices.11, bf16[128,1536]{1,0:T(8,128)(2,1)} %tok_ref.1, bf16[128,1536]{1,0:T(8,128)(2,1)} %copy-done.9, f32[4,4608]{1,0:T(4,128)} %copy-done.48, f32[4,4608]{1,0:T(4,128)} %copy-done.77, ...), custom_call_target="tpu_custom_call" | custom-call | bytes 120000 | tf_op jit(solution)/shard_map/pre/pallas_call | solution.py:123
  41.2 5.8 %collective-permute-done.2.r_ref = bf16[768,256]{1,0:T(8,128)(2,1)S(1)} collective-permute-done((bf16[768,256]{1,0:T(8,128)(2,1)S(1)}, bf16[768,256]{1,0:T(8,128)(2,1)S(1)}, u32[]{:S(2)}, u32[]{:S(2)}) %collective-permute-start.2) | collective-permute-done | bytes 393248 | tf_op jit(solution)/shard_map/ppermute | solution.py:1144
  60.8 8.2 %caption_keys.1 = (f32[384,512]{1,0:T(8,128)}, bf16[4,384,128]{2,1,0:T(8,128)(2,1)}) custom-call(s32[2]{0:T(128)} %pad_add_fusion.ids, bf16[2,768,4096]{2,1,0:T(8,128)(2,1)} %w_ref.5, bf16[512,4096]{1,0:T(8,128)(2,1)} %bitcast.31, f32[1536,3]{1,0:T(8,128)} %copy.41.gains_ref.refs_9_.refs_15_), custom_call_target="tpu_custom_call" | custom-call | bytes 160000 | tf_op jit(solution)/shard_map/caption_keys/pallas_call | solution.py:205
  85.3 6.1 %collective-permute-done.6.cot_b = bf16[128,1536]{1,0:T(8,128)(2,1)S(1)} collective-permute-done((bf16[128,1536]{1,0:T(8,128)(2,1)S(1)}, bf16[128,1536]{1,0:T(8,128)(2,1)S(1)}, u32[]{:S(2)}, u32[]{:S(2)}) %collective-permute-start.6) | collective-permute-done | bytes 393248 | tf_op jit(solution)/shard_map/ppermute | solution.py:1144
  94.1 23.9 %attend.1 = (bf16[192,256]{1,0:T(8,128)(2,1)}, bf16[192,256]{1,0:T(8,128)(2,1)}, bf16[192,256]{1,0:T(8,128)(2,1)}, bf16[192,256]{1,0:T(8,128)(2,1)}, f32[4,192,2...) custom-call(s32[2]{0:T(128)} %pad_add_fusion.ids, ...), custom_call_target="tpu_custom_call" | custom-call | bytes 660000 | tf_op jit(solution)/shard_map/attend/pallas_call | solution.py:310
  125.3 6.4 %collective-permute-done.16.refs_2_ = bf16[192,256]{1,0:T(8,128)(2,1)S(1)} collective-permute-done((bf16[192,256]{1,0:T(8,128)(2,1)}, bf16[192,256]{1,0:T(8,128)(2,1)S(1)}, u32[]{:S(2)}, u32[]{:S(2)}) %collective-permute-start.16) | collective-permute-done | bytes 98336 | tf_op jit(solution)/shard_map/ppermute | solution.py:1147
  134.1 5.3 %collective-permute-done.20.refs_6_ = bf16[192,256]{1,0:T(8,128)(2,1)S(1)} collective-permute-done((bf16[192,256]{1,0:T(8,128)(2,1)S(1)}, bf16[192,256]{1,0:T(8,128)(2,1)S(1)}, u32[]{:S(2)}, u32[]{:S(2)}) %collective-permute-start.20) | collective-permute-done | bytes 98336 | tf_op jit(solution)/shard_map/ppermute | solution.py:1144
  151.1 7.2 %collective-permute-done.22.br_b = bf16[256,768]{1,0:T(8,128)(2,1)S(1)} collective-permute-done((bf16[256,768]{1,0:T(8,128)(2,1)}, bf16[256,768]{1,0:T(8,128)(2,1)S(1)}, u32[]{:S(2)}, u32[]{:S(2)}) %collective-permute-start.22) | collective-permute-done | bytes 393248 | tf_op jit(solution)/shard_map/ppermute | solution.py:1144
  159.5 21.1 %ffn.1 = (bf16[256,1024]{1,0:T(8,128)(2,1)}, bf16[256,1024]{1,0:T(8,128)(2,1)}, bf16[256,2048]{1,0:T(8,128)(2,1)}, bf16[256,2048]{1,0:T(8,128)(2,1)}, bf16[256,1...) custom-call(s32[2]{0:T(128)} %pad_add_fusion.ids, ...), custom_call_target="tpu_custom_call" | custom-call | bytes 360000 | tf_op jit(solution)/shard_map/ffn/pallas_call | solution.py:496
  186.1 10.5 %collective-permute-done.26.recv_ref = bf16[256,896]{1,0:T(8,128)(2,1)} collective-permute-done((bf16[256,896]{1,0:T(8,128)(2,1)}, bf16[256,896]{1,0:T(8,128)(2,1)}, u32[]{:S(2)}, u32[]{:S(2)}) %collective-permute-start.26) | collective-permute-done | bytes 458784 | tf_op jit(solution)/shard_map/ppermute | solution.py:1144
  198.8 5.6 %mid_back.1 = (f32[8,768]{1,0:T(8,128)}, bf16[256,768]{1,0:T(8,128)(2,1)}, f32[128,768]{1,0:T(8,128)}, bf16[128,768]{1,0:T(8,128)(2,1)}, f32[384,256]{1,0:T(8,12...) custom-call(s32[2]{0:T(128)} %pad_add_fusion.ids, ...), custom_call_target="tpu_custom_call" | custom-call | bytes 110000 | tf_op jit(solution)/shard_map/mid_back/pallas_call | solution.py:598
  205.1 6.9 %collective-permute-done.36.refs_6_ = bf16[256,1024]{1,0:T(8,128)(2,1)} collective-permute-done((bf16[256,1024]{1,0:T(8,128)(2,1)}, bf16[256,1024]{1,0:T(8,128)(2,1)}, u32[]{:S(2)}, u32[]{:S(2)}) %collective-permute-start.36) | collective-permute-done | bytes 524320 | tf_op jit(solution)/shard_map/ppermute | solution.py:1147
  239.0 36.7 %attend_back.1 = (bf16[192,256]{1,0:T(8,128)(2,1)}, bf16[192,256]{1,0:T(8,128)(2,1)}, bf16[192,256]{1,0:T(8,128)(2,1)}, bf16[192,256]{1,0:T(8,128)(2,1)}, f32[19...) custom-call(s32[2]{0:T(128)} %pad_add_fusion.ids, ...), custom_call_target="tpu_custom_call" | custom-call | bytes 800000 | tf_op jit(solution)/shard_map/attend_back/pallas_call | solution.py:766
  275.7 6.0 %collective-permute-done.44.refs_6_ = bf16[256,2048]{1,0:T(8,128)(2,1)} collective-permute-done((bf16[256,2048]{1,0:T(8,128)(2,1)S(1)}, bf16[256,2048]{1,0:T(8,128)(2,1)}, u32[]{:S(2)}, u32[]{:S(2)}) %collective-permute-start.44) | collective-permute-done | bytes 1048608 | tf_op jit(solution)/shard_map/ppermute | solution.py:1147
  297.8 5.5 %weight_grads.10.refs_8_ = bf16[4,96,4096]{2,1,0:T(8,128)(2,1)} custom-call(bf16[1,1,4,96,256]{4,3,2,1,0:T(8,128)(2,1)} %get-tuple-element.428.refs_0_, bf16[1,1,4,96,256]{4,3,2,1,0:T(8,128)(2,1)} %copy-done.22, bf16[2,1,4,96,256]{4,3,2,1,0:T(8,128)(2,1)} %copy-done.10, bf16[2,1,4,96,256]{4,3,2,1,0:T(8,128)(2,1)} %copy-done.13, ...), custom_call_target="tpu_custom_call" | custom-call | bytes 100000 | tf_op jit(solution)/shard_map/weight_grads/pallas_call | solution.py:1102
  303.4 5.6 %weight_grads.11 = bf16[4,96,4096]{2,1,0:T(8,128)(2,1)} custom-call(bf16[1,1,4,96,256]{4,3,2,1,0:T(8,128)(2,1)} %get-tuple-element.428.refs_0_, bf16[1,1,4,96,256]{4,3,2,1,0:T(8,128)(2,1)} %copy-done.22, bf16[2,1,4,96,256]{4,3,2,1,0:T(8,128)(2,1)} %copy-done.10, bf16[2,1,4,96,256]{4,3,2,1,0:T(8,128)(2,1)} %copy-done.13, ...), custom_call_target="tpu_custom_call", output_to_operand_aliasing={{}: (8, {})} | custom-call | bytes 100000 | tf_op jit(solution)/shard_map/weight_grads/pallas_call | solution.py:1102
  322.5 11.8 %collective-permute-done.59.refs_6_ = bf16[384,256]{1,0:T(8,128)(2,1)S(1)} collective-permute-done((bf16[384,256]{1,0:T(8,128)(2,1)}, bf16[384,256]{1,0:T(8,128)(2,1)S(1)}, u32[]{:S(2)}, u32[]{:S(2)}) %collective-permute-start.59) | collective-permute-done | bytes 196640 | tf_op jit(solution)/shard_map/ppermute | solution.py:1147
  353.6 7.0 %qkv_back.1 = (f32[128,1536]{1,0:T(8,128)}, bf16[128,1536]{1,0:T(8,128)(2,1)}) custom-call(s32[2]{0:T(128)} %pad_add_fusion.ids, bf16[768,256]{1,0:T(8,128)(2,1)} %get-tuple-element.477.first_ref.refs_4_, bf16[768,256]{1,0:T(8,128)(2,1)} %copy-done.11, bf16[768,256]{1,0:T(8,128)(2,1)} %get-tuple-element.489.second_ref.refs_4_, bf16[2304,1536]{1,0:T(8,128)(2,1)} %w_ref.7), custom_call_target="tpu_custom_call" | custom-call | bytes 120000 | tf_op jit(solution)/shard_map/qkv_back/pallas_call | solution.py:879
  395.8 5.7 %collective-permute-done.80 = f32[48,768]{1,0:T(8,128)S(1)} collective-permute-done((f32[48,768]{1,0:T(8,128)S(1)}, f32[48,768]{1,0:T(8,128)S(1)}, u32[]{:S(2)}, u32[]{:S(2)}) %collective-permute-start.80) | collective-permute-done | bytes 147488 | tf_op jit(solution)/shard_map/ppermute | solution.py:1147
  404.6 15.0 %collective-permute-done.81 = f32[48,768]{1,0:T(8,128)S(1)} collective-permute-done((f32[48,768]{1,0:T(8,128)S(1)}, f32[48,768]{1,0:T(8,128)S(1)}, u32[]{:S(2)}, u32[]{:S(2)}) %collective-permute-start.81) | collective-permute-done | bytes 147488 | tf_op jit(solution)/shard_map/ppermute | solution.py:1147
  429.8 5.0 %fusion.5 = f32[4,1024]{1,0:T(4,128)S(1)} fusion(bf16[4,4608]{1,0:T(4,128)(2,1)S(1)} %convert_element_type.48, bf16[4608,1024]{1,0:T(8,128)(2,1)} %param.24), kind=kOutput, calls=%fused_computation.36 | convolution fusion | flops 37748736 | bytes 9490432 | tf_op jit(solution)/shard_map/dot_general | solution.py:43
  440.0 19.6 %collective-permute-done.86.refs_2_ = bf16[384,256]{1,0:T(8,128)(2,1)S(1)} collective-permute-done((bf16[384,256]{1,0:T(8,128)(2,1)S(1)}, bf16[384,256]{1,0:T(8,128)(2,1)S(1)}, u32[]{:S(2)}, u32[]{:S(2)}) %collective-permute-start.86) | collective-permute-done | bytes 196640 | tf_op jit(solution)/shard_map/ppermute | solution.py:1147
  (415 shorter events, 216.6 us)
Async XLA Ops:
  7.2 152.3 %all-gather.2.cloned.1.call-start = ((), (), s32[]{:S(2)}) async-start(), calls=%async_computation.3 | async-start | bytes 15728640 | tf_op jit(solution)/shard_map/all_gather | solution.py:1201
  47.7 261.3 %reduce-scatter.4.cloned.1.call-start = ((), (), s32[]{:S(2)}) async-start(), calls=%async_computation.4 | async-start | bytes 1966080 | tf_op jit(solution)/shard_map/reduce_scatter | solution.py:1196
  50.3 18.8 %collective-permute-start.3 = (bf16[384,256]{1,0:T(8,128)(2,1)}, bf16[384,256]{1,0:T(8,128)(2,1)S(1)}, u32[]{:S(2)}, u32[]{:S(2)}) collective-permute-start(bf16[384,256]{1,0:T(8,128)(2,1)} %get-tuple-element.296), channel_id=1, source_target_pairs={{0,8},{2,10},{4,12},{6,14},{8,16},{10,18},{12,20},{14,22},{16,24},... | collective-permute-start | bytes 589832 | tf_op jit(solution)/shard_map/ppermute | solution.py:1147
  69.2 22.1 %collective-permute-start.11 = (bf16[4,384,256]{2,1,0:T(8,128)(2,1)S(1)}, bf16[4,384,256]{2,1,0:T(8,128)(2,1)S(1)}, u32[]{:S(2)}, u32[]{:S(2)}) collective-permute-start(bf16[4,384,256]{2,1,0:T(8,128)(2,1)S(1)} %pad_maximum_fusion.refs_4_.kv_ref), channel_id=1, source_target_pairs={{0,4},{2,6},{4,0},{6,2},{8,12},{10,14},{12,8},{14,10},{16,20},{18,... | collective-permute-start | bytes 2359304 | tf_op jit(solution)/shard_map/ppermute | solution.py:1147
  71.1 20.2 %collective-permute-start.10 = (bf16[4,384,256]{2,1,0:T(8,128)(2,1)S(1)}, bf16[4,384,256]{2,1,0:T(8,128)(2,1)S(1)}, u32[]{:S(2)}, u32[]{:S(2)}) collective-permute-start(bf16[4,384,256]{2,1,0:T(8,128)(2,1)S(1)} %pad_maximum_fusion.refs_4_.kv_ref), channel_id=1, source_target_pairs={{0,2},{2,0},{4,6},{6,4},{8,10},{10,8},{12,14},{14,12},{16,18},{18,... | collective-permute-start | bytes 2359304 | tf_op jit(solution)/shard_map/ppermute | solution.py:1147
  71.1 20.2 %collective-permute-start.6 = (bf16[128,1536]{1,0:T(8,128)(2,1)S(1)}, bf16[128,1536]{1,0:T(8,128)(2,1)S(1)}, u32[]{:S(2)}, u32[]{:S(2)}) collective-permute-start(bf16[128,1536]{1,0:T(8,128)(2,1)S(1)} %copy-done.6), channel_id=1, source_target_pairs={{0,1},{1,0},{2,3},{3,2},{4,5},{5,4},{6,7},{7,6},{8,9},{9,8},{10,11... | collective-permute-start | bytes 1179656 | tf_op jit(solution)/shard_map/ppermute | solution.py:1144
  93.0 25.0 %collective-permute-start.13 = (bf16[2,1,4,96,256]{4,3,2,1,0:T(8,128)(2,1)}, bf16[2,1,4,96,256]{4,3,2,1,0:T(8,128)(2,1)S(1)}, u32[]{:S(2)}, u32[]{:S(2)}) collective-permute-start(bf16[2,1,4,96,256]{4,3,2,1,0:T(8,128)(2,1)} %get-tuple-element.323), channel_id=1, source_target_pairs={{0,4},{2,6},{4,0},{6,2},{8,12},{10,14},{12,8},{14,10},{16,20},{18,... | collective-permute-start | bytes 1179656 | tf_op jit(solution)/shard_map/ppermute | solution.py:1147
  93.5 24.5 %collective-permute-start.14 = (bf16[1,1,4,96,256]{4,3,2,1,0:T(8,128)(2,1)}, bf16[1,1,4,96,256]{4,3,2,1,0:T(8,128)(2,1)S(1)}, u32[]{:S(2)}, u32[]{:S(2)}) collective-permute-start(bf16[1,1,4,96,256]{4,3,2,1,0:T(8,128)(2,1)} %get-tuple-element.324), channel_id=1, source_target_pairs={{0,2},{2,0},{4,6},{6,4},{8,10},{10,8},{12,14},{14,12},{16,18},{18,... | collective-permute-start | bytes 589832 | tf_op jit(solution)/shard_map/ppermute | solution.py:1147
  158.3 22.5 %collective-permute-start.23 = (bf16[2,2,4,96,256]{4,3,2,1,0:T(8,128)(2,1)}, bf16[2,2,4,96,256]{4,3,2,1,0:T(8,128)(2,1)S(1)}, u32[]{:S(2)}, u32[]{:S(2)}) collective-permute-start(bf16[2,2,4,96,256]{4,3,2,1,0:T(8,128)(2,1)} %get-tuple-element.335), channel_id=1, source_target_pairs={{0,4},{2,6},{4,0},{6,2},{8,12},{10,14},{12,8},{14,10},{16,20},{18,... | collective-permute-start | bytes 2359304 | tf_op jit(solution)/shard_map/ppermute | solution.py:1147
  158.3 22.5 %collective-permute-start.25 = (bf16[2,1,4,96,256]{4,3,2,1,0:T(8,128)(2,1)S(1)}, bf16[2,1,4,96,256]{4,3,2,1,0:T(8,128)(2,1)S(1)}, u32[]{:S(2)}, u32[]{:S(2)}) collective-permute-start(bf16[2,1,4,96,256]{4,3,2,1,0:T(8,128)(2,1)S(1)} %collective-permute-done.13.refs_2_), channel_id=1, source_target_pairs={{0,2},{2,0},{4,6},{6,4},{8,10},{10,8},{12,14},{14,12},{16,18},{18,... | collective-permute-start | bytes 1179656 | tf_op jit(solution)/shard_map/ppermute | solution.py:1147
  158.4 22.4 %collective-permute-start.24 = (bf16[1,2,4,96,256]{4,3,2,1,0:T(8,128)(2,1)}, bf16[1,2,4,96,256]{4,3,2,1,0:T(8,128)(2,1)S(1)}, u32[]{:S(2)}, u32[]{:S(2)}) collective-permute-start(bf16[1,2,4,96,256]{4,3,2,1,0:T(8,128)(2,1)} %get-tuple-element.336), channel_id=1, source_target_pairs={{0,2},{2,0},{4,6},{6,4},{8,10},{10,8},{12,14},{14,12},{16,18},{18,... | collective-permute-start | bytes 1179656 | tf_op jit(solution)/shard_map/ppermute | solution.py:1147
  212.2 22.5 %collective-permute-start.39 = (bf16[2,1,4,96,256]{4,3,2,1,0:T(8,128)(2,1)}, bf16[2,1,4,96,256]{4,3,2,1,0:T(8,128)(2,1)S(1)}, u32[]{:S(2)}, u32[]{:S(2)}) collective-permute-start(bf16[2,1,4,96,256]{4,3,2,1,0:T(8,128)(2,1)} %get-tuple-element.386), channel_id=1, source_target_pairs={{0,4},{2,6},{4,0},{6,2},{8,12},{10,14},{12,8},{14,10},{16,20},{18,... | collective-permute-start | bytes 1179656 | tf_op jit(solution)/shard_map/ppermute | solution.py:1147
  234.7 41.0 %collective-permute-start.43 = (bf16[256,2048]{1,0:T(8,128)(2,1)}, bf16[256,2048]{1,0:T(8,128)(2,1)}, u32[]{:S(2)}, u32[]{:S(2)}) collective-permute-start(bf16[256,2048]{1,0:T(8,128)(2,1)} %get-tuple-element.411.refs_4_), channel_id=1, source_target_pairs={{0,4},{2,6},{4,0},{6,2},{8,12},{10,14},{12,8},{14,10},{16,20},{18,... | collective-permute-start | bytes 3145736 | tf_op jit(solution)/shard_map/ppermute | solution.py:1147
  235.7 40.0 %collective-permute-start.45 = (bf16[256,2048]{1,0:T(8,128)(2,1)S(1)}, bf16[256,2048]{1,0:T(8,128)(2,1)S(1)}, u32[]{:S(2)}, u32[]{:S(2)}) collective-permute-start(bf16[256,2048]{1,0:T(8,128)(2,1)S(1)} %copy-done.15), channel_id=1, source_target_pairs={{0,2},{2,0},{4,6},{6,4},{8,10},{10,8},{12,14},{14,12},{16,18},{18,... | collective-permute-start | bytes 3145736 | tf_op jit(solution)/shard_map/ppermute | solution.py:1147
  235.7 46.0 %collective-permute-start.44 = (bf16[256,2048]{1,0:T(8,128)(2,1)S(1)}, bf16[256,2048]{1,0:T(8,128)(2,1)}, u32[]{:S(2)}, u32[]{:S(2)}) collective-permute-start(bf16[256,2048]{1,0:T(8,128)(2,1)S(1)} %copy-done.15), channel_id=1, source_target_pairs={{0,4},{2,6},{4,0},{6,2},{8,12},{10,14},{12,8},{14,10},{16,20},{18,... | collective-permute-start | bytes 3145736 | tf_op jit(solution)/shard_map/ppermute | solution.py:1147
  236.9 164.6 %reduce-scatter.6.cloned.1.call-start = ((), (), s32[]{:S(2)}) async-start(), calls=%async_computation.5 | async-start | bytes 3932160 | tf_op jit(solution)/shard_map/reduce_scatter | solution.py:1196
  236.9 38.8 %collective-permute-start.46 = (bf16[128,1536]{1,0:T(8,128)(2,1)S(1)}, bf16[128,1536]{1,0:T(8,128)(2,1)S(1)}, u32[]{:S(2)}, u32[]{:S(2)}) collective-permute-start(bf16[128,1536]{1,0:T(8,128)(2,1)S(1)} %copy-done.85), channel_id=1, source_target_pairs={{0,1},{1,0},{2,3},{3,2},{4,5},{5,4},{6,7},{7,6},{8,9},{9,8},{10,11... | collective-permute-start | bytes 1179656 | tf_op jit(solution)/shard_map/ppermute | solution.py:1144
  237.4 38.3 %collective-permute-start.47 = (bf16[128,768]{1,0:T(8,128)(2,1)}, bf16[128,768]{1,0:T(8,128)(2,1)S(1)}, u32[]{:S(2)}, u32[]{:S(2)}) collective-permute-start(bf16[128,768]{1,0:T(8,128)(2,1)} %get-tuple-element.414), channel_id=1, source_target_pairs={{0,1},{1,0},{2,3},{3,2},{4,5},{5,4},{6,7},{7,6},{8,9},{9,8},{10,11... | collective-permute-start | bytes 589832 | tf_op jit(solution)/shard_map/ppermute | solution.py:1144
  287.1 21.8 %collective-permute-start.51 = (bf16[4,384,256]{2,1,0:T(8,128)(2,1)}, bf16[4,384,256]{2,1,0:T(8,128)(2,1)}, u32[]{:S(2)}, u32[]{:S(2)}) collective-permute-start(bf16[4,384,256]{2,1,0:T(8,128)(2,1)} %add_convert_fusion.1), channel_id=1, source_target_pairs={{0,4},{2,6},{4,0},{6,2},{8,12},{10,14},{12,8},{14,10},{16,20},{18,... | collective-permute-start | bytes 2359304 | tf_op jit(solution)/shard_map/ppermute | solution.py:1147
  312.9 21.5 %collective-permute-start.61 = (bf16[256,768]{1,0:T(8,128)(2,1)S(1)}, bf16[256,768]{1,0:T(8,128)(2,1)S(1)}, u32[]{:S(2)}, u32[]{:S(2)}) collective-permute-start(bf16[256,768]{1,0:T(8,128)(2,1)S(1)} %copy-done.36), channel_id=1, source_target_pairs={{0,4},{2,6},{4,0},{6,2},{8,12},{10,14},{12,8},{14,10},{16,20},{18,... | collective-permute-start | bytes 1179656 | tf_op jit(solution)/shard_map/ppermute | solution.py:1147
  335.1 129.8 %reduce-scatter.8.cloned.1.call-start = ((), (), s32[]{:S(2)}) async-start(), calls=%async_computation.6 | async-start | bytes 2949120 | tf_op jit(solution)/shard_map/reduce_scatter | solution.py:1196
  421.6 41.8 %collective-permute-start.84 = (bf16[96,2048]{1,0:T(8,128)(2,1)S(1)}, bf16[96,2048]{1,0:T(8,128)(2,1)S(1)}, u32[]{:S(2)}, u32[]{:S(2)}) collective-permute-start(bf16[96,2048]{1,0:T(8,128)(2,1)S(1)} %get-tuple-element.553), channel_id=1, source_target_pairs={{0,1},{1,0},{2,3},{3,2},{4,5},{5,4},{6,7},{7,6},{8,9},{9,8},{10,11... | collective-permute-start | bytes 1179656 | tf_op jit(solution)/shard_map/ppermute | solution.py:1144
  424.5 35.1 %collective-permute-start.86 = (bf16[384,256]{1,0:T(8,128)(2,1)S(1)}, bf16[384,256]{1,0:T(8,128)(2,1)S(1)}, u32[]{:S(2)}, u32[]{:S(2)}) collective-permute-start(bf16[384,256]{1,0:T(8,128)(2,1)S(1)} %copy-done.87), channel_id=1, source_target_pairs={{0,16},{2,18},{4,20},{6,22},{8,24},{10,26},{12,28},{14,30},{16,0},... | collective-permute-start | bytes 589832 | tf_op jit(solution)/shard_map/ppermute | solution.py:1147
  424.5 35.1 %collective-permute-start.87 = (bf16[384,256]{1,0:T(8,128)(2,1)S(1)}, bf16[384,256]{1,0:T(8,128)(2,1)S(1)}, u32[]{:S(2)}, u32[]{:S(2)}) collective-permute-start(bf16[384,256]{1,0:T(8,128)(2,1)S(1)} %copy-done.86), channel_id=1, source_target_pairs={{0,8},{2,10},{4,12},{6,14},{8,16},{10,18},{12,20},{14,22},{16,24},... | collective-permute-start | bytes 589832 | tf_op jit(solution)/shard_map/ppermute | solution.py:1147
  (158 other events, 1537.0 us)
Sparse Core Ops, SparseCore 0:
  47.1 100.4 all-gather.1
  237.0 34.6 reduce-scatter.3
  334.5 57.9 reduce-scatter.5
  394.7 67.3 reduce-scatter.7
